TPU v7x, 32 devices: a whole 2x2x4 slice. The times are simulated.
32 devices in a mesh: dp: 4 (over y, x), seq: 8 (over z, core).
Axes of the slice: x: 2, y: 2, z: 4, core: 2. Of those that a mesh axis runs over, the one named last changes fastest.
Arguments:
- layer_input: bfloat16 [2, 4, 4096, 512], P(None, 'dp', 'seq'), may hold values from -6 to 6
- cotangent: bfloat16 [2, 4, 4096, 512], P(None, 'dp', 'seq'), may hold values from -6 to 6
- doc_len: int32 [2, 4, 1], P(None, 'dp'), may hold values from 2048 to 4096, as said below
- doc_offset: int32 [2, 4, 1], P(None, 'dp'), may hold values from 0 to 2048, as said below
- w_query: bfloat16 [512, 512], P(('dp', 'seq')), may hold values from -0.375 to 0.375
- w_key: bfloat16 [512, 512], P(('dp', 'seq')), may hold values from -0.375 to 0.375
- w_value: bfloat16 [512, 512], P(('dp', 'seq')), may hold values from -0.25 to 0.25
- w_out: bfloat16 [512, 512], P(('dp', 'seq')), may hold values from -1 to 1
- w_gate_attn: bfloat16 [512, 512], P(('dp', 'seq')), may hold values from -0.25 to 0.25
- w_gate_ffn: bfloat16 [512, 512], P(('dp', 'seq')), may hold values from -0.25 to 0.25
- w_in: bfloat16 [512, 2048], P(('dp', 'seq')), may hold values from -0.25 to 0.25
- w_back: bfloat16 [2048, 512], P(('dp', 'seq')), may hold values from -0.125 to 0.125
- norm_attn: bfloat16 [512], P(('dp', 'seq')), may hold values from 0.5 to 1.5
- norm_ffn: bfloat16 [512], P(('dp', 'seq')), may hold values from 0.5 to 1.5
- bias_attn: bfloat16 [512], P(('dp', 'seq')), may hold values from -3 to 3
- bias_ffn: bfloat16 [512], P(('dp', 'seq')), may hold values from -3 to 3
Outputs:
- output: bfloat16 [2, 4, 4096, 512], P(None, 'dp', 'seq')
- grad_input: float32 [2, 4, 4096, 512], P(None, 'dp', 'seq')
- grad_w_query: float32 [512, 512], P(('dp', 'seq'))
- grad_w_key: float32 [512, 512], P(('dp', 'seq'))
- grad_w_value: float32 [512, 512], P(('dp', 'seq'))
- grad_w_out: float32 [512, 512], P(('dp', 'seq'))
- grad_w_gate_attn: float32 [512, 512], P(('dp', 'seq'))
- grad_w_gate_ffn: float32 [512, 512], P(('dp', 'seq'))
- grad_w_in: float32 [512, 2048], P(('dp', 'seq'))
- grad_w_back: float32 [2048, 512], P(('dp', 'seq'))
- grad_norm_attn: float32 [512], P(('dp', 'seq'))
- grad_norm_ffn: float32 [512], P(('dp', 'seq'))
- grad_bias_attn: float32 [512], P(('dp', 'seq'))
- grad_bias_ffn: float32 [512], P(('dp', 'seq'))
Inputs may be any that keep to these rules, and one draw needn't show every extreme that they name: The document of region r of a slot takes positions r * 4096 + doc_offset to r * 4096 + doc_offset + doc_len - 1 of that slot; the other positions are padding. Every draw has a document of 4096 positions and one of 2048. doc_offset + doc_len <= 4096 for every document.
All inputs are finite; a program needn't handle non-finite values.
Results may differ from a plain program's by a relative error of at most 0.018.
Values may be sent and summed in bfloat16 or wider, within the bound.
A program may use at most 192 MiB of HBM per device.

v0:
```python
from functools import partial

import jax
import jax.numpy as jnp
from jax import lax
from jax.sharding import PartitionSpec as P

HEADS = 8
HEAD_DIM = 64
DOC_MAX = 4096


EPS = 1e-05


def from_behind(x, axis, by):
    count = lax.axis_size(axis)
    pairs = [(i, i + by) for i in range(count) if 0 <= i + by < count]
    return lax.ppermute(x, axis, pairs)


def passed_along(value, axis, steps):
    count = lax.axis_size(axis)
    pairs = [(source, (source + steps) % count) for source in range(count)]
    return lax.ppermute(value, axis, pairs)


def rms_norm(values, gain):
    return values * lax.rsqrt(jnp.mean(values * values, -1, keepdims=True) + EPS) * gain


def dense(left, right):
    return jnp.dot(left, right, preferred_element_type=jnp.float32)


def dense_tn(left, right):
    return lax.dot_general(
        left, right, (((0,), (0,)), ((), ())), preferred_element_type=jnp.float32
    )


def dense_nt(left, right):
    return lax.dot_general(
        left, right, (((1,), (1,)), ((), ())), preferred_element_type=jnp.float32
    )


def layout_of(lengths, offsets, source, rows, filler):
    positions = source * rows + jnp.arange(rows, dtype=jnp.int32)
    region = positions // DOC_MAX
    inside = positions - region * DOC_MAX
    members = (region[:, None] == jnp.arange(lengths.shape[1], dtype=jnp.int32)[None, :]).astype(
        jnp.int32
    )
    begins = jnp.sum(members[None] * offsets[:, None, :], axis=2)
    spans = jnp.sum(members[None] * lengths[:, None, :], axis=2)
    inside_doc = (inside[None] >= begins) & (inside[None] < begins + spans)
    labels = jnp.where(inside_doc, region[None], filler)
    return (positions, labels, inside_doc)


def allowed_pairs(query_side, key_side):
    same_doc = query_side[1][:, :, None] == key_side[1][:, None, :]
    causal = key_side[0][None, None, :] <= query_side[0][None, :, None]
    return same_doc & causal


def absorb(carry, query, key_piece, value_piece, allowed):
    run_max, run_sum, totals = carry
    scores = jnp.einsum(
        "mqhd,mkhd->mhqk", query, key_piece, preferred_element_type=jnp.float32
    ) * HEAD_DIM ** (-0.5)
    scores = jnp.where(allowed[:, None], scores, -1e30)
    new_max = jnp.maximum(run_max, jnp.max(scores, axis=-1))
    factor = jnp.exp(run_max - new_max)
    weights = jnp.where(allowed[:, None], jnp.exp(scores - new_max[..., None]), 0.0)
    run_sum = run_sum * factor + jnp.sum(weights, axis=-1)
    totals = totals * factor[..., None] + jnp.einsum(
        "mhqk,mkhd->mhqd", weights, value_piece.astype(jnp.float32)
    )
    return (new_max, run_sum, totals)


def hop_grads(query, grad_att, lse, delta, key_piece, value_piece, allowed):
    scores = jnp.einsum(
        "mqhd,mkhd->mhqk", query, key_piece, preferred_element_type=jnp.float32
    ) * HEAD_DIM ** (-0.5)
    probs = jnp.where(allowed[:, None], jnp.exp(scores - lse[..., None]), 0.0)
    grad_value = jnp.einsum("mhqk,mqhd->mkhd", probs, grad_att.astype(jnp.float32))
    grad_probs = jnp.einsum(
        "mqhd,mkhd->mhqk", grad_att, value_piece, preferred_element_type=jnp.float32
    )
    grad_scores = probs * (grad_probs - delta[..., None]) * HEAD_DIM ** (-0.5)
    grad_query = jnp.einsum("mhqk,mkhd->mqhd", grad_scores, key_piece.astype(jnp.float32))
    grad_key = jnp.einsum("mhqk,mqhd->mkhd", grad_scores, query.astype(jnp.float32))
    return (grad_query, grad_key, grad_value)


def shards(
    layer_input,
    cotangent,
    doc_len,
    doc_offset,
    w_query,
    w_key,
    w_value,
    w_out,
    w_gate_attn,
    w_gate_ffn,
    w_in,
    w_back,
    norm_attn,
    norm_ffn,
    bias_attn,
    bias_ffn,
):
    gathered = (
        lax.all_gather(w_query, ("dp", "seq"), axis=0, tiled=True),
        lax.all_gather(w_key, ("dp", "seq"), axis=0, tiled=True),
        lax.all_gather(w_value, ("dp", "seq"), axis=0, tiled=True),
        lax.all_gather(w_out, ("dp", "seq"), axis=0, tiled=True),
        lax.all_gather(w_gate_attn, ("dp", "seq"), axis=0, tiled=True),
        lax.all_gather(w_gate_ffn, ("dp", "seq"), axis=0, tiled=True),
        lax.all_gather(w_in, ("dp", "seq"), axis=0, tiled=True),
        lax.all_gather(w_back, ("dp", "seq"), axis=0, tiled=True),
        lax.all_gather(norm_attn, ("dp", "seq"), axis=0, tiled=True),
        lax.all_gather(norm_ffn, ("dp", "seq"), axis=0, tiled=True),
        lax.all_gather(bias_attn, ("dp", "seq"), axis=0, tiled=True),
        lax.all_gather(bias_ffn, ("dp", "seq"), axis=0, tiled=True),
    )
    (
        full_query,
        full_key,
        full_value,
        full_out,
        full_gate_attn,
        full_gate_ffn,
        full_in,
        full_back,
        gain_attn,
        gain_ffn,
        shift_attn,
        shift_ffn,
    ) = gathered
    micro = layer_input.shape[0]
    rows = layer_input.shape[2]
    width = layer_input.shape[3]
    tokens = micro * rows
    nseq = lax.axis_size("seq")
    me_index = lax.axis_index("seq")
    hops = min(max(DOC_MAX // rows, 1), nseq) - 1
    lengths = doc_len[:, 0]
    offsets = doc_offset[:, 0]

    def key_side(source):
        positions, labels, _ = layout_of(lengths, offsets, source, rows, -2)
        return (positions, labels)

    own_layout = layout_of(lengths, offsets, me_index, rows, -1)
    query_side = (own_layout[0], own_layout[1])
    own_keys = key_side(me_index)
    inputs = layer_input[:, 0].reshape(tokens, width).astype(jnp.float32)
    normed_attn, pull_attn = jax.vjp(rms_norm, inputs, gain_attn.astype(jnp.float32))
    normed_low = normed_attn.astype(jnp.bfloat16)
    query = dense(normed_low, full_query).astype(jnp.bfloat16)
    keys = dense(normed_low, full_key).astype(jnp.bfloat16)
    values = dense(normed_low, full_value).astype(jnp.bfloat16)
    gate_attn = jax.nn.sigmoid(dense(normed_low, full_gate_attn) + shift_attn.astype(jnp.float32))
    head_shape = (micro, rows, HEADS, HEAD_DIM)
    query_h = query.reshape(head_shape)
    keys_h = keys.reshape(head_shape)
    values_h = values.reshape(head_shape)
    start_carry = (
        jnp.full((micro, HEADS, rows), -1e30, jnp.float32),
        jnp.zeros((micro, HEADS, rows), jnp.float32),
        jnp.zeros((micro, HEADS, rows, HEAD_DIM), jnp.float32),
    )
    carry = absorb(start_carry, query_h, keys_h, values_h, allowed_pairs(query_side, own_keys))

    def forward_hop(hop, state):
        pieces, inner = state
        pieces = from_behind((pieces[0], pieces[1]), "seq", 1)
        source = me_index - hop
        inner = absorb(
            inner, query_h, pieces[0], pieces[1], allowed_pairs(query_side, key_side(source))
        )
        return (pieces, inner)

    _, (run_max, run_sum, totals) = lax.fori_loop(
        1, hops + 1, forward_hop, ((keys_h, values_h), carry)
    )
    live = own_layout[2][:, None, :]
    safe_sum = jnp.where(live, run_sum, 1.0)
    attended_h = jnp.where(live[..., None], totals / safe_sum[..., None], 0.0)
    lse = jnp.where(live, run_max + jnp.log(safe_sum), 0.0)
    attended32 = attended_h.transpose(0, 2, 1, 3).reshape(tokens, width)
    attended = attended32.astype(jnp.bfloat16)
    branch_attn = dense(attended, full_out)
    hidden = gate_attn * branch_attn + (1.0 - gate_attn) * inputs
    normed_ffn, pull_ffn = jax.vjp(rms_norm, hidden, gain_ffn.astype(jnp.float32))
    normed_ffn_low = normed_ffn.astype(jnp.bfloat16)
    pre = dense(normed_ffn_low, full_in)
    act32, pull_gelu = jax.vjp(partial(jax.nn.gelu, approximate=True), pre)
    act = act32.astype(jnp.bfloat16)
    branch_ffn = dense(act, full_back)
    gate_ffn = jax.nn.sigmoid(dense(normed_ffn_low, full_gate_ffn) + shift_ffn.astype(jnp.float32))
    output = gate_ffn * branch_ffn + (1.0 - gate_ffn) * hidden
    again = (
        lax.all_gather(w_query, ("dp", "seq"), axis=0, tiled=True),
        lax.all_gather(w_key, ("dp", "seq"), axis=0, tiled=True),
        lax.all_gather(w_value, ("dp", "seq"), axis=0, tiled=True),
        lax.all_gather(w_out, ("dp", "seq"), axis=0, tiled=True),
        lax.all_gather(w_gate_attn, ("dp", "seq"), axis=0, tiled=True),
        lax.all_gather(w_gate_ffn, ("dp", "seq"), axis=0, tiled=True),
        lax.all_gather(w_in, ("dp", "seq"), axis=0, tiled=True),
        lax.all_gather(w_back, ("dp", "seq"), axis=0, tiled=True),
        lax.all_gather(norm_attn, ("dp", "seq"), axis=0, tiled=True),
        lax.all_gather(norm_ffn, ("dp", "seq"), axis=0, tiled=True),
        lax.all_gather(bias_attn, ("dp", "seq"), axis=0, tiled=True),
        lax.all_gather(bias_ffn, ("dp", "seq"), axis=0, tiled=True),
    )
    (
        back_query,
        back_key,
        back_value,
        back_out,
        back_gate_attn,
        back_gate_ffn,
        back_in,
        back_back,
        _,
        _,
        _,
        _,
    ) = again
    upstream = cotangent[:, 0].reshape(tokens, width).astype(jnp.float32)
    d_logit_ffn = (upstream * (branch_ffn - hidden) * gate_ffn * (1.0 - gate_ffn)).astype(
        jnp.bfloat16
    )
    d_branch_ffn = (upstream * gate_ffn).astype(jnp.bfloat16)
    grad_back = dense_tn(act, d_branch_ffn)
    (d_pre32,) = pull_gelu(dense_nt(d_branch_ffn, back_back))
    d_pre = d_pre32.astype(jnp.bfloat16)
    grad_in = dense_tn(normed_ffn_low, d_pre)
    grad_gate_ffn = dense_tn(normed_ffn_low, d_logit_ffn)
    grad_bias_ffn = jnp.sum(d_logit_ffn.astype(jnp.float32), axis=0)
    d_normed_ffn = dense_nt(d_pre, back_in) + dense_nt(d_logit_ffn, back_gate_ffn)
    d_hidden_norm, grad_gain_ffn = pull_ffn(d_normed_ffn)
    d_hidden = upstream * (1.0 - gate_ffn) + d_hidden_norm
    d_branch_attn = (d_hidden * gate_attn).astype(jnp.bfloat16)
    d_logit_attn = (d_hidden * (branch_attn - inputs) * gate_attn * (1.0 - gate_attn)).astype(
        jnp.bfloat16
    )
    grad_out = dense_tn(attended, d_branch_attn)
    d_attended = dense_nt(d_branch_attn, back_out).astype(jnp.bfloat16)
    grad_att = d_attended.reshape(head_shape)
    delta = jnp.einsum(
        "mqhd,mqhd->mhq", grad_att.astype(jnp.float32), attended32.reshape(head_shape)
    )
    first_q, first_k, first_v = hop_grads(
        query_h, grad_att, lse, delta, keys_h, values_h, allowed_pairs(query_side, own_keys)
    )

    def backward_hop(hop, state):
        pieces, moving, grad_q = state
        pieces = from_behind((pieces[0], pieces[1]), "seq", 1)
        moving = (
            passed_along(moving[0].astype(jnp.bfloat16), "seq", 1).astype(jnp.float32),
            passed_along(moving[1].astype(jnp.bfloat16), "seq", 1).astype(jnp.float32),
        )
        source = me_index - hop
        step_q, step_k, step_v = hop_grads(
            query_h,
            grad_att,
            lse,
            delta,
            pieces[0],
            pieces[1],
            allowed_pairs(query_side, key_side(source)),
        )
        return (pieces, (moving[0] + step_k, moving[1] + step_v), grad_q + step_q)

    _, moving, grad_q = lax.fori_loop(
        1, hops + 1, backward_hop, ((keys_h, values_h), (first_k, first_v), first_q)
    )
    moving = (
        passed_along(moving[0].astype(jnp.bfloat16), "seq", -hops).astype(jnp.float32),
        passed_along(moving[1].astype(jnp.bfloat16), "seq", -hops).astype(jnp.float32),
    )
    grad_k, grad_v = moving
    d_query = grad_q.reshape(tokens, width).astype(jnp.bfloat16)
    d_key = grad_k.reshape(tokens, width).astype(jnp.bfloat16)
    d_value = grad_v.reshape(tokens, width).astype(jnp.bfloat16)
    grad_query = dense_tn(normed_low, d_query)
    grad_key = dense_tn(normed_low, d_key)
    grad_value = dense_tn(normed_low, d_value)
    grad_gate_attn = dense_tn(normed_low, d_logit_attn)
    grad_bias_attn = jnp.sum(d_logit_attn.astype(jnp.float32), axis=0)
    d_normed_attn = (
        dense_nt(d_query, back_query)
        + dense_nt(d_key, back_key)
        + dense_nt(d_value, back_value)
        + dense_nt(d_logit_attn, back_gate_attn)
    )
    d_inputs_norm, grad_gain_attn = pull_attn(d_normed_attn)
    grad_input = d_hidden * (1.0 - gate_attn) + d_inputs_norm
    owned = (
        lax.psum_scatter(grad_query, ("dp", "seq"), scatter_dimension=0, tiled=True),
        lax.psum_scatter(grad_key, ("dp", "seq"), scatter_dimension=0, tiled=True),
        lax.psum_scatter(grad_value, ("dp", "seq"), scatter_dimension=0, tiled=True),
        lax.psum_scatter(grad_out, ("dp", "seq"), scatter_dimension=0, tiled=True),
        lax.psum_scatter(grad_gate_attn, ("dp", "seq"), scatter_dimension=0, tiled=True),
        lax.psum_scatter(grad_gate_ffn, ("dp", "seq"), scatter_dimension=0, tiled=True),
        lax.psum_scatter(grad_in, ("dp", "seq"), scatter_dimension=0, tiled=True),
        lax.psum_scatter(grad_back, ("dp", "seq"), scatter_dimension=0, tiled=True),
        lax.psum_scatter(grad_gain_attn, ("dp", "seq"), scatter_dimension=0, tiled=True),
        lax.psum_scatter(grad_gain_ffn, ("dp", "seq"), scatter_dimension=0, tiled=True),
        lax.psum_scatter(grad_bias_attn, ("dp", "seq"), scatter_dimension=0, tiled=True),
        lax.psum_scatter(grad_bias_ffn, ("dp", "seq"), scatter_dimension=0, tiled=True),
    )
    return (
        output.reshape(micro, 1, rows, width).astype(jnp.bfloat16),
        grad_input.reshape(micro, 1, rows, width),
        owned[0],
        owned[1],
        owned[2],
        owned[3],
        owned[4],
        owned[5],
        owned[6],
        owned[7],
        owned[8],
        owned[9],
        owned[10],
        owned[11],
    )


def solution(mesh):
    placed = (
        P(None, "dp", "seq", None),
        P(None, "dp", "seq", None),
        P(None, "dp", None),
        P(None, "dp", None),
        P(("dp", "seq"), None),
        P(("dp", "seq"), None),
        P(("dp", "seq"), None),
        P(("dp", "seq"), None),
        P(("dp", "seq"), None),
        P(("dp", "seq"), None),
        P(("dp", "seq"), None),
        P(("dp", "seq"), None),
        P(("dp", "seq")),
        P(("dp", "seq")),
        P(("dp", "seq")),
        P(("dp", "seq")),
    )
    return jax.shard_map(
        shards,
        mesh=mesh,
        in_specs=placed,
        out_specs=(
            P(None, "dp", "seq", None),
            P(None, "dp", "seq", None),
            P(("dp", "seq"), None),
            P(("dp", "seq"), None),
            P(("dp", "seq"), None),
            P(("dp", "seq"), None),
            P(("dp", "seq"), None),
            P(("dp", "seq"), None),
            P(("dp", "seq"), None),
            P(("dp", "seq"), None),
            P(("dp", "seq")),
            P(("dp", "seq")),
            P(("dp", "seq")),
            P(("dp", "seq")),
        ),
        check_vma=False,
    )
```

profile of v0, /device:TPU:0, one launch (start us, length us, event | category | flops | bytes accessed | tf_op | source)
XLA Modules:
  0.0 1951.9 jit_solution(1333651285589154342)
XLA Ops:
  13.2 42.1 %all-reduce.9 = (bf16[512]{0:T(512)(128)(2,1)S(1)}, bf16[512]{0:T(512)(128)(2,1)S(1)}, bf16[512]{0:T(512)(128)(2,1)S(1)}, bf16[512]{0:T(512)(128)(2,1)S(1)}) all-reduce(bf16[512]{0:T(512)(128)(2,1)S(1)} %dynamic-update-slice, bf16[512]{0:T(512)(128)(2,1)S(1)} %dynamic-update-slice.1, ...), channel_id=1, replica_groups=mesh['dp'=4,'seq'=8] {'dp','seq'}, use_global_device_ids=true, to_apply=%add | all-reduce | flops 2048 | bytes 8192
  57.4 43.0 %all_gather.49 = bf16[512,512]{1,0:T(8,128)(2,1)S(1)} all-gather(bf16[16,512]{1,0:T(8,128)(2,1)} %param.24), channel_id=1, replica_groups=mesh['dp'=4,'seq'=8] {'dp','seq'}, dimensions={0}, use_global_device_ids=true | all-gather | bytes 540672 | tf_op jit(solution)/shard_map/all_gather | solution.py:118
  105.6 38.9 %all_gather.47 = bf16[512,512]{1,0:T(8,128)(2,1)S(1)} all-gather(bf16[16,512]{1,0:T(8,128)(2,1)S(1)} %copy-done.72), channel_id=1, replica_groups=mesh['dp'=4,'seq'=8] {'dp','seq'}, dimensions={0}, use_global_device_ids=true | all-gather | bytes 540672 | tf_op jit(solution)/shard_map/all_gather | solution.py:119
  166.2 41.6 %all_gather.48 = bf16[512,512]{1,0:T(8,128)(2,1)S(1)} all-gather(bf16[16,512]{1,0:T(8,128)(2,1)S(1)} %copy-done.73), channel_id=1, replica_groups=mesh['dp'=4,'seq'=8] {'dp','seq'}, dimensions={0}, use_global_device_ids=true | all-gather | bytes 540672 | tf_op jit(solution)/shard_map/all_gather | solution.py:120
  217.8 9.5 fusion.71
  227.2 229.1 %while.48 = (s32[]{:T(128)}, bf16[2,512,8,64]{1,3,2,0:T(8,128)(2,1)}, bf16[2,512,8,64]{1,3,2,0:T(8,128)(2,1)}, f32[2,8,512]{2,1,0:T(8,128)S(1)}, f32[2,8,512]{2,...) while((s32[]{:T(128)}, ...), condition=%wide.region_6.7_spmd.clone, body=%wide.region_3.6_spmd.clone.sunk | while | flops 1126481920 | bytes 90220944 | solution.py:189
  248.9 12.8 collective-permute-start
  283.5 12.8 collective-permute-start
  318.1 12.8 collective-permute-start
  352.7 12.8 collective-permute-start
  387.2 12.8 collective-permute-start
  421.8 12.8 collective-permute-start
  459.7 51.6 %all_gather.50 = bf16[512,512]{1,0:T(8,128)(2,1)S(1)} all-gather(bf16[16,512]{1,0:T(8,128)(2,1)S(1)} %copy-done.74), channel_id=1, replica_groups=mesh['dp'=4,'seq'=8] {'dp','seq'}, dimensions={0}, use_global_device_ids=true | all-gather | bytes 540672 | tf_op jit(solution)/shard_map/all_gather | solution.py:121
  511.3 39.2 %all_gather.45 = bf16[512,512]{1,0:T(8,128)(2,1)S(1)} all-gather(bf16[16,512]{1,0:T(8,128)(2,1)S(1)} %copy-done.75), channel_id=1, replica_groups=mesh['dp'=4,'seq'=8] {'dp','seq'}, dimensions={0}, use_global_device_ids=true | all-gather | bytes 540672 | tf_op jit(solution)/shard_map/all_gather | solution.py:122
  553.9 42.7 %all_gather.52 = bf16[512,512]{1,0:T(8,128)(2,1)} all-gather(bf16[16,512]{1,0:T(8,128)(2,1)S(1)} %copy-done.76), channel_id=1, replica_groups=mesh['dp'=4,'seq'=8] {'dp','seq'}, dimensions={0}, use_global_device_ids=true | all-gather | bytes 540672 | tf_op jit(solution)/shard_map/all_gather | solution.py:123
  618.7 9.7 fusion.41
  644.7 9.9 multiply_multiply_fusion.1
  670.2 8.7 fusion.70
  679.0 414.6 %while.49 = (s32[]{:T(128)}, bf16[2,512,8,64]{1,3,2,0:T(8,128)(2,1)}, bf16[2,512,8,64]{1,3,2,0:T(8,128)(2,1)}, bf16[2,512,8,64]{1,3,2,0:T(8,128)(2,1)}, bf16[2,5...) while((s32[]{:T(128)}, ...), condition=%wide.region_10.11_spmd.clone, body=%wide.region_9.10_spmd.clone.sunk | while | flops 2731311104 | bytes 135408144 | solution.py:283
  695.4 9.6 multiply_multiply_fusion.7
  713.5 9.4 bitcast_add_fusion.7
  722.8 19.6 %collective-permute-start.2 = (bf16[2,512,8,64]{1,3,2,0:T(8,128)(2,1)}, bf16[2,512,8,64]{1,3,2,0:T(8,128)(2,1)S(1)}, u32[]{:S(2)}, u32[]{:S(2)}) collective-permute-start(bf16[2,512,8,64]{1,3,2,0:T(8,128)(2,1)} %get-tuple-element.1320), channel_id=1, source_target_pairs={{0,1},{1,2},{2,3},{3,4},{4,5},{5,6},{6,7},{8,9},{9,10},{10,11},{11... | collective-permute-start | bytes 3145736 | tf_op jit(solution)/shard_map/while/body/eval_jaxpr/ppermute | solution.py:19
  759.0 9.6 multiply_multiply_fusion.7
  775.5 9.7 bitcast_add_fusion.7
  785.3 19.8 %collective-permute-start.2 = (bf16[2,512,8,64]{1,3,2,0:T(8,128)(2,1)}, bf16[2,512,8,64]{1,3,2,0:T(8,128)(2,1)S(1)}, u32[]{:S(2)}, u32[]{:S(2)}) collective-permute-start(bf16[2,512,8,64]{1,3,2,0:T(8,128)(2,1)} %get-tuple-element.1320), channel_id=1, source_target_pairs={{0,1},{1,2},{2,3},{3,4},{4,5},{5,6},{6,7},{8,9},{9,10},{10,11},{11... | collective-permute-start | bytes 3145736 | tf_op jit(solution)/shard_map/while/body/eval_jaxpr/ppermute | solution.py:19
  821.3 9.6 multiply_multiply_fusion.7
  839.5 9.4 bitcast_add_fusion.7
  848.9 19.9 %collective-permute-start.2 = (bf16[2,512,8,64]{1,3,2,0:T(8,128)(2,1)}, bf16[2,512,8,64]{1,3,2,0:T(8,128)(2,1)S(1)}, u32[]{:S(2)}, u32[]{:S(2)}) collective-permute-start(bf16[2,512,8,64]{1,3,2,0:T(8,128)(2,1)} %get-tuple-element.1320), channel_id=1, source_target_pairs={{0,1},{1,2},{2,3},{3,4},{4,5},{5,6},{6,7},{8,9},{9,10},{10,11},{11... | collective-permute-start | bytes 3145736 | tf_op jit(solution)/shard_map/while/body/eval_jaxpr/ppermute | solution.py:19
  885.0 9.6 multiply_multiply_fusion.7
  902.6 9.4 bitcast_add_fusion.7
  912.0 20.1 %collective-permute-start.2 = (bf16[2,512,8,64]{1,3,2,0:T(8,128)(2,1)}, bf16[2,512,8,64]{1,3,2,0:T(8,128)(2,1)S(1)}, u32[]{:S(2)}, u32[]{:S(2)}) collective-permute-start(bf16[2,512,8,64]{1,3,2,0:T(8,128)(2,1)} %get-tuple-element.1320), channel_id=1, source_target_pairs={{0,1},{1,2},{2,3},{3,4},{4,5},{5,6},{6,7},{8,9},{9,10},{10,11},{11... | collective-permute-start | bytes 3145736 | tf_op jit(solution)/shard_map/while/body/eval_jaxpr/ppermute | solution.py:19
  948.3 9.6 multiply_multiply_fusion.7
  964.5 10.1 bitcast_add_fusion.7
  974.6 17.0 collective-permute-start.2
  1007.8 9.6 multiply_multiply_fusion.7
  1024.0 10.1 bitcast_add_fusion.7
  1034.1 17.0 collective-permute-start.2
  1067.3 9.6 multiply_multiply_fusion.7
  1083.5 10.1 bitcast_add_fusion.7
  1101.3 15.3 collective-permute-start.6
  1123.1 13.1 collective-permute-start.7
  1167.1 51.0 %all-reduce.8 = (f32[512]{0:T(512)S(1)}, f32[512]{0:T(512)S(1)}, f32[512]{0:T(512)S(1)}, f32[512]{0:T(512)S(1)}) all-reduce(f32[512]{0:T(512)S(1)} %get-tuple-element.901, f32[512]{0:T(512)S(1)} %copy-done.78, f32[512]{0:T(512)S(1)} %copy-done.77, f32[512]{0:T(512)S(1)} %copy-done.79), channel_id=10, replica_groups=mesh['dp'=4,'seq'=8] {'dp','seq'}, use_global_device_ids=true, to_apply=%region_21.22.clone | all-reduce | flops 2048 | bytes 16384
  1224.7 25.8 %reduce-scatter.9.cloned.1.call-done = f32[16,512]{1,0:T(8,128)} async-done(((f32[512,512]{1,0:T(8,128)}), f32[16,512]{1,0:T(8,128)}) %reduce-scatter.9.cloned.1.call-update) | async-done | bytes 32784 | tf_op jit(solution)/shard_map/reduce_scatter | solution.py:308
  1250.5 135.9 %reduce-scatter.17.cloned.1.call-done = f32[16,512]{1,0:T(8,128)} async-done(((f32[512,512]{1,0:T(8,128)}), f32[16,512]{1,0:T(8,128)}) %reduce-scatter.17.cloned.1.call-update) | async-done | bytes 32784 | tf_op jit(solution)/shard_map/reduce_scatter | solution.py:312
  1386.4 135.6 %reduce-scatter.11.cloned.1.call-done = f32[16,512]{1,0:T(8,128)} async-done(((f32[512,512]{1,0:T(8,128)}), f32[16,512]{1,0:T(8,128)}) %reduce-scatter.11.cloned.1.call-update) | async-done | bytes 32784 | tf_op jit(solution)/shard_map/reduce_scatter | solution.py:309
  1522.0 135.7 %reduce-scatter.13.cloned.1.call-done = f32[16,512]{1,0:T(8,128)} async-done(((f32[512,512]{1,0:T(8,128)}), f32[16,512]{1,0:T(8,128)}) %reduce-scatter.13.cloned.1.call-update) | async-done | bytes 32784 | tf_op jit(solution)/shard_map/reduce_scatter | solution.py:310
  1657.8 143.2 %reduce-scatter.21.cloned.1.call-done = f32[16,2048]{1,0:T(8,128)} async-done(((f32[512,2048]{1,0:T(8,128)}), f32[16,2048]{1,0:T(8,128)}) %reduce-scatter.21.cloned.1.call-update) | async-done | bytes 131088 | tf_op jit(solution)/shard_map/reduce_scatter | solution.py:314
  1800.9 143.9 %reduce-scatter.23.cloned.1.call-done = f32[64,512]{1,0:T(8,128)} async-done(((f32[2048,512]{1,0:T(8,128)}), f32[64,512]{1,0:T(8,128)}) %reduce-scatter.23.cloned.1.call-update) | async-done | bytes 131088 | tf_op jit(solution)/shard_map/reduce_scatter | solution.py:315
  (629 shorter events, 472.2 us)
Async XLA Ops:
  7.2 590.8 %all-gather.3.cloned.1.call-start = ((), (), s32[]{:S(2)}) async-start(), calls=%async_computation.8 | async-start | bytes 2162688 | tf_op jit(solution)/shard_map/all_gather | solution.py:124
  7.9 598.5 %all-gather.5.cloned.1.call-start = ((), (), s32[]{:S(2)}) async-start(), calls=%async_computation.9 | async-start | bytes 2162688 | tf_op jit(solution)/shard_map/all_gather | solution.py:125
  8.7 1216.0 %reduce-scatter.19.cloned.1.call-start = ((), (), s32[]{:S(2)}) async-start(), calls=%async_computation.15 | async-start | bytes 1081344 | tf_op jit(solution)/shard_map/reduce_scatter | solution.py:313
  248.9 18.0 collective-permute-start
  261.8 13.7 collective-permute-start.1
  283.5 18.0 collective-permute-start
  318.1 18.0 collective-permute-start
  330.9 13.7 collective-permute-start.1
  352.7 18.0 collective-permute-start
  365.5 13.7 collective-permute-start.1
  387.2 18.0 collective-permute-start
  421.8 18.0 collective-permute-start
  434.6 13.7 collective-permute-start.1
  644.3 580.3 %reduce-scatter.15.cloned.1.call-start = ((), (), s32[]{:S(2)}) async-start(), calls=%async_computation.13 | async-start | bytes 1081344 | tf_op jit(solution)/shard_map/reduce_scatter | solution.py:311
  678.9 571.5 %reduce-scatter.9.cloned.1.call-start = ((), (), s32[]{:S(2)}) async-start(), calls=%async_computation.10 | async-start | bytes 1081344 | tf_op jit(solution)/shard_map/reduce_scatter | solution.py:308
  683.4 21.7 %collective-permute-start.4 = (bf16[2,512,8,64]{1,3,2,0:T(8,128)(2,1)}, bf16[2,512,8,64]{1,3,2,0:T(8,128)(2,1)}, u32[]{:S(2)}, u32[]{:S(2)}) collective-permute-start(bf16[2,512,8,64]{1,3,2,0:T(8,128)(2,1)} %get-tuple-element.1322), channel_id=1, source_target_pairs={{0,1},{1,2},{2,3},{3,4},{4,5},{5,6},{6,7},{7,0},{8,9},{9,10},{10,1... | collective-permute-start | bytes 3145736 | tf_op jit(solution)/shard_map/while/body/eval_jaxpr/ppermute | solution.py:25
  683.7 29.8 %collective-permute-start.5 = (bf16[2,512,8,64]{1,3,2,0:T(8,128)(2,1)}, bf16[2,512,8,64]{1,3,2,0:T(8,128)(2,1)}, u32[]{:S(2)}, u32[]{:S(2)}) collective-permute-start(bf16[2,512,8,64]{1,3,2,0:T(8,128)(2,1)} %get-tuple-element.1323), channel_id=1, source_target_pairs={{0,1},{1,2},{2,3},{3,4},{4,5},{5,6},{6,7},{7,0},{8,9},{9,10},{10,1... | collective-permute-start | bytes 3145736 | tf_op jit(solution)/shard_map/while/body/eval_jaxpr/ppermute | solution.py:25
  722.8 25.4 %collective-permute-start.2 = (bf16[2,512,8,64]{1,3,2,0:T(8,128)(2,1)}, bf16[2,512,8,64]{1,3,2,0:T(8,128)(2,1)S(1)}, u32[]{:S(2)}, u32[]{:S(2)}) collective-permute-start(bf16[2,512,8,64]{1,3,2,0:T(8,128)(2,1)} %get-tuple-element.1320), channel_id=1, source_target_pairs={{0,1},{1,2},{2,3},{3,4},{4,5},{5,6},{6,7},{8,9},{9,10},{10,11},{11... | collective-permute-start | bytes 3145736 | tf_op jit(solution)/shard_map/while/body/eval_jaxpr/ppermute | solution.py:19
  742.4 14.9 collective-permute-start.3
  746.8 21.8 %collective-permute-start.4 = (bf16[2,512,8,64]{1,3,2,0:T(8,128)(2,1)}, bf16[2,512,8,64]{1,3,2,0:T(8,128)(2,1)}, u32[]{:S(2)}, u32[]{:S(2)}) collective-permute-start(bf16[2,512,8,64]{1,3,2,0:T(8,128)(2,1)} %get-tuple-element.1322), channel_id=1, source_target_pairs={{0,1},{1,2},{2,3},{3,4},{4,5},{5,6},{6,7},{7,0},{8,9},{9,10},{10,1... | collective-permute-start | bytes 3145736 | tf_op jit(solution)/shard_map/while/body/eval_jaxpr/ppermute | solution.py:25
  746.9 28.6 %collective-permute-start.5 = (bf16[2,512,8,64]{1,3,2,0:T(8,128)(2,1)}, bf16[2,512,8,64]{1,3,2,0:T(8,128)(2,1)}, u32[]{:S(2)}, u32[]{:S(2)}) collective-permute-start(bf16[2,512,8,64]{1,3,2,0:T(8,128)(2,1)} %get-tuple-element.1323), channel_id=1, source_target_pairs={{0,1},{1,2},{2,3},{3,4},{4,5},{5,6},{6,7},{7,0},{8,9},{9,10},{10,1... | collective-permute-start | bytes 3145736 | tf_op jit(solution)/shard_map/while/body/eval_jaxpr/ppermute | solution.py:25
  785.3 25.3 %collective-permute-start.2 = (bf16[2,512,8,64]{1,3,2,0:T(8,128)(2,1)}, bf16[2,512,8,64]{1,3,2,0:T(8,128)(2,1)S(1)}, u32[]{:S(2)}, u32[]{:S(2)}) collective-permute-start(bf16[2,512,8,64]{1,3,2,0:T(8,128)(2,1)} %get-tuple-element.1320), channel_id=1, source_target_pairs={{0,1},{1,2},{2,3},{3,4},{4,5},{5,6},{6,7},{8,9},{9,10},{10,11},{11... | collective-permute-start | bytes 3145736 | tf_op jit(solution)/shard_map/while/body/eval_jaxpr/ppermute | solution.py:19
  805.1 14.6 collective-permute-start.3
  809.5 21.5 %collective-permute-start.4 = (bf16[2,512,8,64]{1,3,2,0:T(8,128)(2,1)}, bf16[2,512,8,64]{1,3,2,0:T(8,128)(2,1)}, u32[]{:S(2)}, u32[]{:S(2)}) collective-permute-start(bf16[2,512,8,64]{1,3,2,0:T(8,128)(2,1)} %get-tuple-element.1322), channel_id=1, source_target_pairs={{0,1},{1,2},{2,3},{3,4},{4,5},{5,6},{6,7},{7,0},{8,9},{9,10},{10,1... | collective-permute-start | bytes 3145736 | tf_op jit(solution)/shard_map/while/body/eval_jaxpr/ppermute | solution.py:25
  809.6 29.9 %collective-permute-start.5 = (bf16[2,512,8,64]{1,3,2,0:T(8,128)(2,1)}, bf16[2,512,8,64]{1,3,2,0:T(8,128)(2,1)}, u32[]{:S(2)}, u32[]{:S(2)}) collective-permute-start(bf16[2,512,8,64]{1,3,2,0:T(8,128)(2,1)} %get-tuple-element.1323), channel_id=1, source_target_pairs={{0,1},{1,2},{2,3},{3,4},{4,5},{5,6},{6,7},{7,0},{8,9},{9,10},{10,1... | collective-permute-start | bytes 3145736 | tf_op jit(solution)/shard_map/while/body/eval_jaxpr/ppermute | solution.py:25
  848.9 25.3 %collective-permute-start.2 = (bf16[2,512,8,64]{1,3,2,0:T(8,128)(2,1)}, bf16[2,512,8,64]{1,3,2,0:T(8,128)(2,1)S(1)}, u32[]{:S(2)}, u32[]{:S(2)}) collective-permute-start(bf16[2,512,8,64]{1,3,2,0:T(8,128)(2,1)} %get-tuple-element.1320), channel_id=1, source_target_pairs={{0,1},{1,2},{2,3},{3,4},{4,5},{5,6},{6,7},{8,9},{9,10},{10,11},{11... | collective-permute-start | bytes 3145736 | tf_op jit(solution)/shard_map/while/body/eval_jaxpr/ppermute | solution.py:19
  868.8 14.6 collective-permute-start.3
  873.2 21.5 %collective-permute-start.4 = (bf16[2,512,8,64]{1,3,2,0:T(8,128)(2,1)}, bf16[2,512,8,64]{1,3,2,0:T(8,128)(2,1)}, u32[]{:S(2)}, u32[]{:S(2)}) collective-permute-start(bf16[2,512,8,64]{1,3,2,0:T(8,128)(2,1)} %get-tuple-element.1322), channel_id=1, source_target_pairs={{0,1},{1,2},{2,3},{3,4},{4,5},{5,6},{6,7},{7,0},{8,9},{9,10},{10,1... | collective-permute-start | bytes 3145736 | tf_op jit(solution)/shard_map/while/body/eval_jaxpr/ppermute | solution.py:25
  873.2 29.4 %collective-permute-start.5 = (bf16[2,512,8,64]{1,3,2,0:T(8,128)(2,1)}, bf16[2,512,8,64]{1,3,2,0:T(8,128)(2,1)}, u32[]{:S(2)}, u32[]{:S(2)}) collective-permute-start(bf16[2,512,8,64]{1,3,2,0:T(8,128)(2,1)} %get-tuple-element.1323), channel_id=1, source_target_pairs={{0,1},{1,2},{2,3},{3,4},{4,5},{5,6},{6,7},{7,0},{8,9},{9,10},{10,1... | collective-permute-start | bytes 3145736 | tf_op jit(solution)/shard_map/while/body/eval_jaxpr/ppermute | solution.py:25
  912.0 25.6 %collective-permute-start.2 = (bf16[2,512,8,64]{1,3,2,0:T(8,128)(2,1)}, bf16[2,512,8,64]{1,3,2,0:T(8,128)(2,1)S(1)}, u32[]{:S(2)}, u32[]{:S(2)}) collective-permute-start(bf16[2,512,8,64]{1,3,2,0:T(8,128)(2,1)} %get-tuple-element.1320), channel_id=1, source_target_pairs={{0,1},{1,2},{2,3},{3,4},{4,5},{5,6},{6,7},{8,9},{9,10},{10,11},{11... | collective-permute-start | bytes 3145736 | tf_op jit(solution)/shard_map/while/body/eval_jaxpr/ppermute | solution.py:19
  932.1 14.6 collective-permute-start.3
  936.5 21.5 %collective-permute-start.4 = (bf16[2,512,8,64]{1,3,2,0:T(8,128)(2,1)}, bf16[2,512,8,64]{1,3,2,0:T(8,128)(2,1)}, u32[]{:S(2)}, u32[]{:S(2)}) collective-permute-start(bf16[2,512,8,64]{1,3,2,0:T(8,128)(2,1)} %get-tuple-element.1322), channel_id=1, source_target_pairs={{0,1},{1,2},{2,3},{3,4},{4,5},{5,6},{6,7},{7,0},{8,9},{9,10},{10,1... | collective-permute-start | bytes 3145736 | tf_op jit(solution)/shard_map/while/body/eval_jaxpr/ppermute | solution.py:25
  936.6 27.9 %collective-permute-start.5 = (bf16[2,512,8,64]{1,3,2,0:T(8,128)(2,1)}, bf16[2,512,8,64]{1,3,2,0:T(8,128)(2,1)}, u32[]{:S(2)}, u32[]{:S(2)}) collective-permute-start(bf16[2,512,8,64]{1,3,2,0:T(8,128)(2,1)} %get-tuple-element.1323), channel_id=1, source_target_pairs={{0,1},{1,2},{2,3},{3,4},{4,5},{5,6},{6,7},{7,0},{8,9},{9,10},{10,1... | collective-permute-start | bytes 3145736 | tf_op jit(solution)/shard_map/while/body/eval_jaxpr/ppermute | solution.py:25
  974.6 22.4 %collective-permute-start.2 = (bf16[2,512,8,64]{1,3,2,0:T(8,128)(2,1)}, bf16[2,512,8,64]{1,3,2,0:T(8,128)(2,1)S(1)}, u32[]{:S(2)}, u32[]{:S(2)}) collective-permute-start(bf16[2,512,8,64]{1,3,2,0:T(8,128)(2,1)} %get-tuple-element.1320), channel_id=1, source_target_pairs={{0,1},{1,2},{2,3},{3,4},{4,5},{5,6},{6,7},{8,9},{9,10},{10,11},{11... | collective-permute-start | bytes 3145736 | tf_op jit(solution)/shard_map/while/body/eval_jaxpr/ppermute | solution.py:19
  991.6 14.6 collective-permute-start.3
  996.0 21.5 %collective-permute-start.4 = (bf16[2,512,8,64]{1,3,2,0:T(8,128)(2,1)}, bf16[2,512,8,64]{1,3,2,0:T(8,128)(2,1)}, u32[]{:S(2)}, u32[]{:S(2)}) collective-permute-start(bf16[2,512,8,64]{1,3,2,0:T(8,128)(2,1)} %get-tuple-element.1322), channel_id=1, source_target_pairs={{0,1},{1,2},{2,3},{3,4},{4,5},{5,6},{6,7},{7,0},{8,9},{9,10},{10,1... | collective-permute-start | bytes 3145736 | tf_op jit(solution)/shard_map/while/body/eval_jaxpr/ppermute | solution.py:25
  996.0 27.9 %collective-permute-start.5 = (bf16[2,512,8,64]{1,3,2,0:T(8,128)(2,1)}, bf16[2,512,8,64]{1,3,2,0:T(8,128)(2,1)}, u32[]{:S(2)}, u32[]{:S(2)}) collective-permute-start(bf16[2,512,8,64]{1,3,2,0:T(8,128)(2,1)} %get-tuple-element.1323), channel_id=1, source_target_pairs={{0,1},{1,2},{2,3},{3,4},{4,5},{5,6},{6,7},{7,0},{8,9},{9,10},{10,1... | collective-permute-start | bytes 3145736 | tf_op jit(solution)/shard_map/while/body/eval_jaxpr/ppermute | solution.py:25
  1034.1 22.4 %collective-permute-start.2 = (bf16[2,512,8,64]{1,3,2,0:T(8,128)(2,1)}, bf16[2,512,8,64]{1,3,2,0:T(8,128)(2,1)S(1)}, u32[]{:S(2)}, u32[]{:S(2)}) collective-permute-start(bf16[2,512,8,64]{1,3,2,0:T(8,128)(2,1)} %get-tuple-element.1320), channel_id=1, source_target_pairs={{0,1},{1,2},{2,3},{3,4},{4,5},{5,6},{6,7},{8,9},{9,10},{10,11},{11... | collective-permute-start | bytes 3145736 | tf_op jit(solution)/shard_map/while/body/eval_jaxpr/ppermute | solution.py:19
  1051.1 14.6 collective-permute-start.3
  1055.5 21.5 %collective-permute-start.4 = (bf16[2,512,8,64]{1,3,2,0:T(8,128)(2,1)}, bf16[2,512,8,64]{1,3,2,0:T(8,128)(2,1)}, u32[]{:S(2)}, u32[]{:S(2)}) collective-permute-start(bf16[2,512,8,64]{1,3,2,0:T(8,128)(2,1)} %get-tuple-element.1322), channel_id=1, source_target_pairs={{0,1},{1,2},{2,3},{3,4},{4,5},{5,6},{6,7},{7,0},{8,9},{9,10},{10,1... | collective-permute-start | bytes 3145736 | tf_op jit(solution)/shard_map/while/body/eval_jaxpr/ppermute | solution.py:25
  1055.5 27.9 %collective-permute-start.5 = (bf16[2,512,8,64]{1,3,2,0:T(8,128)(2,1)}, bf16[2,512,8,64]{1,3,2,0:T(8,128)(2,1)}, u32[]{:S(2)}, u32[]{:S(2)}) collective-permute-start(bf16[2,512,8,64]{1,3,2,0:T(8,128)(2,1)} %get-tuple-element.1323), channel_id=1, source_target_pairs={{0,1},{1,2},{2,3},{3,4},{4,5},{5,6},{6,7},{7,0},{8,9},{9,10},{10,1... | collective-permute-start | bytes 3145736 | tf_op jit(solution)/shard_map/while/body/eval_jaxpr/ppermute | solution.py:25
  1099.4 287.0 %reduce-scatter.17.cloned.1.call-start = ((), (), s32[]{:S(2)}) async-start(), calls=%async_computation.14 | async-start | bytes 1081344 | tf_op jit(solution)/shard_map/reduce_scatter | solution.py:312
  1101.2 420.8 %reduce-scatter.11.cloned.1.call-start = ((), (), s32[]{:S(2)}) async-start(), calls=%async_computation.11 | async-start | bytes 1081344 | tf_op jit(solution)/shard_map/reduce_scatter | solution.py:309
  1101.3 17.6 collective-permute-start.6
  1123.0 534.8 %reduce-scatter.13.cloned.1.call-start = ((), (), s32[]{:S(2)}) async-start(), calls=%async_computation.12 | async-start | bytes 1081344 | tf_op jit(solution)/shard_map/reduce_scatter | solution.py:310
  1123.1 17.3 collective-permute-start.7
  1144.5 656.5 %reduce-scatter.21.cloned.1.call-start = ((), (), s32[]{:S(2)}) async-start(), calls=%async_computation.16 | async-start | bytes 4325376 | tf_op jit(solution)/shard_map/reduce_scatter | solution.py:314
  1151.3 793.6 %reduce-scatter.23.cloned.1.call-start = ((), (), s32[]{:S(2)}) async-start(), calls=%async_computation.17 | async-start | bytes 4325376 | tf_op jit(solution)/shard_map/reduce_scatter | solution.py:315
  (119 other events, 1825.1 us)
Sparse Core Ops, SparseCore 0:
  11.0 59.3 all-gather.2
  73.4 55.5 all-gather.4
  644.5 135.2 reduce-scatter.18
  782.5 138.9 reduce-scatter.14
  1099.5 150.9 reduce-scatter.8
  1253.1 133.2 reduce-scatter.16
  1389.2 132.7 reduce-scatter.10
  1524.8 132.8 reduce-scatter.12
  1660.6 140.2 reduce-scatter.20
  1803.6 141.1 reduce-scatter.22
where the time goes:
time: 1960 us; the launch traced here: 1950 us
  waiting for transfers between devices  734 us (37%)
  matrix products  409 us (21%)
  blocking collectives  350 us (18%)
  starting transfers between devices  281 us (14%)
  local copies, waits for them, and re-layouts  97.8 us (5%)
  other arithmetic  62.3 us (3%)
    ppermute x28, starting transfers between devices, from_behind(): return lax.ppermute(x, axis, pairs)  251 us
    reduce_scatter x1, waiting for transfers between devices, shards(): lax.psum_scatter(grad_back, ('dp', 'seq'), scatter_dimension=0, tiled=True)  144 us
    reduce_scatter x1, waiting for transfers between devices, shards(): lax.psum_scatter(grad_in, ('dp', 'seq'), scatter_dimension=0, tiled=True)  143 us
    reduce_scatter x1, waiting for transfers between devices, shards(): lax.psum_scatter(grad_gate_attn, ('dp', 'seq'), scatter_dimension=0, tile...  136 us
    reduce_scatter x1, waiting for transfers between devices, shards(): lax.psum_scatter(grad_value, ('dp', 'seq'), scatter_dimension=0, tiled=True)  136 us
    reduce_scatter x1, waiting for transfers between devices, shards(): lax.psum_scatter(grad_key, ('dp', 'seq'), scatter_dimension=0, tiled=True)  136 us
    unnamed x2, blocking collectives  93.1 us
    dot_general x8, matrix products, hop_grads(): jnp.einsum('mqhd,mkhd->mhqk', grad_att, value_piece, preferred_element_ty...  77.3 us
  transfers between devices with their start and end apart: 54, of which 12 were waited for; matrix products, arithmetic and copies ran while one was open for 26% of the time, Pallas kernels for 0%

commit v1 on v0

--- a/solution.py
+++ b/solution.py
@@ -3,14 +3,883 @@
 import jax
 import jax.numpy as jnp
 from jax import lax
+from jax.experimental import pallas as pl
+from jax.experimental.pallas import tpu as pltpu
 from jax.sharding import PartitionSpec as P
 
 HEADS = 8
 HEAD_DIM = 64
 DOC_MAX = 4096
 
-
 EPS = 1e-05
+MESH = pl.DeviceIdType.MESH
+BF = jnp.bfloat16
+F32 = jnp.float32
+VMEM_LIMIT = 66_000_000
+LANES = 128
+SIDE = 64
+GELU_C = 0.7978845608028654
+GELU_A = 0.044715
+NEG = -1e30
+ANY = pl.BlockSpec(memory_space=pl.ANY)
+INVM = pl.BlockSpec(memory_space=pltpu.VMEM)
+INSM = pl.BlockSpec(memory_space=pltpu.SMEM)
+
+
+def nn(a, b):
+    return lax.dot_general(a, b, (((1,), (0,)), ((), ())), preferred_element_type=F32)
+
+
+def nt(a, b):
+    return lax.dot_general(a, b, (((1,), (1,)), ((), ())), preferred_element_type=F32)
+
+
+def tn(a, b):
+    return lax.dot_general(a, b, (((0,), (0,)), ((), ())), preferred_element_type=F32)
+
+
+def remote(src, dst, send, recv, dp, seq):
+    return pltpu.make_async_remote_copy(
+        src_ref=src, dst_ref=dst, send_sem=send, recv_sem=recv,
+        device_id=(dp, seq), device_id_type=MESH,
+    )
+
+
+def greet(peers):
+    barrier = pltpu.get_barrier_semaphore()
+    for dp, seq in peers:
+        pl.semaphore_signal(barrier, inc=1, device_id=(dp, seq), device_id_type=MESH)
+    pl.semaphore_wait(barrier, len(peers))
+
+
+def place():
+    d = lax.axis_index("dp")
+    j = lax.axis_index("seq")
+    z = j // 2
+    c = j % 2
+    dx = d + 1 - 2 * (d % 2)
+    dy = (d + 2) % 4
+    dxy = 3 - d
+    return d, j, z, c, dx, dy, dxy
+
+
+CK = 4
+
+
+def gather_kernel(x_ref, s_ref, xg_ref, wg_ref, xv, sv, lsem, wsend, wrecv, xsend, xrecv):
+    d, j, z, c, dx, dy, dxy = place()
+    g = z // 2
+    pj = j + 1 - 2 * c
+    za, zb, zc = z + 1 - 2 * (z % 2), (z + 2) % 4, 3 - z
+    near = jnp.logical_or(z == 1, z == 2)
+    far = jnp.logical_or(z == 0, z == 3)
+    ja, jb, jc = 2 * za + c, 2 * zb + c, 2 * zc + c
+    lx = pltpu.make_async_copy(x_ref.at[g], xv, lsem.at[0])
+    ls = pltpu.make_async_copy(s_ref, sv, lsem.at[1])
+    lx.start()
+    ls.start()
+    greet([(d, ja), (d, jb), (d, jc), (dx, j), (dy, j), (d, pj)])
+    rows = xv.shape[0] // CK
+    count = [0]
+    waits = []
+
+    def wcopy(slot, dp, seq, own=False):
+        i = count[0]
+        count[0] += 1
+        copy = remote(
+            s_ref if own else wg_ref.at[slot], wg_ref.at[slot], wsend.at[i], wrecv.at[slot], dp, seq
+        )
+        copy.start()
+        waits.append(copy)
+
+    def warrive(slot):
+        remote(s_ref, wg_ref.at[slot], wsend.at[0], wrecv.at[slot], d, pj).wait_recv()
+
+    def xcopy(k, part, block, dp, seq, src=None):
+        piece = pl.ds(part * rows, rows)
+        source = xg_ref.at[block, piece] if src is None else x_ref.at[src, piece]
+        return remote(
+            source, xg_ref.at[block, piece], xsend.at[k, part], xrecv.at[block, part], dp, seq
+        )
+
+    def xarrive(part, block):
+        xcopy(0, part, block, d, pj).wait_recv()
+
+    me = d * 8 + j
+    for dp, seq in [(d, ja), (d, jb), (d, jc), (dx, j), (dy, j), (d, pj)]:
+        wcopy(me, dp, seq, True)
+    xwaits = []
+    jn = 2 * (2 - g) + c
+    for part in range(CK):
+        for k, (src, seq) in enumerate([(1 - g, jn), (g, ja), (g, pj)]):
+            copy = xcopy(k, part, j, d, seq, src)
+            copy.start()
+            xwaits.append(copy)
+    lx.wait()
+    ls.wait()
+    ox = pltpu.make_async_copy(xv, xg_ref.at[j], lsem.at[0])
+    ow = pltpu.make_async_copy(sv, wg_ref.at[me], lsem.at[1])
+    ox.start()
+    ow.start()
+
+    def zarr(jz):
+        slot = d * 8 + jz
+        warrive(slot)
+        wcopy(slot, dx, j)
+        wcopy(slot, dy, j)
+        wcopy(slot, d, pj)
+
+    def xyarr(zz):
+        jz = 2 * zz + c
+        sx, sy = dx * 8 + jz, dy * 8 + jz
+        even = zz % 2 == 0
+        warrive(sx)
+        wcopy(sx, d, pj)
+        warrive(sy)
+        wcopy(sy, d, pj)
+        i = count[0]
+        count[0] += 1
+
+        def on(slot, dp):
+            return remote(wg_ref.at[slot], wg_ref.at[slot], wsend.at[i], wrecv.at[slot], dp, j)
+
+        @pl.when(even)
+        def _():
+            on(sx, dy).start()
+
+        @pl.when(jnp.logical_not(even))
+        def _():
+            on(sy, dx).start()
+
+        waits.append(on(sx, dy))
+
+    zarr(ja)
+    xyarr(z)
+    zarr(jb)
+    xyarr(za)
+    zarr(jc)
+    xyarr(zb)
+    xyarr(zc)
+    b1 = 2 * (2 - g) + c
+    b2 = 2 * (3 * (1 - g)) + c
+    for k, block in ((3, b1), (5, b2)):
+        for part in range(CK):
+            xarrive(part, block)
+            copy = xcopy(k, part, block, d, pj)
+            copy.start()
+            xwaits.append(copy)
+
+            @pl.when(near)
+            def _():
+                xcopy(k + 1, part, block, d, ja).start()
+
+    for part in range(CK):
+        xarrive(part, ja)
+        copy = xcopy(7, part, ja, d, pj)
+        copy.start()
+        xwaits.append(copy)
+    for zz in (z, za, zb, zc):
+        slot = dxy * 8 + 2 * zz + c
+        warrive(slot)
+        wcopy(slot, d, pj)
+    for dp in (d, dx, dy, dxy):
+        for zz in (z, za, zb, zc):
+            warrive(dp * 8 + 2 * zz + 1 - c)
+    for block in (j, ja, b1, b2):
+        for part in range(CK):
+            xarrive(part, block + 1 - 2 * c)
+    for copy in waits:
+        copy.wait_send()
+    for copy in xwaits:
+        copy.wait_send()
+
+    @pl.when(near)
+    def _():
+        for k, block in ((4, b1), (6, b2)):
+            for part in range(CK):
+                xcopy(k, part, block, d, ja).wait_send()
+
+    ox.wait()
+    ow.wait()
+
+
+def gather(x, shard):
+    _, rows, width = x.shape
+    return pl.pallas_call(
+        gather_kernel,
+        out_shape=(
+            jax.ShapeDtypeStruct((8, rows, width), BF),
+            jax.ShapeDtypeStruct((32,) + shard.shape, BF),
+        ),
+        in_specs=[ANY, ANY],
+        out_specs=(ANY, ANY),
+        scratch_shapes=[
+            pltpu.VMEM((rows, width), BF),
+            pltpu.VMEM(shard.shape, BF),
+            pltpu.SemaphoreType.DMA((2,)),
+            pltpu.SemaphoreType.DMA((32,)),
+            pltpu.SemaphoreType.DMA((32,)),
+            pltpu.SemaphoreType.DMA((8, CK)),
+            pltpu.SemaphoreType.DMA((8, CK)),
+        ],
+        compiler_params=pltpu.CompilerParams(collective_id=0, has_side_effects=True),
+    )(x, shard)
+
+
+def swap_kernel(a_ref, b_ref, av, lsem, send, recv):
+    d = lax.axis_index("dp")
+    j = lax.axis_index("seq")
+    load = pltpu.make_async_copy(a_ref.at[j], av, lsem)
+    load.start()
+    peers = [(d, (j + k) % 8) for k in range(1, 8)]
+    greet(peers)
+    copies = []
+    for k, (dp, seq) in enumerate(peers):
+        copy = remote(a_ref.at[seq], b_ref.at[j], send.at[k], recv.at[k], dp, seq)
+        copy.start()
+        copies.append(copy)
+    load.wait()
+    keep = pltpu.make_async_copy(av, b_ref.at[j], lsem)
+    keep.start()
+    for copy in copies:
+        copy.wait()
+    keep.wait()
+
+
+def swap(a, cid):
+    return pl.pallas_call(
+        swap_kernel,
+        out_shape=jax.ShapeDtypeStruct(a.shape, a.dtype),
+        in_specs=[ANY],
+        out_specs=ANY,
+        scratch_shapes=[
+            pltpu.VMEM(a.shape[1:], a.dtype),
+            pltpu.SemaphoreType.DMA,
+            pltpu.SemaphoreType.DMA((7,)),
+            pltpu.SemaphoreType.DMA((7,)),
+        ],
+        compiler_params=pltpu.CompilerParams(collective_id=cid, has_side_effects=True),
+    )(a)
+
+
+def lane_of(rows):
+    return lax.broadcasted_iota(jnp.int32, (rows, LANES), 1)
+
+
+def three(v):
+    a = v.astype(BF).astype(F32)
+    b = (v - a).astype(BF).astype(F32)
+    return a, b, v - a - b
+
+
+def beside(h, lane, values, parts):
+    first = SIDE * (1 - h)
+    own = (lane < SIDE) if h == 0 else (lane >= SIDE)
+    out = jnp.where(own, values, 0.0)
+    for k, part in enumerate(parts):
+        if part is not None:
+            out = jnp.where(lane == first + k, part, out)
+    return out.astype(BF)
+
+
+def attend_kernel(doc, x_ref, w_ref, gain_ref, o_ref, o32_ref, qa, ka, va):
+    blocks, rows, width = x_ref.shape
+    off = doc[0]
+    end = off + doc[1]
+    lane = lane_of(rows)
+    up = lax.broadcasted_iota(jnp.int32, (rows, 1), 0)
+    gain = gain_ref[...].astype(F32)
+
+    def project(b, _):
+        x = x_ref[b].astype(F32)
+        n = (x * lax.rsqrt(jnp.mean(x * x, -1, keepdims=True) + EPS) * gain).astype(BF)
+        p = nn(n, w_ref[...])
+        pos = b * rows + up
+        bad = jnp.where(jnp.logical_and(pos >= off, pos < end), 0.0, NEG)
+        q = p[:, :LANES].astype(BF).astype(F32) * HEAD_DIM ** (-0.5)
+        k = p[:, LANES : 2 * LANES]
+        v = p[:, 2 * LANES :]
+        for h in range(2):
+            qa[h, b] = beside(h, lane, q, (1.0,))
+            ka[h, b] = beside(h, lane, k, (bad, 1.0, 1.0, 1.0))
+            va[h, b] = beside(h, lane, v, (None, 1.0, 1.0, 1.0))
+        return 0
+
+    lax.fori_loop(0, blocks, project, 0)
+    first = off // rows
+    last = (end - 1) // rows
+    diag = lax.broadcasted_iota(jnp.int32, (rows, rows), 0) >= lax.broadcasted_iota(
+        jnp.int32, (rows, rows), 1
+    )
+
+    def one(b, _):
+        inside = jnp.logical_and(b >= first, b <= last)
+
+        @pl.when(jnp.logical_not(inside))
+        def _():
+            o_ref[b] = jnp.zeros((rows, LANES), BF)
+            o32_ref[b] = jnp.zeros((rows, LANES), F32)
+            for h in range(2):
+                qa[h, b] = beside(h, lane, qa[h, b].astype(F32), (1.0, NEG))
+
+        @pl.when(inside)
+        def _():
+            pos = b * rows + up
+            live = jnp.logical_and(pos >= off, pos < end)
+            outs = []
+            for h in range(2):
+                q = qa[h, b]
+
+                def step(kb, carry, masked=False):
+                    m, acc = carry
+                    s = nt(q, ka[h, kb])
+                    if masked:
+                        s = jnp.where(diag, s, NEG)
+                    new = jnp.maximum(m, jnp.max(s, -1, keepdims=True))
+                    p = jnp.exp(s - new).astype(BF)
+                    acc = acc * jnp.exp(m - new) + nn(p, va[h, kb])
+                    return new, acc
+
+                start = (jnp.full((rows, 1), NEG, F32), jnp.zeros((rows, LANES), F32))
+                m, acc = step(b, lax.fori_loop(first, b, step, start), True)
+                one_at = SIDE * (1 - h) + 1
+                total = acc[:, one_at : one_at + 1]
+                lse = jnp.where(live, m + jnp.log(total), -NEG)
+                a, bb, cc = three(lse)
+                qa[h, b] = beside(h, lane, q.astype(F32), (1.0, -a, -bb, -cc))
+                outs.append(jnp.where(live, acc / total, 0.0))
+            out = jnp.where(lane < SIDE, outs[0], outs[1])
+            o32_ref[b] = out
+            o_ref[b] = out.astype(BF)
+
+        return 0
+
+    lax.fori_loop(0, blocks, one, 0)
+
+
+def attend(doc, xg, w, gain):
+    blocks, rows, width = xg.shape
+    side = jax.ShapeDtypeStruct((2, blocks, rows, LANES), BF)
+    return pl.pallas_call(
+        attend_kernel,
+        out_shape=(
+            jax.ShapeDtypeStruct((blocks, rows, LANES), BF),
+            jax.ShapeDtypeStruct((blocks, rows, LANES), F32),
+            side, side, side,
+        ),
+        in_specs=[INSM, INVM, INVM, INVM],
+        out_specs=(INVM,) * 5,
+        compiler_params=pltpu.CompilerParams(vmem_limit_bytes=VMEM_LIMIT),
+    )(doc, xg, w, gain)
+
+
+def attend_back_kernel(
+    doc, x_ref, w_ref, gain_ref, o32_ref, do_ref, qa, ka, va, dn_ref, dw_ref, dgain_ref, da, dq, dk, dv
+):
+    blocks, rows, width = x_ref.shape
+    off = doc[0]
+    end = off + doc[1]
+    lane = lane_of(rows)
+    first = off // rows
+    last = (end - 1) // rows
+    low = lax.broadcasted_iota(jnp.int32, (rows, rows), 0) <= lax.broadcasted_iota(
+        jnp.int32, (rows, rows), 1
+    )
+
+    def prepare(b, _):
+        do = do_ref[b].astype(F32)
+        both = do * o32_ref[b]
+        for h in range(2):
+            own = (lane < SIDE) if h == 0 else (lane >= SIDE)
+            delta = jnp.sum(jnp.where(own, both, 0.0), -1, keepdims=True)
+            a, bb, cc = three(delta)
+            da[h, b] = beside(h, lane, do, (None, -a, -bb, -cc))
+            dq[h, b] = jnp.zeros((rows, LANES), F32)
+            dk[h, b] = jnp.zeros((rows, LANES), F32)
+            dv[h, b] = jnp.zeros((rows, LANES), F32)
+        return 0
+
+    lax.fori_loop(0, blocks, prepare, 0)
+
+    def keys(kb, _):
+        for h in range(2):
+            k = ka[h, kb]
+            v = va[h, kb]
+
+            def queries(b, carry, masked=False):
+                q = qa[h, b]
+                do = da[h, b]
+                p = jnp.exp(nt(k, q))
+                if masked:
+                    p = jnp.where(low, p, 0.0)
+                ds = (p * nt(v, do)).astype(BF)
+                dv[h, kb] += nn(p.astype(BF), do)
+                dk[h, kb] += nn(ds, q)
+                dq[h, b] += tn(ds, k)
+                return carry
+
+            queries(kb, 0, True)
+            lax.fori_loop(kb + 1, last + 1, queries, 0)
+        return 0
+
+    lax.fori_loop(first, last + 1, keys, 0)
+    gain = gain_ref[...].astype(F32)
+    dw_ref[...] = jnp.zeros_like(dw_ref)
+    dgain_ref[...] = jnp.zeros_like(dgain_ref)
+
+    def finish(b, _):
+        x = x_ref[b].astype(F32)
+        n1 = x * lax.rsqrt(jnp.mean(x * x, -1, keepdims=True) + EPS)
+        n = (n1 * gain).astype(BF)
+        left = lane < SIDE
+        q = jnp.where(left, dq[0, b], dq[1, b]) * HEAD_DIM ** (-0.5)
+        k = jnp.where(left, dk[0, b], dk[1, b])
+        v = jnp.where(left, dv[0, b], dv[1, b])
+        p = jnp.concatenate([q.astype(BF), k.astype(BF), v.astype(BF)], axis=1)
+        dw_ref[...] += tn(n, p)
+        dn = nt(p, w_ref[...])
+        dn_ref[b] = dn.astype(BF)
+        dgain_ref[...] += jnp.sum(dn * n1, 0, keepdims=True)
+        return 0
+
+    lax.fori_loop(0, blocks, finish, 0)
+
+
+def attend_back(doc, xg, w, gain, o32, do, qa, ka, va):
+    blocks, rows, width = xg.shape
+    return pl.pallas_call(
+        attend_back_kernel,
+        out_shape=(
+            jax.ShapeDtypeStruct((blocks, rows, width), BF),
+            jax.ShapeDtypeStruct((width, 3 * LANES), F32),
+            jax.ShapeDtypeStruct((1, width), F32),
+        ),
+        in_specs=[INSM] + [INVM] * 8,
+        out_specs=(INVM,) * 3,
+        scratch_shapes=[
+            pltpu.VMEM((2, blocks, rows, LANES), BF),
+            pltpu.VMEM((2, blocks, rows, LANES), F32),
+            pltpu.VMEM((2, blocks, rows, LANES), F32),
+            pltpu.VMEM((2, blocks, rows, LANES), F32),
+        ],
+        compiler_params=pltpu.CompilerParams(vmem_limit_bytes=VMEM_LIMIT),
+    )(doc, xg, w, gain, o32, do, qa, ka, va)
+
+
+def token_kernel(
+    x_ref, c_ref, a_ref, wg, vec, out_ref, da_ref, dh_ref, dn_ref, g_ref, v_ref,
+    gp, act, g_out, g_ga, g_gf, g_in, g_back,
+):
+    step = pl.program_id(0)
+    rows, width = x_ref.shape[1:]
+    ff = gp.shape[0]
+    per = width // 32
+
+    def weight(lo):
+        return wg[:, lo : lo + per, :].reshape(width, width)
+
+    def back(k):
+        n = wg.shape[0] // ff
+        return wg[k * n : (k + 1) * n, 10 * per : 10 * per + ff * per, :].reshape(width, width)
+
+    @pl.when(step == 0)
+    def _():
+        for ref in (g_out, g_ga, g_gf, g_in, g_back, v_ref):
+            ref[...] = jnp.zeros_like(ref)
+
+    x = x_ref[0].astype(F32)
+    gain_a, gain_f = vec[0:1].astype(F32), vec[1:2].astype(F32)
+    shift_a, shift_f = vec[2:3].astype(F32), vec[3:4].astype(F32)
+    n1 = x * lax.rsqrt(jnp.mean(x * x, -1, keepdims=True) + EPS)
+    na = (n1 * gain_a).astype(BF)
+    ga = jax.nn.sigmoid(nn(na, weight(4 * per)) + shift_a)
+    att = jnp.concatenate([a_ref[i] for i in range(4)], axis=1)
+    br = nn(att, weight(3 * per))
+    hid = ga * br + (1.0 - ga) * x
+    r2 = lax.rsqrt(jnp.mean(hid * hid, -1, keepdims=True) + EPS)
+    n2 = hid * r2
+    nf = (n2 * gain_f).astype(BF)
+    bf = jnp.zeros((rows, width), F32)
+    for k in range(ff):
+        pre = nn(nf, weight((6 + k) * per))
+        sq = pre * pre
+        t = jnp.tanh(GELU_C * pre * (1.0 + GELU_A * sq))
+        half = 0.5 * (1.0 + t)
+        act[k] = (pre * half).astype(BF)
+        gp[k] = half + 0.5 * pre * (1.0 - t * t) * (GELU_C * (1.0 + 3.0 * GELU_A * sq))
+        bf += nn(act[k], back(k))
+    gf = jax.nn.sigmoid(nn(nf, weight(5 * per)) + shift_f)
+    out_ref[0] = (gf * bf + (1.0 - gf) * hid).astype(BF)
+    c = c_ref[0].astype(F32)
+    dlf = (c * (bf - hid) * gf * (1.0 - gf)).astype(BF)
+    dbf = (c * gf).astype(BF)
+    dnf = nt(dlf, weight(5 * per))
+    g_gf[...] += tn(nf, dlf)
+    for k in range(ff):
+        dpre = (nt(dbf, back(k)) * gp[k]).astype(BF)
+        g_back[k] += tn(act[k], dbf)
+        g_in[k] += tn(nf, dpre)
+        dnf += nt(dpre, weight((6 + k) * per))
+    g2 = dnf * gain_f
+    dh = c * (1.0 - gf) + r2 * (g2 - n2 * jnp.mean(g2 * n2, -1, keepdims=True))
+    dba = (dh * ga).astype(BF)
+    dla = (dh * (br - x) * ga * (1.0 - ga)).astype(BF)
+    g_out[...] += tn(att, dba)
+    g_ga[...] += tn(na, dla)
+    datt = nt(dba, weight(3 * per)).astype(BF)
+    for i in range(4):
+        da_ref[i] = datt[:, i * LANES : (i + 1) * LANES]
+    dna = nt(dla, weight(4 * per))
+    dh_ref[0] = dh * (1.0 - ga)
+    dn_ref[0] = dna
+    v_ref[0:1] += jnp.sum(dna * n1, 0, keepdims=True)
+    v_ref[1:2] += jnp.sum(dnf * n2, 0, keepdims=True)
+    v_ref[2:3] += jnp.sum(dla.astype(F32), 0, keepdims=True)
+    v_ref[3:4] += jnp.sum(dlf.astype(F32), 0, keepdims=True)
+
+    @pl.when(step == pl.num_programs(0) - 1)
+    def _():
+        def put(lo, value):
+            g_ref[:, lo : lo + per, :] = value.astype(BF).reshape(32, per, width)
+
+        put(0, g_out[...])
+        put(per, g_ga[...])
+        put(2 * per, g_gf[...])
+        for k in range(ff):
+            put((3 + k) * per, g_in[k])
+            n = 32 // ff
+            g_ref[k * n : (k + 1) * n, (3 + ff) * per :, :] = (
+                g_back[k].astype(BF).reshape(n, ff * per, width)
+            )
+
+
+def tokens(x, cot, att, wg, vec):
+    micro, rows, width = x.shape
+    ff = 4
+    per = width // 32
+    tok = pl.BlockSpec((1, rows, width), lambda i: (i, 0, 0))
+    head = pl.BlockSpec((4, rows, LANES), lambda i: (i, 0, 0))
+
+    def whole(shape):
+        return pl.BlockSpec(shape, lambda i: (0,) * len(shape), pipeline_mode=pl.Buffered(1))
+
+    grads = (32, (3 + 2 * ff) * per, width)
+    return pl.pallas_call(
+        token_kernel,
+        grid=(micro,),
+        out_shape=(
+            jax.ShapeDtypeStruct((micro, rows, width), BF),
+            jax.ShapeDtypeStruct((4 * micro, rows, LANES), BF),
+            jax.ShapeDtypeStruct((micro, rows, width), F32),
+            jax.ShapeDtypeStruct((micro, rows, width), F32),
+            jax.ShapeDtypeStruct(grads, BF),
+            jax.ShapeDtypeStruct((8, width), F32),
+        ),
+        in_specs=[tok, tok, head, whole(wg.shape), whole(vec.shape)],
+        out_specs=(tok, head, tok, tok, whole(grads), whole((8, width))),
+        scratch_shapes=[
+            pltpu.VMEM((ff, rows, width), F32),
+            pltpu.VMEM((ff, rows, width), BF),
+            pltpu.VMEM((width, width), F32),
+            pltpu.VMEM((width, width), F32),
+            pltpu.VMEM((width, width), F32),
+            pltpu.VMEM((ff, width, width), F32),
+            pltpu.VMEM((ff, width, width), F32),
+        ],
+        compiler_params=pltpu.CompilerParams(vmem_limit_bytes=VMEM_LIMIT),
+    )(x, cot, att, wg, vec)
+
+
+def add_into(dst, src):
+    rows = dst.shape[0]
+    n = rows // 16
+    per = 16 * max(k for k in range(1, 9) if n % k == 0)
+
+    def body(i, _):
+        piece = pl.ds(i * per, per)
+        dst[piece, :] = (dst[piece, :].astype(F32) + src[piece, :].astype(F32)).astype(BF)
+        return 0
+
+    lax.fori_loop(0, rows // per, body, 0)
+
+
+def reduce_kernel(
+    p_ref, g_ref, h_ref, dn_ref, gf_ref, gq_ref, gv_ref,
+    acc, b1, b2, b3, b4, qs, q1, q2, hb, own,
+    l1, l2, lo, s1, r1, s2, r2, s3, r3, s4, r4, ps, pr, ts, tr, us, ur, hs, hr,
+):
+    d, j, z, c, dx, dy, dxy = place()
+    me = d * 8 + j
+    g = z // 2
+    pj = j + 1 - 2 * c
+    za, zb, zc = z + 1 - 2 * (z % 2), (z + 2) % 4, 3 - z
+    ja, jb, jc = 2 * za + c, 2 * zb + c, 2 * zc + c
+    near = jnp.logical_or(z == 1, z == 2)
+    far = jnp.logical_or(z == 0, z == 3)
+    w3, w2, wn, wf = 3 * (1 - g), 2 - g, 1 + g, 3 * g
+    order = (w3, wf, w2, wn)
+    first = [(zz, dp) for zz in range(4) for dp in ((dx, dxy) if zz % 2 == 0 else (dy, dxy))]
+    rest = [(zz, dp) for zz in range(4) for dp in ((d, dy) if zz % 2 == 0 else (d, dx))]
+
+    ploads = []
+    for k, zz in enumerate(order):
+        copy = pltpu.make_async_copy(p_ref.at[2 * zz + c], qs.at[zz], l1.at[k])
+        copy.start()
+        ploads.append(copy)
+    gloads = []
+    for k, (zz, dp) in enumerate(first + rest):
+        copy = pltpu.make_async_copy(g_ref.at[dp * 8 + 2 * zz + c], acc.at[dp * 4 + zz], l2.at[k])
+        copy.start()
+        gloads.append(copy)
+    hload = pltpu.make_async_copy(h_ref.at[me], hb.at[me], lo.at[0])
+    hload.start()
+
+    barrier = pltpu.get_barrier_semaphore()
+
+    def hello(k, _):
+        slot = (me + k) % 32
+        pl.semaphore_signal(
+            barrier, inc=1, device_id=(slot // 8, slot % 8), device_id_type=MESH
+        )
+        return 0
+
+    lax.fori_loop(1, 32, hello, 0)
+    pl.semaphore_wait(barrier, 31)
+
+    sent = []
+
+    def go(copy):
+        copy.start()
+        sent.append(copy)
+
+    def pcopy(zz):
+        return remote(p_ref.at[2 * zz + 1 - c], q1.at[zz], ps.at[zz], pr.at[zz], d, pj)
+
+    def gcopy(zz, dp):
+        i = dp * 4 + zz
+        return remote(g_ref.at[dp * 8 + 2 * zz + 1 - c], b1.at[i], s1.at[i], r1.at[i], d, pj)
+
+    for zz in order:
+        go(pcopy(zz))
+    for zz, dp in first + rest:
+        go(gcopy(zz, dp))
+
+    def hcopy(k):
+        slot = (me + k) % 32
+        return remote(h_ref.at[slot], hb.at[me], hs.at[k], hr.at[me], slot // 8, slot % 8)
+
+    def hstart(k, _):
+        hcopy(k).start()
+        return 0
+
+    lax.fori_loop(1, 32, hstart, 0)
+
+    def tcopy(zz):
+        return remote(qs.at[zz], q2.at[zz], ts.at[zz], tr.at[zz], d, ja)
+
+    for k, zz in enumerate(order):
+        ploads[k].wait()
+        pcopy(zz).wait_recv()
+        add_into(qs.at[zz], q1.at[zz])
+        if k == 1:
+
+            @pl.when(near)
+            def _():
+                tcopy(zz).start()
+        else:
+
+            @pl.when(far)
+            def _():
+                tcopy(zz).start()
+
+    def stage2(zz, dp):
+        i = dp * 4 + zz
+        to = dx if zz % 2 == 0 else dy
+        return remote(acc.at[i], b2.at[i], s2.at[i], r2.at[i], to, j)
+
+    def stage3(zz):
+        to = dy if zz % 2 == 0 else dx
+        return remote(acc.at[to * 4 + zz], b3.at[zz], s3.at[zz], r3.at[zz], to, j)
+
+    def stage4(k, zz, jz):
+        return remote(acc.at[d * 4 + zz], b4.at[z], s4.at[k], r4.at[z], d, jz)
+
+    def ucopy(k, zz):
+        return remote(qs.at[zz], dn_ref.at[g], us.at[k], ur.at[0], d, 2 * zz + c)
+
+    def pass_on(k, zz):
+        @pl.when(near)
+        def _():
+            tcopy(zz).wait_recv()
+            add_into(qs.at[zz], q2.at[zz])
+            ucopy(k, zz).start()
+
+    for k, (zz, dp) in enumerate(first):
+        gloads[k].wait()
+        gcopy(zz, dp).wait_recv()
+        add_into(acc.at[dp * 4 + zz], b1.at[dp * 4 + zz])
+        go(stage2(zz, dp))
+    for k, (zz, dp) in enumerate(rest):
+        gloads[len(first) + k].wait()
+        gcopy(zz, dp).wait_recv()
+        add_into(acc.at[dp * 4 + zz], b1.at[dp * 4 + zz])
+    pass_on(0, w3)
+    for pick in (1, 0):
+        for zz in range(4):
+            dp = (d, dy if zz % 2 == 0 else dx)[pick]
+            stage2(zz, dp).wait_recv()
+            add_into(acc.at[dp * 4 + zz], b2.at[dp * 4 + zz])
+            if pick:
+                go(stage3(zz))
+    for zz in range(4):
+        stage3(zz).wait_recv()
+        add_into(acc.at[d * 4 + zz], b3.at[zz])
+    for k, (zz, jz) in enumerate(((za, ja), (zb, jb), (zc, jc))):
+        go(stage4(k, zz, jz))
+    pass_on(1, w2)
+    tcopy(z).wait_recv()
+
+    def mine(i, _):
+        piece = pl.ds(i * 128, 128)
+        own[piece, :] = (qs[z, piece, :].astype(F32) + q2[z, piece, :].astype(F32)).astype(BF)
+        return 0
+
+    lax.fori_loop(0, own.shape[0] // 128, mine, 0)
+    keep = pltpu.make_async_copy(own, dn_ref.at[g], lo.at[1])
+    keep.start()
+    for zz in (za, zb, zc):
+        remote(acc.at[0], b4.at[zz], s4.at[0], r4.at[zz], d, ja).wait_recv()
+    gf_ref[...] = (
+        acc[d * 4 + z].astype(F32)
+        + b4[za].astype(F32) + b4[zb].astype(F32) + b4[zc].astype(F32)
+    )
+    hload.wait()
+
+    def harrive(k, _):
+        slot = (me + k) % 32
+        remote(h_ref.at[0], hb.at[slot], hs.at[0], hr.at[slot], d, pj).wait_recv()
+        return 0
+
+    lax.fori_loop(1, 32, harrive, 0)
+    per = gq_ref.shape[1]
+    total = jnp.zeros(gv_ref.shape, F32)
+    for hi in range(4):
+        part = jnp.zeros((per, 3 * LANES), F32)
+        for k in range(8):
+            slot = (k // 2) * 8 + (k % 2) * 4 + hi
+            part += hb[slot, :per].astype(F32)
+            total += hb[slot, per:].astype(F32)
+        for m in range(3):
+            gq_ref[m, :, hi * LANES : (hi + 1) * LANES] = part[:, m * LANES : (m + 1) * LANES]
+    gv_ref[...] = total
+    ucopy(0, w3).wait_recv()
+    for copy in sent:
+        copy.wait_send()
+
+    def hsent(k, _):
+        hcopy(k).wait_send()
+        return 0
+
+    lax.fori_loop(1, 32, hsent, 0)
+
+    @pl.when(near)
+    def _():
+        tcopy(wf).wait_send()
+        ucopy(0, w3).wait_send()
+        ucopy(1, w2).wait_send()
+
+    @pl.when(far)
+    def _():
+        for zz in (w3, w2, wn):
+            tcopy(zz).wait_send()
+
+    keep.wait()
+
+
+def reduce(p, grads, h):
+    blocks, rows, width = p.shape
+    g = grads.shape[1:]
+    per = h.shape[1] // 2
+    dma = pltpu.SemaphoreType.DMA
+    return pl.pallas_call(
+        reduce_kernel,
+        out_shape=(
+            jax.ShapeDtypeStruct((2, rows, width), BF),
+            jax.ShapeDtypeStruct(g, F32),
+            jax.ShapeDtypeStruct((3, per, width), F32),
+            jax.ShapeDtypeStruct((per, 3 * LANES), F32),
+        ),
+        in_specs=[ANY, ANY, ANY],
+        out_specs=(ANY, INVM, INVM, INVM),
+        scratch_shapes=[
+            pltpu.VMEM((16,) + g, BF),
+            pltpu.VMEM((16,) + g, BF),
+            pltpu.VMEM((16,) + g, BF),
+            pltpu.VMEM((4,) + g, BF),
+            pltpu.VMEM((4,) + g, BF),
+            pltpu.VMEM((4, rows, width), BF),
+            pltpu.VMEM((4, rows, width), BF),
+            pltpu.VMEM((4, rows, width), BF),
+            pltpu.VMEM((32,) + h.shape[1:], BF),
+            pltpu.VMEM((rows, width), BF),
+            dma((4,)), dma((16,)), dma((2,)),
+            dma((16,)), dma((16,)), dma((16,)), dma((16,)), dma((4,)), dma((4,)), dma((4,)), dma((4,)),
+            dma((4,)), dma((4,)), dma((4,)), dma((4,)), dma((2,)), dma((1,)), dma((32,)), dma((32,)),
+        ],
+        compiler_params=pltpu.CompilerParams(
+            collective_id=3, has_side_effects=True, vmem_limit_bytes=VMEM_LIMIT
+        ),
+    )(p, grads, h)
+
+
+def by_heads(
+    layer_input, cotangent, doc_len, doc_offset,
+    w_query, w_key, w_value, w_out, w_gate_attn, w_gate_ffn, w_in, w_back,
+    norm_attn, norm_ffn, bias_attn, bias_ffn,
+):
+    micro, _, rows, width = layer_input.shape
+    per = w_query.shape[0]
+    ff = w_in.shape[1] // width
+    j = lax.axis_index("seq")
+    g = j // 4
+    hi = j % 4
+    x = layer_input[:, 0]
+    cot = cotangent[:, 0]
+    vec = jnp.stack([norm_attn, norm_ffn, bias_attn, bias_ffn])
+    shard = jnp.concatenate(
+        [w_query, w_key, w_value, w_out, w_gate_attn, w_gate_ffn]
+        + [w_in[:, k * width : (k + 1) * width] for k in range(ff)]
+        + [w_back, jnp.pad(vec, ((0, 12), (0, width - per)))]
+    )
+    xg, wg = gather(x, shard)
+    vecs = wg[:, -16:-12, :per].transpose(1, 0, 2).reshape(4, width)
+    w = lax.dynamic_slice(wg, (0, 0, hi * LANES), (32, 3 * per, LANES))
+    w = w.reshape(32, 3, per, LANES).transpose(0, 2, 1, 3).reshape(width, 3 * LANES)
+    doc = jnp.stack([doc_offset[g, 0, 0], doc_len[g, 0, 0]])
+    gain = vecs[0:1]
+    o, o32, qa, ka, va = attend(doc, xg, w, gain)
+    att = swap(o, 1)
+    out, datt, dh, dna, grads, sums = tokens(x, cot, att, wg, vecs)
+    do = swap(datt, 2)
+    dn, dw, dgain = attend_back(doc, xg, w, gain, o32, do, qa, ka, va)
+    sums = jnp.concatenate([sums[0:1] + dgain, sums[1:4]]).reshape(4, 32, per).transpose(1, 0, 2)
+    sums = jnp.pad(sums, ((0, 0), (0, per - 4), (0, 3 * LANES - per)))
+    h = jnp.concatenate([dw.reshape(32, per, 3 * LANES), sums], axis=1).astype(BF)
+    dn, gf, gq, gv = reduce(dn, grads, h)
+    x32 = x.astype(F32)
+    r1 = lax.rsqrt(jnp.mean(x32 * x32, -1, keepdims=True) + EPS)
+    n1 = x32 * r1
+    g1 = (dna + dn.astype(F32)) * gain.astype(F32)
+    grad = dh + r1 * (g1 - n1 * jnp.mean(g1 * n1, -1, keepdims=True))
+    return (
+        out[:, None],
+        grad[:, None],
+        gq[0], gq[1], gq[2],
+        gf[:per], gf[per : 2 * per], gf[2 * per : 3 * per],
+        gf[3 * per : (3 + ff) * per].reshape(ff, per, width).transpose(1, 0, 2).reshape(per, ff * width),
+        gf[(3 + ff) * per :],
+        gv[0, :per], gv[1, :per], gv[2, :per], gv[3, :per],
+    )
 
 
 def from_behind(x, axis, by):
@@ -355,8 +1224,21 @@
         P(("dp", "seq")),
         P(("dp", "seq")),
     )
+    def pick(layer_input, *others):
+        micro, _, rows, width = layer_input.shape
+        fits = (
+            dict(mesh.shape) == {"dp": 4, "seq": 8}
+            and micro == 2
+            and others[1].shape[2] == 1
+            and width == HEADS * HEAD_DIM
+            and width == 4 * LANES
+            and rows % 128 == 0
+            and others[10].shape == (width // 8, width)
+        )
+        return (by_heads if fits else shards)(layer_input, *others)
+
     return jax.shard_map(
-        shards,
+        pick,
         mesh=mesh,
         in_specs=placed,
         out_specs=(

time: 1960 us -> 401 us (0.20)
  waiting for transfers between devices: 734 us -> 0 us
  matrix products: 409 us -> 0 us
  Pallas kernels: 0 us -> 362 us
  blocking collectives: 350 us -> 0 us
  starting transfers between devices: 281 us -> 0 us
  local copies, waits for them, and re-layouts: 97.8 us -> 20.4 us
  other arithmetic: 62.3 us -> 13.7 us
    reduce_scatter x8 -> x0, waiting for transfers between devices: 720 us -> none  [the longest x1 144 us: shards(): lax.psum_scatter(grad_back, ('dp', 'seq'), scatter_dimension=0, tiled=True)]
    dot_general x79 -> x0, matrix products: 409 us -> none  [the longest x8 77.3 us: hop_grads(): jnp.einsum('mqhd,mkhd->mhqk', grad_att, value_piece, preferred_element_ty...]
    pallas_call x0 -> x7, Pallas kernels: none -> 362 us  [the longest x1 79.7 us: attend_back(): pl.pallas_call(attend_back_kernel, out_shape=(jax.ShapeDtypeStruct((block...]
    ppermute x44 -> x0, starting transfers between devices: 281 us -> none  [the longest x28 251 us: from_behind(): return lax.ppermute(x, axis, pairs)]
    all_gather x6 -> x0, blocking collectives: 257 us -> none  [the longest x1 51.6 us: shards(): lax.all_gather(w_out, ('dp', 'seq'), axis=0, tiled=True)]
    unnamed x2 -> x0, blocking collectives: 93.1 us -> none
    while x105 -> x0, local copies, waits for them, and re-layouts: 48.1 us -> none
    reduce_sum x10 -> x2, other arithmetic: 37.4 us -> 4.51 us  [the longest x1 3.01 us: by_heads(): grad = dh + r1 * (g1 - n1 * jnp.mean(g1 * n1, -1, keepdims=True))]
  transfers between devices with their start and end apart: 54 -> 0, of which waited for: 12 -> 0; matrix products, arithmetic and copies ran while one was open for 26% -> 0% of each run, Pallas kernels for 0% -> 0%
where the time goes in v1:
time: 401 us; the launch traced here: 397 us
  Pallas kernels  362 us (90%)
  local copies, waits for them, and re-layouts  20.4 us (5%)
  other arithmetic  13.7 us (3%)
    pallas_call x1, Pallas kernels, attend_back(): pl.pallas_call(attend_back_kernel, out_shape=(jax.ShapeDtypeStruct((block...  79.7 us
    pallas_call x1, Pallas kernels, reduce(): pl.pallas_call(reduce_kernel, out_shape=(jax.ShapeDtypeStruct((2, rows, w...  73.2 us
    pallas_call x1, Pallas kernels, gather(): pl.pallas_call(gather_kernel, out_shape=(jax.ShapeDtypeStruct((8, rows, w...  70.8 us
    pallas_call x1, Pallas kernels, attend(): pl.pallas_call(attend_kernel, out_shape=(jax.ShapeDtypeStruct((blocks, ro...  59.8 us
    pallas_call x2, Pallas kernels, swap(): pl.pallas_call(swap_kernel, out_shape=jax.ShapeDtypeStruct(a.shape, a.dty...  46.5 us
    pallas_call x1, Pallas kernels, tokens(): pl.pallas_call(token_kernel, grid=(micro,), out_shape=(jax.ShapeDtypeStru...  32.1 us
    unnamed x22, local copies, waits for them, and re-layouts  9.92 us

profile of v1, /device:TPU:0, one launch (start us, length us, event | category | flops | bytes accessed | tf_op | source)
XLA Modules:
  0.0 397.0 jit_solution(9693501099423014535)
XLA Ops:
  0.7 1.3 constant_dynamic-slice_fusion.1
  1.9 1.9 pad_add_fusion.doc
  3.8 1.5 fusion.7
  5.3 0.7 constant_dynamic-update-slice_fusion.11
  6.1 0.7 constant_dynamic-update-slice_fusion.10
  6.8 0.7 constant_dynamic-update-slice_fusion.9
  7.5 0.7 constant_dynamic-update-slice_fusion.8
  8.2 0.7 constant_dynamic-update-slice_fusion.7
  8.9 0.7 constant_dynamic-update-slice_fusion.6
  9.7 0.7 constant_dynamic-update-slice_fusion.5
  10.4 0.7 constant_dynamic-update-slice_fusion.4
  11.1 0.7 constant_dynamic-update-slice_fusion.3
  11.8 0.7 constant_dynamic-update-slice_fusion.2
  12.5 0.8 constant_dynamic-update-slice_fusion.1
  13.4 0.7 constant_dynamic-update-slice_fusion.s_ref
  14.1 0.0 copy-start.4
  14.1 0.7 copy-done.4
  14.8 70.8 %shard_map.263 = (bf16[8,512,512]{2,1,0:T(8,128)(2,1)}, bf16[32,240,512]{2,1,0:T(8,128)(2,1)}) custom-call(bf16[2,512,512]{2,1,0:T(8,128)(2,1)} %bitcast.51, bf16[240,512]{1,0:T(8,128)(2,1)} %copy-done.4), custom_call_target="tpu_custom_call" | custom-call | tf_op jit(solution)/shard_map/pallas_call | solution.py:208
  85.6 0.9 slice_bitcast_fusion.3
  86.5 0.1 slice_reduce_fusion
  86.5 0.7 slice.70.gain_ref
  87.3 0.1 reshape.81
  87.4 0.7 reshape.76.vec
  88.1 1.0 constant_dynamic-slice_fusion
  89.1 0.3 copy.34
  89.4 0.8 copy.44
  90.2 59.8 %shard_map.264 = (bf16[8,512,128]{2,1,0:T(8,128)(2,1)}, f32[8,512,128]{2,1,0:T(8,128)}, bf16[2,8,512,128]{3,2,1,0:T(8,128)(2,1)}, bf16[2,8,512,128]{3,2,1,0:T(8,128)(2,1)}, bf16[2,8,512,128]{3,2,1,0:T(8,128)(2,1)}) custom-call(s32[2]{0:T(128)} %pad_add_fusion.doc, bf16[8,512,512]{2,1,0:T(8,128)(2,1)} %get-tuple-element.34.x_ref, bf16[512,384]{1,0:T(8,128)(2,1)} %bitcast.53, ...), custom_call_target="tpu_custom_call" | custom-call | tf_op jit(solution)/shard_map/pallas_call | solution.py:363
  149.9 20.3 %shard_map.265.a_ref = bf16[8,512,128]{2,1,0:T(8,128)(2,1)} custom-call(bf16[8,512,128]{2,1,0:T(8,128)(2,1)} %get-tuple-element.36.a_ref), custom_call_target="tpu_custom_call" | custom-call | tf_op jit(solution)/shard_map/pallas_call | solution.py:250
  170.2 32.1 %shard_map.266 = (bf16[2,512,512]{2,1,0:T(8,128)(2,1)}, bf16[8,512,128]{2,1,0:T(8,128)(2,1)}, f32[2,512,512]{2,1,0:T(8,128)}, f32[2,512,512]{2,1,0:T(8,128)}, bf...) custom-call(bf16[2,512,512]{2,1,0:T(8,128)(2,1)} %bitcast.52, bf16[2,512,512]{2,1,0:T(8,128)(2,1)} %bitcast.58, ...), custom_call_target="tpu_custom_call" | custom-call | tf_op jit(solution)/shard_map/pallas_call | solution.py:567
  202.3 0.7 slice.103
  203.0 26.2 %shard_map.267.do_ref = bf16[8,512,128]{2,1,0:T(8,128)(2,1)} custom-call(bf16[8,512,128]{2,1,0:T(8,128)(2,1)} %get-tuple-element.41.a_ref), custom_call_target="tpu_custom_call" | custom-call | tf_op jit(solution)/shard_map/pallas_call | solution.py:250
  229.3 79.7 %shard_map.268 = (bf16[8,512,512]{2,1,0:T(8,128)(2,1)}, f32[512,384]{1,0:T(8,128)}, f32[1,512]{1,0:T(1,128)}) custom-call(s32[2]{0:T(128)} %pad_add_fusion.doc, bf16[8,512,512]{2,1,0:T(8,128)(2,1)} %get-tuple-element.34.x_ref, bf16[512,384]{1,0:T(8,128)(2,1)} %bitcast.54, bf16[1,512]{1,0:T(2,128)(2,1)} %slice.70.gain_ref, ...), custom_call_target="tpu_custom_call" | custom-call | tf_op jit(solution)/shard_map/pallas_call | solution.py:450
  309.0 0.7 add_convert_fusion
  309.8 0.1 reshape.78
  309.9 1.2 convert.17
  311.1 1.0 fusion.9.h_ref
  312.0 73.2 %shard_map.269 = (bf16[2,512,512]{2,1,0:T(8,128)(2,1)}, f32[176,512]{1,0:T(8,128)}, f32[3,16,512]{2,1,0:T(8,128)}, f32[16,384]{1,0:T(8,128)}) custom-call(bf16[8,512,512]{2,1,0:T(8,128)(2,1)} %get-tuple-element.45.p_ref, bf16[32,176,512]{2,1,0:T(8,128)(2,1)} %get-tuple-element.46.g_ref, bf16[32,32,384]{2,1,0:T(8,128)(2,1)} %fusion.9.h_ref), custom_call_target="tpu_custom_call" | custom-call | tf_op jit(solution)/shard_map/pallas_call | solution.py:804
  385.2 1.4 slice_bitcast_fusion
  386.6 1.4 slice_bitcast_fusion.4
  388.0 3.0 fusion.2
  391.0 0.0 copy-done
  391.0 0.1 copy-done.1
  391.2 0.3 copy-done.2
  391.4 3.6 fusion.6
  395.0 0.0 copy-done.3
  395.0 0.6 fusion.23
  395.7 0.7 fusion.22
  396.3 0.7 copy.40
  (10 shorter events, 0.1 us)
Async XLA Ops:
  14.1 0.7 copy-start.4
  388.0 3.0 copy-start
  388.0 3.2 copy-start.1
  388.0 3.4 copy-start.2
  391.4 3.6 copy-start.3

commit v2 on v1

--- a/solution.py
+++ b/solution.py
@@ -262,6 +262,9 @@
     )(a)
 
 
+LOG2E = 1.4426950408889634
+
+
 def lane_of(rows):
     return lax.broadcasted_iota(jnp.int32, (rows, LANES), 1)
 
@@ -282,13 +285,22 @@
     return out.astype(BF)
 
 
-def attend_kernel(doc, x_ref, w_ref, gain_ref, o_ref, o32_ref, qa, ka, va):
+def upper(rows):
+    return lax.broadcasted_iota(jnp.int32, (rows, rows), 0) <= lax.broadcasted_iota(
+        jnp.int32, (rows, rows), 1
+    )
+
+
+def attend_kernel(doc, x_ref, w_ref, gain_ref, o_ref, o32_ref, qa, ka, va, vt):
     blocks, rows, width = x_ref.shape
     off = doc[0]
     end = off + doc[1]
     lane = lane_of(rows)
     up = lax.broadcasted_iota(jnp.int32, (rows, 1), 0)
+    along = lax.broadcasted_iota(jnp.int32, (1, rows), 1)
     gain = gain_ref[...].astype(F32)
+    tall = lax.broadcasted_iota(jnp.int32, (16, rows), 0)
+    ones = jnp.where(tall == 0, 1.0, 0.0).astype(BF)
 
     def project(b, _):
         x = x_ref[b].astype(F32)
@@ -296,62 +308,61 @@
         p = nn(n, w_ref[...])
         pos = b * rows + up
         bad = jnp.where(jnp.logical_and(pos >= off, pos < end), 0.0, NEG)
-        q = p[:, :LANES].astype(BF).astype(F32) * HEAD_DIM ** (-0.5)
+        q = p[:, :LANES] * (HEAD_DIM ** (-0.5) * LOG2E)
         k = p[:, LANES : 2 * LANES]
         v = p[:, 2 * LANES :]
         for h in range(2):
             qa[h, b] = beside(h, lane, q, (1.0,))
             ka[h, b] = beside(h, lane, k, (bad, 1.0, 1.0, 1.0))
             va[h, b] = beside(h, lane, v, (None, 1.0, 1.0, 1.0))
+        turned = v.astype(BF).T
+        for h in range(2):
+            vt[h, b, :SIDE] = turned[h * SIDE : (h + 1) * SIDE]
+            vt[h, b, SIDE:] = ones
         return 0
 
     lax.fori_loop(0, blocks, project, 0)
-    first = off // rows
-    last = (end - 1) // rows
-    diag = lax.broadcasted_iota(jnp.int32, (rows, rows), 0) >= lax.broadcasted_iota(
-        jnp.int32, (rows, rows), 1
-    )
+    keep = upper(rows)
+    sub = lax.broadcasted_iota(jnp.int32, (LANES, rows), 0)
 
     def one(b, _):
-        inside = jnp.logical_and(b >= first, b <= last)
-
-        @pl.when(jnp.logical_not(inside))
-        def _():
-            o_ref[b] = jnp.zeros((rows, LANES), BF)
-            o32_ref[b] = jnp.zeros((rows, LANES), F32)
-            for h in range(2):
-                qa[h, b] = beside(h, lane, qa[h, b].astype(F32), (1.0, NEG))
-
-        @pl.when(inside)
-        def _():
-            pos = b * rows + up
-            live = jnp.logical_and(pos >= off, pos < end)
-            outs = []
-            for h in range(2):
-                q = qa[h, b]
-
-                def step(kb, carry, masked=False):
-                    m, acc = carry
-                    s = nt(q, ka[h, kb])
-                    if masked:
-                        s = jnp.where(diag, s, NEG)
-                    new = jnp.maximum(m, jnp.max(s, -1, keepdims=True))
-                    p = jnp.exp(s - new).astype(BF)
-                    acc = acc * jnp.exp(m - new) + nn(p, va[h, kb])
-                    return new, acc
-
-                start = (jnp.full((rows, 1), NEG, F32), jnp.zeros((rows, LANES), F32))
-                m, acc = step(b, lax.fori_loop(first, b, step, start), True)
-                one_at = SIDE * (1 - h) + 1
-                total = acc[:, one_at : one_at + 1]
-                lse = jnp.where(live, m + jnp.log(total), -NEG)
-                a, bb, cc = three(lse)
-                qa[h, b] = beside(h, lane, q.astype(F32), (1.0, -a, -bb, -cc))
-                outs.append(jnp.where(live, acc / total, 0.0))
-            out = jnp.where(lane < SIDE, outs[0], outs[1])
-            o32_ref[b] = out
-            o_ref[b] = out.astype(BF)
-
+        pos = b * rows + along
+        live = jnp.logical_and(pos >= off, pos < end)
+
+        def score(h, kb, masked):
+            s = nt(ka[h, kb], qa[h, b])
+            return jnp.where(keep, s, NEG) if masked else s
+
+        def step(kb, carry, masked=False):
+            ss = [score(h, kb, masked) for h in range(2)]
+            new = [jnp.maximum(carry[h][0], jnp.max(ss[h], 0, keepdims=True)) for h in range(2)]
+            ps = [jnp.exp2(ss[h] - new[h]).astype(BF) for h in range(2)]
+            return tuple(
+                (new[h], carry[h][1] * jnp.exp2(carry[h][0] - new[h]) + nn(vt[h, kb], ps[h])) for h in range(2)
+            )
+
+        start = ((jnp.full((1, rows), NEG, F32), jnp.zeros((SIDE + 16, rows), F32)),) * 2
+        done = step(b, lax.fori_loop(0, b, step, start), True)
+        m = [v[0] for v in done]
+        acc = [v[1] for v in done]
+        outs = []
+        for h in range(2):
+            total = acc[h][SIDE : SIDE + 1]
+            lse = jnp.where(live, m[h] + jnp.log2(total), -NEG)
+            own = jnp.where(live, acc[h][:SIDE] / total, 0.0)
+            parts = three(lse)
+            side = jnp.zeros((SIDE, rows), F32)
+            for k in range(3):
+                side = jnp.where(sub[:SIDE] == k + 1, -parts[k], side)
+            both = (own, side) if h == 0 else (side, own)
+            out = jnp.concatenate(both, axis=0).T
+            first = SIDE * (1 - h)
+            aug = jnp.logical_and(lane > first, lane < first + 4)
+            qa[h, b] = jnp.where(aug, out, qa[h, b].astype(F32)).astype(BF)
+            outs.append(out)
+        out = jnp.where(lane < SIDE, outs[0], outs[1])
+        o32_ref[b] = out
+        o_ref[b] = out.astype(BF)
         return 0
 
     lax.fori_loop(0, blocks, one, 0)
@@ -369,101 +380,10 @@
         ),
         in_specs=[INSM, INVM, INVM, INVM],
         out_specs=(INVM,) * 5,
+        scratch_shapes=[pltpu.VMEM((2, blocks, SIDE + 16, rows), BF)],
         compiler_params=pltpu.CompilerParams(vmem_limit_bytes=VMEM_LIMIT),
+        name="attend",
     )(doc, xg, w, gain)
-
-
-def attend_back_kernel(
-    doc, x_ref, w_ref, gain_ref, o32_ref, do_ref, qa, ka, va, dn_ref, dw_ref, dgain_ref, da, dq, dk, dv
-):
-    blocks, rows, width = x_ref.shape
-    off = doc[0]
-    end = off + doc[1]
-    lane = lane_of(rows)
-    first = off // rows
-    last = (end - 1) // rows
-    low = lax.broadcasted_iota(jnp.int32, (rows, rows), 0) <= lax.broadcasted_iota(
-        jnp.int32, (rows, rows), 1
-    )
-
-    def prepare(b, _):
-        do = do_ref[b].astype(F32)
-        both = do * o32_ref[b]
-        for h in range(2):
-            own = (lane < SIDE) if h == 0 else (lane >= SIDE)
-            delta = jnp.sum(jnp.where(own, both, 0.0), -1, keepdims=True)
-            a, bb, cc = three(delta)
-            da[h, b] = beside(h, lane, do, (None, -a, -bb, -cc))
-            dq[h, b] = jnp.zeros((rows, LANES), F32)
-            dk[h, b] = jnp.zeros((rows, LANES), F32)
-            dv[h, b] = jnp.zeros((rows, LANES), F32)
-        return 0
-
-    lax.fori_loop(0, blocks, prepare, 0)
-
-    def keys(kb, _):
-        for h in range(2):
-            k = ka[h, kb]
-            v = va[h, kb]
-
-            def queries(b, carry, masked=False):
-                q = qa[h, b]
-                do = da[h, b]
-                p = jnp.exp(nt(k, q))
-                if masked:
-                    p = jnp.where(low, p, 0.0)
-                ds = (p * nt(v, do)).astype(BF)
-                dv[h, kb] += nn(p.astype(BF), do)
-                dk[h, kb] += nn(ds, q)
-                dq[h, b] += tn(ds, k)
-                return carry
-
-            queries(kb, 0, True)
-            lax.fori_loop(kb + 1, last + 1, queries, 0)
-        return 0
-
-    lax.fori_loop(first, last + 1, keys, 0)
-    gain = gain_ref[...].astype(F32)
-    dw_ref[...] = jnp.zeros_like(dw_ref)
-    dgain_ref[...] = jnp.zeros_like(dgain_ref)
-
-    def finish(b, _):
-        x = x_ref[b].astype(F32)
-        n1 = x * lax.rsqrt(jnp.mean(x * x, -1, keepdims=True) + EPS)
-        n = (n1 * gain).astype(BF)
-        left = lane < SIDE
-        q = jnp.where(left, dq[0, b], dq[1, b]) * HEAD_DIM ** (-0.5)
-        k = jnp.where(left, dk[0, b], dk[1, b])
-        v = jnp.where(left, dv[0, b], dv[1, b])
-        p = jnp.concatenate([q.astype(BF), k.astype(BF), v.astype(BF)], axis=1)
-        dw_ref[...] += tn(n, p)
-        dn = nt(p, w_ref[...])
-        dn_ref[b] = dn.astype(BF)
-        dgain_ref[...] += jnp.sum(dn * n1, 0, keepdims=True)
-        return 0
-
-    lax.fori_loop(0, blocks, finish, 0)
-
-
-def attend_back(doc, xg, w, gain, o32, do, qa, ka, va):
-    blocks, rows, width = xg.shape
-    return pl.pallas_call(
-        attend_back_kernel,
-        out_shape=(
-            jax.ShapeDtypeStruct((blocks, rows, width), BF),
-            jax.ShapeDtypeStruct((width, 3 * LANES), F32),
-            jax.ShapeDtypeStruct((1, width), F32),
-        ),
-        in_specs=[INSM] + [INVM] * 8,
-        out_specs=(INVM,) * 3,
-        scratch_shapes=[
-            pltpu.VMEM((2, blocks, rows, LANES), BF),
-            pltpu.VMEM((2, blocks, rows, LANES), F32),
-            pltpu.VMEM((2, blocks, rows, LANES), F32),
-            pltpu.VMEM((2, blocks, rows, LANES), F32),
-        ],
-        compiler_params=pltpu.CompilerParams(vmem_limit_bytes=VMEM_LIMIT),
-    )(doc, xg, w, gain, o32, do, qa, ka, va)
 
 
 def token_kernel(
@@ -603,11 +523,15 @@
     lax.fori_loop(0, rows // per, body, 0)
 
 
-def reduce_kernel(
-    p_ref, g_ref, h_ref, dn_ref, gf_ref, gq_ref, gv_ref,
-    acc, b1, b2, b3, b4, qs, q1, q2, hb, own,
-    l1, l2, lo, s1, r1, s2, r2, s3, r3, s4, r4, ps, pr, ts, tr, us, ur, hs, hr,
+def attend_back_kernel(
+    x_ref, w_ref, gain_ref, o32_ref, do_ref, qa, ka, va, sum_ref, g_ref,
+    dn_ref, gf_ref, gq_ref, gv_ref,
+    da, qt, kt, dot, dq, dk, dv, dw, pb, hs_buf, vs_buf,
+    acc, b1, b2, b3, b4, q1, q2, hb, vb, own,
+    l2, lo, s1, r1, s2, r2, s3, r3, s4, r4, ps, pr, ts, tr, us, ur, hs, hr, vs, vr,
 ):
+    blocks, rows, width = x_ref.shape
+    per = width // 32
     d, j, z, c, dx, dy, dxy = place()
     me = d * 8 + j
     g = z // 2
@@ -617,22 +541,14 @@
     near = jnp.logical_or(z == 1, z == 2)
     far = jnp.logical_or(z == 0, z == 3)
     w3, w2, wn, wf = 3 * (1 - g), 2 - g, 1 + g, 3 * g
-    order = (w3, wf, w2, wn)
     first = [(zz, dp) for zz in range(4) for dp in ((dx, dxy) if zz % 2 == 0 else (dy, dxy))]
     rest = [(zz, dp) for zz in range(4) for dp in ((d, dy) if zz % 2 == 0 else (d, dx))]
 
-    ploads = []
-    for k, zz in enumerate(order):
-        copy = pltpu.make_async_copy(p_ref.at[2 * zz + c], qs.at[zz], l1.at[k])
-        copy.start()
-        ploads.append(copy)
     gloads = []
     for k, (zz, dp) in enumerate(first + rest):
         copy = pltpu.make_async_copy(g_ref.at[dp * 8 + 2 * zz + c], acc.at[dp * 4 + zz], l2.at[k])
         copy.start()
         gloads.append(copy)
-    hload = pltpu.make_async_copy(h_ref.at[me], hb.at[me], lo.at[0])
-    hload.start()
 
     barrier = pltpu.get_barrier_semaphore()
 
@@ -646,51 +562,9 @@
     lax.fori_loop(1, 32, hello, 0)
     pl.semaphore_wait(barrier, 31)
 
-    sent = []
-
-    def go(copy):
-        copy.start()
-        sent.append(copy)
-
-    def pcopy(zz):
-        return remote(p_ref.at[2 * zz + 1 - c], q1.at[zz], ps.at[zz], pr.at[zz], d, pj)
-
     def gcopy(zz, dp):
         i = dp * 4 + zz
         return remote(g_ref.at[dp * 8 + 2 * zz + 1 - c], b1.at[i], s1.at[i], r1.at[i], d, pj)
-
-    for zz in order:
-        go(pcopy(zz))
-    for zz, dp in first + rest:
-        go(gcopy(zz, dp))
-
-    def hcopy(k):
-        slot = (me + k) % 32
-        return remote(h_ref.at[slot], hb.at[me], hs.at[k], hr.at[me], slot // 8, slot % 8)
-
-    def hstart(k, _):
-        hcopy(k).start()
-        return 0
-
-    lax.fori_loop(1, 32, hstart, 0)
-
-    def tcopy(zz):
-        return remote(qs.at[zz], q2.at[zz], ts.at[zz], tr.at[zz], d, ja)
-
-    for k, zz in enumerate(order):
-        ploads[k].wait()
-        pcopy(zz).wait_recv()
-        add_into(qs.at[zz], q1.at[zz])
-        if k == 1:
-
-            @pl.when(near)
-            def _():
-                tcopy(zz).start()
-        else:
-
-            @pl.when(far)
-            def _():
-                tcopy(zz).start()
 
     def stage2(zz, dp):
         i = dp * 4 + zz
@@ -704,80 +578,219 @@
     def stage4(k, zz, jz):
         return remote(acc.at[d * 4 + zz], b4.at[z], s4.at[k], r4.at[z], d, jz)
 
+    def pcopy(zz):
+        return remote(pb.at[2 * zz + 1 - c], q1.at[zz], ps.at[zz], pr.at[zz], d, pj)
+
+    def tcopy(zz):
+        return remote(pb.at[2 * zz + c], q2.at[zz], ts.at[zz], tr.at[zz], d, ja)
+
     def ucopy(k, zz):
-        return remote(qs.at[zz], dn_ref.at[g], us.at[k], ur.at[0], d, 2 * zz + c)
+        return remote(pb.at[2 * zz + c], dn_ref.at[g], us.at[k], ur.at[0], d, 2 * zz + c)
+
+    def hcopy(k):
+        slot = (me + k) % 32
+        return remote(hs_buf.at[slot], hb.at[me], hs.at[k], hr.at[me], slot // 8, slot % 8)
+
+    def vcopy(k):
+        slot = (me + k) % 32
+        return remote(vs_buf, vb.at[me], vs.at[k], vr.at[me], slot // 8, slot % 8)
+
+    for zz, dp in first + rest:
+        gcopy(zz, dp).start()
+
+    def sums1():
+        for k, (zz, dp) in enumerate(first + rest):
+            gloads[k].wait()
+            gcopy(zz, dp).wait_recv()
+            add_into(acc.at[dp * 4 + zz], b1.at[dp * 4 + zz])
+            if k < len(first):
+                stage2(zz, dp).start()
+
+    def sums2():
+        for pick in (1, 0):
+            for zz in range(4):
+                dp = (d, dy if zz % 2 == 0 else dx)[pick]
+                stage2(zz, dp).wait_recv()
+                add_into(acc.at[dp * 4 + zz], b2.at[dp * 4 + zz])
+                if pick:
+                    stage3(zz).start()
+
+    def sums3():
+        for zz in range(4):
+            stage3(zz).wait_recv()
+            add_into(acc.at[d * 4 + zz], b3.at[zz])
+        for k, (zz, jz) in enumerate(((za, ja), (zb, jb), (zc, jc))):
+            stage4(k, zz, jz).start()
+
+    def both_cores(zz):
+        pcopy(zz).wait_recv()
+        add_into(pb.at[2 * zz + c], q1.at[zz])
 
     def pass_on(k, zz):
         @pl.when(near)
         def _():
             tcopy(zz).wait_recv()
-            add_into(qs.at[zz], q2.at[zz])
+            add_into(pb.at[2 * zz + c], q2.at[zz])
             ucopy(k, zz).start()
 
-    for k, (zz, dp) in enumerate(first):
-        gloads[k].wait()
-        gcopy(zz, dp).wait_recv()
-        add_into(acc.at[dp * 4 + zz], b1.at[dp * 4 + zz])
-        go(stage2(zz, dp))
-    for k, (zz, dp) in enumerate(rest):
-        gloads[len(first) + k].wait()
-        gcopy(zz, dp).wait_recv()
-        add_into(acc.at[dp * 4 + zz], b1.at[dp * 4 + zz])
-    pass_on(0, w3)
-    for pick in (1, 0):
-        for zz in range(4):
-            dp = (d, dy if zz % 2 == 0 else dx)[pick]
-            stage2(zz, dp).wait_recv()
-            add_into(acc.at[dp * 4 + zz], b2.at[dp * 4 + zz])
-            if pick:
-                go(stage3(zz))
-    for zz in range(4):
-        stage3(zz).wait_recv()
-        add_into(acc.at[d * 4 + zz], b3.at[zz])
-    for k, (zz, jz) in enumerate(((za, ja), (zb, jb), (zc, jc))):
-        go(stage4(k, zz, jz))
-    pass_on(1, w2)
-    tcopy(z).wait_recv()
-
-    def mine(i, _):
-        piece = pl.ds(i * 128, 128)
-        own[piece, :] = (qs[z, piece, :].astype(F32) + q2[z, piece, :].astype(F32)).astype(BF)
+    def to_near(zz):
+        @pl.when(far)
+        def _():
+            tcopy(zz).start()
+
+    def event0():
+        both_cores(w3)
+        to_near(w3)
+
+    def event1():
+        both_cores(w2)
+        to_near(w2)
+        pass_on(0, w3)
+
+    def event2():
+        both_cores(wn)
+        to_near(wn)
+        pass_on(1, w2)
+
+    events = {(0, 3): sums1, (1, 4): sums2, (2, 0): event0, (2, 3): sums3, (4, 0): event1, (6, 0): event2}
+
+    lane = lane_of(rows)
+    low = upper(rows)
+    left = lane < SIDE
+
+    def prepare(b, _):
+        do = do_ref[b].astype(F32)
+        both = do * o32_ref[b]
+        for h in range(2):
+            mine = left if h == 0 else jnp.logical_not(left)
+            delta = jnp.sum(jnp.where(mine, both, 0.0), -1, keepdims=True)
+            a, bb, cc = three(delta)
+            da[h, b] = beside(h, lane, do, (None, -a, -bb, -cc))
+        qt[b] = jnp.where(left, qa[0, b], qa[1, b]).T
+        kt[b] = jnp.where(left, ka[0, b], ka[1, b]).T
+        dot[b] = do_ref[b].T
+        dq[b] = jnp.zeros((LANES, rows), F32)
+        dk[b] = jnp.zeros((LANES, rows), F32)
+        dv[b] = jnp.zeros((LANES, rows), F32)
         return 0
 
-    lax.fori_loop(0, own.shape[0] // 128, mine, 0)
-    keep = pltpu.make_async_copy(own, dn_ref.at[g], lo.at[1])
-    keep.start()
+    lax.fori_loop(0, blocks, prepare, 0)
+    gain = gain_ref[...].astype(F32)
+    dw[...] = jnp.zeros_like(dw)
+    vs_buf[...] = sum_ref[...]
+
+    def finish(b):
+        x = x_ref[b].astype(F32)
+        n1 = x * lax.rsqrt(jnp.mean(x * x, -1, keepdims=True) + EPS)
+        n = (n1 * gain).astype(BF)
+        q = (dq[b] * HEAD_DIM ** (-0.5)).astype(BF)
+        k = (dk[b] * (1.0 / LOG2E)).astype(BF)
+        pt = jnp.concatenate([q, k, dv[b].astype(BF)], axis=0)
+        dw[...] += nn(pt, n)
+        dn = nt(pt.T, w_ref[...])
+        pb[b] = dn.astype(BF)
+        vs_buf[0:1] += jnp.sum(dn * n1, 0, keepdims=True)
+
+    def pair(kb, b, masked=False):
+        for h in range(2):
+            part = slice(h * SIDE, (h + 1) * SIDE)
+            p = jnp.exp2(nt(ka[h, kb], qa[h, b]))
+            if masked:
+                p = jnp.where(low, p, 0.0)
+            ds = (p * nt(va[h, kb], da[h, b])).astype(BF)
+            dv[kb, part] += nt(dot[b, part], p.astype(BF))
+            dk[kb, part] += nt(qt[b, part], ds)
+            dq[b, part] += nn(kt[kb, part], ds)
+
+    def outer(i, _):
+        o = g * i + (1 - g) * (blocks - 1 - i)
+        pair(o, o, True)
+
+        def inner(t, _):
+            pair(g * o + (1 - g) * (o - 1 - t), g * (o + 1 + t) + (1 - g) * o)
+            for (ei, et), event in events.items():
+                pl.when(jnp.logical_and(i == ei, t == et))(event)
+            return 0
+
+        lax.fori_loop(0, blocks - 1 - i, inner, 0)
+        finish(o)
+
+        @pl.when(o % 2 != c)
+        def _():
+            pcopy(o // 2).start()
+
+        return 0
+
+    lax.fori_loop(0, blocks, outer, 0)
+    wide = dw[...].T.astype(BF)
+    hs_buf[...] = wide.reshape(32, per, 3 * LANES)
+    keep_h = pltpu.make_async_copy(hs_buf.at[me], hb.at[me], lo.at[0])
+    keep_v = pltpu.make_async_copy(vs_buf, vb.at[me], lo.at[1])
+    keep_h.start()
+    keep_v.start()
+
+    def hstart(k, _):
+        hcopy(k).start()
+        vcopy(k).start()
+        return 0
+
+    both_cores(wf)
+
+    @pl.when(near)
+    def _():
+        tcopy(wf).start()
+
+    lax.fori_loop(1, 32, hstart, 0)
     for zz in (za, zb, zc):
         remote(acc.at[0], b4.at[zz], s4.at[0], r4.at[zz], d, ja).wait_recv()
     gf_ref[...] = (
         acc[d * 4 + z].astype(F32)
         + b4[za].astype(F32) + b4[zb].astype(F32) + b4[zc].astype(F32)
     )
-    hload.wait()
+    keep_h.wait()
+    keep_v.wait()
 
     def harrive(k, _):
         slot = (me + k) % 32
-        remote(h_ref.at[0], hb.at[slot], hs.at[0], hr.at[slot], d, pj).wait_recv()
+        remote(hs_buf.at[0], hb.at[slot], hs.at[0], hr.at[slot], d, pj).wait_recv()
+        remote(vs_buf, vb.at[slot], vs.at[0], vr.at[slot], d, pj).wait_recv()
         return 0
 
     lax.fori_loop(1, 32, harrive, 0)
-    per = gq_ref.shape[1]
     total = jnp.zeros(gv_ref.shape, F32)
     for hi in range(4):
         part = jnp.zeros((per, 3 * LANES), F32)
         for k in range(8):
             slot = (k // 2) * 8 + (k % 2) * 4 + hi
-            part += hb[slot, :per].astype(F32)
-            total += hb[slot, per:].astype(F32)
+            part += hb[slot].astype(F32)
+            total += vb[slot]
         for m in range(3):
             gq_ref[m, :, hi * LANES : (hi + 1) * LANES] = part[:, m * LANES : (m + 1) * LANES]
     gv_ref[...] = total
+    tcopy(z).wait_recv()
+
+    def mine(i, _):
+        piece = pl.ds(i * 128, 128)
+        own[piece, :] = (pb[j, piece, :].astype(F32) + q2[z, piece, :].astype(F32)).astype(BF)
+        return 0
+
+    lax.fori_loop(0, rows // 128, mine, 0)
+    keep = pltpu.make_async_copy(own, dn_ref.at[g], lo.at[2])
+    keep.start()
     ucopy(0, w3).wait_recv()
-    for copy in sent:
-        copy.wait_send()
+    for zz, dp in first + rest:
+        gcopy(zz, dp).wait_send()
+    for zz, dp in first:
+        stage2(zz, dp).wait_send()
+    for zz in range(4):
+        stage3(zz).wait_send()
+        pcopy(zz).wait_send()
+    for k, (zz, jz) in enumerate(((za, ja), (zb, jb), (zc, jc))):
+        stage4(k, zz, jz).wait_send()
 
     def hsent(k, _):
         hcopy(k).wait_send()
+        vcopy(k).wait_send()
         return 0
 
     lax.fori_loop(1, 32, hsent, 0)
@@ -796,22 +809,29 @@
     keep.wait()
 
 
-def reduce(p, grads, h):
-    blocks, rows, width = p.shape
+def attend_back(xg, w, gain, o32, do, qa, ka, va, sums, grads):
+    blocks, rows, width = xg.shape
     g = grads.shape[1:]
-    per = h.shape[1] // 2
+    per = width // 32
     dma = pltpu.SemaphoreType.DMA
+    turned = pltpu.VMEM((blocks, LANES, rows), BF)
+    total = pltpu.VMEM((blocks, LANES, rows), F32)
     return pl.pallas_call(
-        reduce_kernel,
+        attend_back_kernel,
         out_shape=(
             jax.ShapeDtypeStruct((2, rows, width), BF),
             jax.ShapeDtypeStruct(g, F32),
             jax.ShapeDtypeStruct((3, per, width), F32),
-            jax.ShapeDtypeStruct((per, 3 * LANES), F32),
+            jax.ShapeDtypeStruct(sums.shape, F32),
         ),
-        in_specs=[ANY, ANY, ANY],
+        in_specs=[INVM] * 9 + [ANY],
         out_specs=(ANY, INVM, INVM, INVM),
         scratch_shapes=[
+            pltpu.VMEM((2, blocks, rows, LANES), BF), turned, turned, turned, total, total, total,
+            pltpu.VMEM((3 * LANES, width), F32),
+            pltpu.VMEM((blocks, rows, width), BF),
+            pltpu.VMEM((32, per, 3 * LANES), BF),
+            pltpu.VMEM(sums.shape, F32),
             pltpu.VMEM((16,) + g, BF),
             pltpu.VMEM((16,) + g, BF),
             pltpu.VMEM((16,) + g, BF),
@@ -819,17 +839,19 @@
             pltpu.VMEM((4,) + g, BF),
             pltpu.VMEM((4, rows, width), BF),
             pltpu.VMEM((4, rows, width), BF),
-            pltpu.VMEM((4, rows, width), BF),
-            pltpu.VMEM((32,) + h.shape[1:], BF),
+            pltpu.VMEM((32, per, 3 * LANES), BF),
+            pltpu.VMEM((32,) + sums.shape, F32),
             pltpu.VMEM((rows, width), BF),
-            dma((4,)), dma((16,)), dma((2,)),
+            dma((16,)), dma((3,)),
             dma((16,)), dma((16,)), dma((16,)), dma((16,)), dma((4,)), dma((4,)), dma((4,)), dma((4,)),
-            dma((4,)), dma((4,)), dma((4,)), dma((4,)), dma((2,)), dma((1,)), dma((32,)), dma((32,)),
+            dma((4,)), dma((4,)), dma((4,)), dma((4,)), dma((2,)), dma((1,)),
+            dma((32,)), dma((32,)), dma((32,)), dma((32,)),
         ],
         compiler_params=pltpu.CompilerParams(
             collective_id=3, has_side_effects=True, vmem_limit_bytes=VMEM_LIMIT
         ),
-    )(p, grads, h)
+        name="attend_back",
+    )(xg, w, gain, o32, do, qa, ka, va, sums, grads)
 
 
 def by_heads(
@@ -861,16 +883,13 @@
     att = swap(o, 1)
     out, datt, dh, dna, grads, sums = tokens(x, cot, att, wg, vecs)
     do = swap(datt, 2)
-    dn, dw, dgain = attend_back(doc, xg, w, gain, o32, do, qa, ka, va)
-    sums = jnp.concatenate([sums[0:1] + dgain, sums[1:4]]).reshape(4, 32, per).transpose(1, 0, 2)
-    sums = jnp.pad(sums, ((0, 0), (0, per - 4), (0, 3 * LANES - per)))
-    h = jnp.concatenate([dw.reshape(32, per, 3 * LANES), sums], axis=1).astype(BF)
-    dn, gf, gq, gv = reduce(dn, grads, h)
+    dn, gf, gq, gv = attend_back(xg, w, gain, o32, do, qa, ka, va, sums, grads)
     x32 = x.astype(F32)
     r1 = lax.rsqrt(jnp.mean(x32 * x32, -1, keepdims=True) + EPS)
     n1 = x32 * r1
     g1 = (dna + dn.astype(F32)) * gain.astype(F32)
     grad = dh + r1 * (g1 - n1 * jnp.mean(g1 * n1, -1, keepdims=True))
+    gv = lax.dynamic_slice(gv, (0, (lax.axis_index("dp") * 8 + j) * per), (4, per))
     return (
         out[:, None],
         grad[:, None],
@@ -878,7 +897,7 @@
         gf[:per], gf[per : 2 * per], gf[2 * per : 3 * per],
         gf[3 * per : (3 + ff) * per].reshape(ff, per, width).transpose(1, 0, 2).reshape(per, ff * width),
         gf[(3 + ff) * per :],
-        gv[0, :per], gv[1, :per], gv[2, :per], gv[3, :per],
+        gv[0], gv[1], gv[2], gv[3],
     )
 
 

time: 401 us -> 346 us (0.86)
  Pallas kernels: 362 us -> 314 us
    pallas_call x2 -> x1, Pallas kernels: 153 us -> 122 us  [attend_back(): pl.pallas_call(attend_back_kernel, out_shape=(jax.ShapeDtypeStruct((2, ro...]
    pallas_call x1, Pallas kernels: 59.8 us -> 43.1 us  [attend(): pl.pallas_call(attend_kernel, out_shape=(jax.ShapeDtypeStruct((blocks, ro...]
where the time goes in v2:
time: 346 us; the launch traced here: 345 us
  Pallas kernels  314 us (91%)
  local copies, waits for them, and re-layouts  19.5 us (6%)
  other arithmetic  10.8 us (3%)
    pallas_call x1, Pallas kernels, attend_back(): pl.pallas_call(attend_back_kernel, out_shape=(jax.ShapeDtypeStruct((2, ro...  122 us
    pallas_call x1, Pallas kernels, gather(): pl.pallas_call(gather_kernel, out_shape=(jax.ShapeDtypeStruct((8, rows, w...  70.8 us
    pallas_call x2, Pallas kernels, swap(): pl.pallas_call(swap_kernel, out_shape=jax.ShapeDtypeStruct(a.shape, a.dty...  46.6 us
    pallas_call x1, Pallas kernels, attend(): pl.pallas_call(attend_kernel, out_shape=(jax.ShapeDtypeStruct((blocks, ro...  43.1 us
    pallas_call x1, Pallas kernels, tokens(): pl.pallas_call(token_kernel, grid=(micro,), out_shape=(jax.ShapeDtypeStru...  32 us
    unnamed x22, local copies, waits for them, and re-layouts  9.93 us

profile of v2, /device:TPU:0, one launch (start us, length us, event | category | flops | bytes accessed | tf_op | source)
XLA Modules:
  0.0 345.5 jit_solution(16653817351316598112)
XLA Ops:
  0.7 1.3 constant_dynamic-slice_fusion.2
  1.9 1.9 pad_add_fusion.doc
  3.8 1.5 fusion.7
  5.3 0.7 constant_dynamic-update-slice_fusion.11
  6.1 0.7 constant_dynamic-update-slice_fusion.10
  6.8 0.7 constant_dynamic-update-slice_fusion.9
  7.5 0.7 constant_dynamic-update-slice_fusion.8
  8.2 0.7 constant_dynamic-update-slice_fusion.7
  8.9 0.7 constant_dynamic-update-slice_fusion.6
  9.7 0.7 constant_dynamic-update-slice_fusion.5
  10.4 0.7 constant_dynamic-update-slice_fusion.4
  11.1 0.7 constant_dynamic-update-slice_fusion.3
  11.8 0.7 constant_dynamic-update-slice_fusion.2
  12.5 0.8 constant_dynamic-update-slice_fusion.1
  13.4 0.7 constant_dynamic-update-slice_fusion.s_ref
  14.1 0.0 copy-start.4
  14.1 0.7 copy-done.4
  14.8 70.8 %shard_map.263 = (bf16[8,512,512]{2,1,0:T(8,128)(2,1)}, bf16[32,240,512]{2,1,0:T(8,128)(2,1)}) custom-call(bf16[2,512,512]{2,1,0:T(8,128)(2,1)} %bitcast.47, bf16[240,512]{1,0:T(8,128)(2,1)} %copy-done.4), custom_call_target="tpu_custom_call" | custom-call | tf_op jit(solution)/shard_map/pallas_call | solution.py:208
  85.6 0.9 slice_bitcast_fusion.3
  86.5 0.1 slice_reduce_fusion
  86.5 0.7 slice.63.gain_ref
  87.3 0.1 reshape.71
  87.4 0.7 reshape.68.vec
  88.1 1.0 constant_dynamic-slice_fusion.1
  89.1 0.3 copy.34
  89.4 0.8 copy.42
  90.2 43.1 %attend.1 = (bf16[8,512,128]{2,1,0:T(8,128)(2,1)}, f32[8,512,128]{2,1,0:T(8,128)}, bf16[2,8,512,128]{3,2,1,0:T(8,128)(2,1)}, bf16[2,8,512,128]{3,2,1,0:T(8,128)(2,1)}, bf16[2,8,512,128]{3,2,1,0:T(8,128)(2,1)}) custom-call(s32[2]{0:T(128)} %pad_add_fusion.doc, bf16[8,512,512]{2,1,0:T(8,128)(2,1)} %get-tuple-element.31.x_ref, bf16[512,384]{1,0:T(8,128)(2,1)} %bitcast.49, ...), custom_call_target="tpu_custom_call" | custom-call | tf_op jit(solution)/shard_map/attend/pallas_call | solution.py:374
  133.3 20.3 %shard_map.264.a_ref = bf16[8,512,128]{2,1,0:T(8,128)(2,1)} custom-call(bf16[8,512,128]{2,1,0:T(8,128)(2,1)} %get-tuple-element.33.a_ref), custom_call_target="tpu_custom_call" | custom-call | tf_op jit(solution)/shard_map/pallas_call | solution.py:250
  153.6 32.0 %shard_map.265 = (bf16[2,512,512]{2,1,0:T(8,128)(2,1)}, bf16[8,512,128]{2,1,0:T(8,128)(2,1)}, f32[2,512,512]{2,1,0:T(8,128)}, f32[2,512,512]{2,1,0:T(8,128)}, bf...) custom-call(bf16[2,512,512]{2,1,0:T(8,128)(2,1)} %bitcast.48, bf16[2,512,512]{2,1,0:T(8,128)(2,1)} %bitcast.53, ...), custom_call_target="tpu_custom_call" | custom-call | tf_op jit(solution)/shard_map/pallas_call | solution.py:487
  185.6 26.3 %shard_map.266.do_ref = bf16[8,512,128]{2,1,0:T(8,128)(2,1)} custom-call(bf16[8,512,128]{2,1,0:T(8,128)(2,1)} %get-tuple-element.38.a_ref), custom_call_target="tpu_custom_call" | custom-call | tf_op jit(solution)/shard_map/pallas_call | solution.py:250
  212.0 121.8 %attend_back.1 = (bf16[2,512,512]{2,1,0:T(8,128)(2,1)}, f32[176,512]{1,0:T(8,128)}, f32[3,16,512]{2,1,0:T(8,128)}, f32[8,512]{1,0:T(8,128)}) custom-call(bf16[8,512,512]{2,1,0:T(8,128)(2,1)} %get-tuple-element.31.x_ref, bf16[512,384]{1,0:T(8,128)(2,1)} %bitcast.50, bf16[1,512]{1,0:T(2,128)(2,1)} %slice.63.gain_ref, ...), custom_call_target="tpu_custom_call" | custom-call | tf_op jit(solution)/shard_map/attend_back/pallas_call | solution.py:819
  333.8 1.4 slice_bitcast_fusion
  335.2 0.8 constant_dynamic-slice_fusion
  335.9 0.5 slice_bitcast_fusion.4
  336.5 0.0 copy-start
  336.5 0.0 copy-start.1
  336.5 0.0 copy-start.2
  336.5 3.0 fusion.2
  339.5 0.0 copy-done
  339.5 0.1 copy-done.1
  339.6 0.3 copy-done.2
  339.9 0.0 copy-start.3
  339.9 3.6 %fusion.6 = f32[2,1,512,512]{3,2,1,0:T(8,128)} fusion(f32[2,512,512]{2,1,0:T(8,128)} %get-tuple-element.35, f32[2,512,512]{2,1,0:T(8,128)S(1)} %copy-done.1, bf16[2,512,512]{2,1,0:T(8,128)(2,1)S(1)} %copy-done.2, f32[2,512]{1,0:T(2,128)S(1)} %broadcast_multiply_fusion, f32[512]{0:T(512)S(1)} %reshape.71, f32[2,512]{1,0:T(2,128)S(1)} %add_rsqrt_fusion, ...), kind=kLoop, calls=%fused_computation.8 | loop fusion | flops 4718592 | bytes 8398848
  343.5 0.0 copy-done.3
  343.5 0.6 fusion.21
  344.1 0.7 fusion.20
  344.8 0.7 copy.39
  (4 shorter events, 0.1 us)
Async XLA Ops:
  14.1 0.7 copy-start.4
  336.5 3.0 copy-start
  336.5 3.2 copy-start.1
  336.5 3.4 copy-start.2
  339.9 3.6 %copy-start.3 = (f32[176,512]{1,0:T(8,128)S(1)}, f32[176,512]{1,0:T(8,128)}, u32[]{:S(2)}) copy-start(f32[176,512]{1,0:T(8,128)} %get-tuple-element.46) | copy-start | bytes 1081348

commit v3 on v2

--- a/solution.py
+++ b/solution.py
@@ -66,164 +66,430 @@
 CK = 4
 
 
-def gather_kernel(x_ref, s_ref, xg_ref, wg_ref, xv, sv, lsem, wsend, wrecv, xsend, xrecv):
+class Spread:
+    def __init__(self, dst, send, recv):
+        self.dst, self.send, self.recv = dst, send, recv
+        self.at = place()
+        self.count = 0
+        self.sent = []
+        d, j, z, c, dx, dy, dxy = self.at
+        self.pj = j + 1 - 2 * c
+        self.lines = (z, z + 1 - 2 * (z % 2), (z + 2) % 4, 3 - z)
+        self.slots = {
+            dp: [where * 8 + 2 * zz + c for zz in self.lines]
+            for dp, where in (("d", d), ("x", dx), ("y", dy), ("xy", dxy))
+        }
+
+    def make(self, slot, i, dp, seq, src=None):
+        return remote(
+            self.dst.at[slot] if src is None else src, self.dst.at[slot],
+            self.send.at[i], self.recv.at[slot], dp, seq,
+        )
+
+    def put(self, slot, dp, seq, src=None):
+        i = self.count
+        self.count += 1
+        self.make(slot, i, dp, seq, src).start()
+        self.sent.append((slot, i))
+
+    def arrive(self, slot):
+        self.make(slot, 0, self.at[0], self.pj).wait_recv()
+
+    def in_plane(self, src):
+        d, j, z, c, dx, dy, dxy = self.at
+        for dp, seq in ((dx, j), (dy, j), (d, self.pj)):
+            self.put(self.slots["d"][0], dp, seq, src)
+
+    def along(self, srcs):
+        d, j, z, c, dx, dy, dxy = self.at
+        for zz, src in zip(self.lines[1:], srcs):
+            self.put(self.slots["d"][0], d, 2 * zz + c, src)
+
+    def from_line(self, k):
+        d, j, z, c, dx, dy, dxy = self.at
+        slot = self.slots["d"][k]
+        self.arrive(slot)
+        for dp, seq in ((dx, j), (dy, j), (d, self.pj)):
+            self.put(slot, dp, seq)
+
+    def from_plane(self, k):
+        d, j, z, c, dx, dy, dxy = self.at
+        sx, sy = self.slots["x"][k], self.slots["y"][k]
+        for slot in (sx, sy):
+            self.arrive(slot)
+            self.put(slot, d, self.pj)
+        even = self.lines[k] % 2 == 0
+        i = self.count
+        self.count += 1
+        self.sent.append((sx, i))
+
+        @pl.when(even)
+        def _():
+            self.make(sx, i, dy, j).start()
+
+        @pl.when(jnp.logical_not(even))
+        def _():
+            self.make(sy, i, dx, j).start()
+
+    def from_corner(self):
+        for slot in self.slots["xy"]:
+            self.arrive(slot)
+            self.put(slot, self.at[0], self.pj)
+
+    def from_core(self):
+        c = self.at[3]
+        for slots in self.slots.values():
+            for slot in slots:
+                self.arrive(slot + 1 - 2 * c)
+
+    def wait_sent(self):
+        for slot, i in self.sent:
+            self.make(slot, i, self.at[0], self.pj).wait_send()
+
+
+LOG2E = 1.4426950408889634
+
+
+def lane_of(rows):
+    return lax.broadcasted_iota(jnp.int32, (rows, LANES), 1)
+
+
+def three(v):
+    a = v.astype(BF).astype(F32)
+    b = (v - a).astype(BF).astype(F32)
+    return a, b, v - a - b
+
+
+def beside(h, lane, values, parts):
+    first = SIDE * (1 - h)
+    own = (lane < SIDE) if h == 0 else (lane >= SIDE)
+    out = jnp.where(own, values, 0.0)
+    for k, part in enumerate(parts):
+        if part is not None:
+            out = jnp.where(lane == first + k, part, out)
+    return out.astype(BF)
+
+
+def upper(rows):
+    return lax.broadcasted_iota(jnp.int32, (rows, rows), 0) <= lax.broadcasted_iota(
+        jnp.int32, (rows, rows), 1
+    )
+
+
+def front_kernel(
+    doc_len, doc_off, x_ref, wq, wk, wv, wo, wga, wgf, win, wback, small_ref,
+    xg, wg, w_ref, vec_ref, att, o32_ref, qa, ka, va,
+    hv, hg, sv, vt, top, acc, ov,
+    lsem, xsem, hsend, hrecv, wsend, wrecv, xsend, xrecv, ssend, srecv,
+):
+    blocks, rows, width = xg.shape
+    per = wq.shape[0]
+    half = width // 2
     d, j, z, c, dx, dy, dxy = place()
+    me = d * 8 + j
     g = z // 2
     pj = j + 1 - 2 * c
     za, zb, zc = z + 1 - 2 * (z % 2), (z + 2) % 4, 3 - z
+    ja = 2 * za + c
     near = jnp.logical_or(z == 1, z == 2)
     far = jnp.logical_or(z == 0, z == 3)
-    ja, jb, jc = 2 * za + c, 2 * zb + c, 2 * zc + c
-    lx = pltpu.make_async_copy(x_ref.at[g], xv, lsem.at[0])
-    ls = pltpu.make_async_copy(s_ref, sv, lsem.at[1])
-    lx.start()
-    ls.start()
-    greet([(d, ja), (d, jb), (d, jc), (dx, j), (dy, j), (d, pj)])
-    rows = xv.shape[0] // CK
-    count = [0]
-    waits = []
-
-    def wcopy(slot, dp, seq, own=False):
-        i = count[0]
-        count[0] += 1
-        copy = remote(
-            s_ref if own else wg_ref.at[slot], wg_ref.at[slot], wsend.at[i], wrecv.at[slot], dp, seq
-        )
-        copy.start()
-        waits.append(copy)
-
-    def warrive(slot):
-        remote(s_ref, wg_ref.at[slot], wsend.at[0], wrecv.at[slot], d, pj).wait_recv()
+    loads = []
+    pieces = [(m, hv.at[k * per : (k + 1) * per]) for k, m in enumerate((wq, wk, wv))]
+    pieces += [(m, sv.at[k * per : (k + 1) * per]) for k, m in enumerate((wo, wga, wgf))]
+    ff = win.shape[1] // width
+    for k in range(ff):
+        pieces.append((win.at[:, k * width : (k + 1) * width], sv.at[(3 + k) * per : (4 + k) * per]))
+    pieces.append((wback, sv.at[(3 + ff) * per :]))
+    for k, (src, dst) in enumerate(pieces):
+        loads.append(pltpu.make_async_copy(src, dst, lsem.at[k]))
+        loads[-1].start()
+    own = pltpu.make_async_copy(x_ref.at[g], xg.at[j], xsem)
+    own.start()
+    lanes = lax.broadcasted_iota(jnp.int32, (LANES, half), 1)
+    subs = lax.broadcasted_iota(jnp.int32, (LANES, half), 0)
+    spots = [
+        nn(small_ref[...], jnp.where(lanes + k * half == me * per + subs, 1.0, 0.0).astype(BF)) for k in range(2)
+    ]
+    row = lax.broadcasted_iota(jnp.int32, (16, half), 0)
+    tile = jnp.where(row < 4, spots[0], spots[1]).astype(BF)
+    hv[3 * per :, :half] = tile
+    hv[3 * per :, half:] = tile
+    for k in range(3):
+        loads[k].wait()
+    greet([(d, (j + k) % 8) for k in range(1, 8)] + [(dx, j), (dy, j)])
+
+    heads = Spread(hg, hsend, hrecv)
+    weights = Spread(wg, wsend, wrecv)
+
+    def side(zz):
+        return hv.at[:, pl.ds(pl.multiple_of(half * (zz % 2), half), half)]
+
+    heads.along([side(zz) for zz in (za, zb, zc)])
+    heads.in_plane(side(z))
 
     def xcopy(k, part, block, dp, seq, src=None):
-        piece = pl.ds(part * rows, rows)
-        source = xg_ref.at[block, piece] if src is None else x_ref.at[src, piece]
-        return remote(
-            source, xg_ref.at[block, piece], xsend.at[k, part], xrecv.at[block, part], dp, seq
-        )
-
-    def xarrive(part, block):
-        xcopy(0, part, block, d, pj).wait_recv()
-
-    me = d * 8 + j
-    for dp, seq in [(d, ja), (d, jb), (d, jc), (dx, j), (dy, j), (d, pj)]:
-        wcopy(me, dp, seq, True)
-    xwaits = []
+        piece = pl.ds(part * (rows // CK), rows // CK)
+        source = xg.at[block, piece] if src is None else x_ref.at[src, piece]
+        return remote(source, xg.at[block, piece], xsend.at[k, part], xrecv.at[block, part], dp, seq)
+
+    def xarrive(block):
+        for part in range(CK):
+            xcopy(0, part, block, d, pj).wait_recv()
+
     jn = 2 * (2 - g) + c
     for part in range(CK):
-        for k, (src, seq) in enumerate([(1 - g, jn), (g, ja), (g, pj)]):
-            copy = xcopy(k, part, j, d, seq, src)
-            copy.start()
-            xwaits.append(copy)
-    lx.wait()
-    ls.wait()
-    ox = pltpu.make_async_copy(xv, xg_ref.at[j], lsem.at[0])
-    ow = pltpu.make_async_copy(sv, wg_ref.at[me], lsem.at[1])
-    ox.start()
-    ow.start()
-
-    def zarr(jz):
-        slot = d * 8 + jz
-        warrive(slot)
-        wcopy(slot, dx, j)
-        wcopy(slot, dy, j)
-        wcopy(slot, d, pj)
-
-    def xyarr(zz):
-        jz = 2 * zz + c
-        sx, sy = dx * 8 + jz, dy * 8 + jz
-        even = zz % 2 == 0
-        warrive(sx)
-        wcopy(sx, d, pj)
-        warrive(sy)
-        wcopy(sy, d, pj)
-        i = count[0]
-        count[0] += 1
-
-        def on(slot, dp):
-            return remote(wg_ref.at[slot], wg_ref.at[slot], wsend.at[i], wrecv.at[slot], dp, j)
-
-        @pl.when(even)
+        xcopy(0, part, j, d, ja, g).start()
+        xcopy(1, part, j, d, pj, g).start()
+    for part in range(CK):
+        xcopy(2, part, j, d, jn, 1 - g).start()
+    hg[me] = jnp.where(z % 2 == 0, hv[:, :half], hv[:, half:])
+    for copy in loads[3:]:
+        copy.wait()
+    keep = pltpu.make_async_copy(sv, wg.at[me], lsem.at[0])
+    keep.start()
+    weights.in_plane(sv)
+
+    heads.from_line(1)
+    heads.from_plane(0)
+    heads.from_line(2)
+    heads.from_plane(1)
+    heads.from_line(3)
+    heads.from_plane(2)
+    heads.from_plane(3)
+    heads.from_corner()
+    heads.from_core()
+
+    vecs = jnp.zeros((16, half), F32)
+    for k in range(32):
+        vecs += hg[k, 3 * per :].astype(F32)
+    for k in range(2):
+        vec_ref[:, k * half : (k + 1) * half] = vecs[4 * k : 4 * k + 4]
+    for k in range(3):
+        both = hg[:, k * per : (k + 1) * per, :]
+        picked = jnp.where(c == 0, both[:, :, :LANES], both[:, :, LANES:])
+        w_ref[:, k * LANES : (k + 1) * LANES] = picked.reshape(width, LANES)
+
+    off = doc_off[g, 0, 0]
+    end = off + doc_len[g, 0, 0]
+    lane = lane_of(rows)
+    up = lax.broadcasted_iota(jnp.int32, (rows, 1), 0)
+    along = lax.broadcasted_iota(jnp.int32, (1, rows), 1)
+    tall = lax.broadcasted_iota(jnp.int32, (16, rows), 0)
+    ones = jnp.where(tall == 0, 1.0, 0.0).astype(BF)
+
+    def project(b):
+        x = xg[b].astype(F32)
+        n = (x * lax.rsqrt(jnp.mean(x * x, -1, keepdims=True) + EPS) * vec_ref[0:1]).astype(BF)
+        p = nn(n, w_ref[...])
+        pos = b * rows + up
+        bad = jnp.where(jnp.logical_and(pos >= off, pos < end), 0.0, NEG)
+        q = p[:, :LANES] * (HEAD_DIM ** (-0.5) * LOG2E)
+        k = p[:, LANES : 2 * LANES]
+        v = p[:, 2 * LANES :]
+        for h in range(2):
+            qa[h, b] = beside(h, lane, q, (1.0,))
+            ka[h, b] = beside(h, lane, k, (bad, 1.0, 1.0, 1.0))
+            va[h, b] = beside(h, lane, v, (None, 1.0, 1.0, 1.0))
+        turned = v.astype(BF).T
+        for h in range(2):
+            vt[h, b, :SIDE] = turned[h * SIDE : (h + 1) * SIDE]
+            vt[h, b, SIDE:] = ones
+
+    def project_two(base):
+        def body(k, _):
+            project(base + k)
+            return 0
+
+        lax.fori_loop(0, 2, body, 0)
+
+    z1 = 2 - g
+    z2 = 3 * (1 - g)
+    b1, b2 = 2 * z1 + c, 2 * z2 + c
+    own.wait()
+    xarrive(pj)
+    project_two(2 * z)
+    for part in range(CK):
+        xcopy(0, part, ja, d, pj).wait_recv()
+        xcopy(3, part, ja, d, pj).start()
+
+        @pl.when(near)
         def _():
-            on(sx, dy).start()
-
-        @pl.when(jnp.logical_not(even))
+            xcopy(0, part, b1, d, pj).wait_recv()
+            xcopy(6, part, b1, d, ja).start()
+            xcopy(4, part, b1, d, pj).start()
+
+    xarrive(ja + 1 - 2 * c)
+    project_two(2 * za)
+
+    keep_low = upper(rows)
+    sub = lax.broadcasted_iota(jnp.int32, (SIDE, rows), 0)
+
+    def scores(q, k):
+        return [nt(ka[h, k], qa[h, q]) for h in range(2)]
+
+    def first(q):
+        ss = [jnp.where(keep_low, s, NEG) for s in scores(q, q)]
+        new = [jnp.max(s, 0, keepdims=True) for s in ss]
+        ps = [jnp.exp2(s - n).astype(BF) for s, n in zip(ss, new)]
+        for h in range(2):
+            top[h, q] = new[h]
+            acc[h, q] = nn(vt[h, q], ps[h])
+
+    def pair(q, k):
+        ss = scores(q, k)
+        old = [top[h, q] for h in range(2)]
+        new = [jnp.maximum(old[h], jnp.max(ss[h], 0, keepdims=True)) for h in range(2)]
+        ps = [jnp.exp2(ss[h] - new[h]).astype(BF) for h in range(2)]
+        for h in range(2):
+            top[h, q] = new[h]
+            acc[h, q] = acc[h, q] * jnp.exp2(old[h] - new[h]) + nn(vt[h, k], ps[h])
+
+    def acopy(q):
+        return remote(ov.at[q], att.at[j], ssend.at[q], srecv.at[j], d, q)
+
+    def finish(b):
+        pos = b * rows + along
+        live = jnp.logical_and(pos >= off, pos < end)
+        outs = []
+        for h in range(2):
+            total = acc[h, b, SIDE : SIDE + 1]
+            lse = jnp.where(live, top[h, b] + jnp.log2(total), -NEG)
+            mine = jnp.where(live, acc[h, b, :SIDE] / total, 0.0)
+            parts = three(lse)
+            beyond = jnp.zeros((SIDE, rows), F32)
+            for k in range(3):
+                beyond = jnp.where(sub == k + 1, -parts[k], beyond)
+            both = (mine, beyond) if h == 0 else (beyond, mine)
+            out = jnp.concatenate(both, axis=0).T
+            start = SIDE * (1 - h)
+            aug = jnp.logical_and(lane > start, lane < start + 4)
+            qa[h, b] = jnp.where(aug, out, qa[h, b].astype(F32)).astype(BF)
+            outs.append(out)
+        out = jnp.where(lane < SIDE, outs[0], outs[1])
+        o32_ref[b] = out
+        ov[b] = out.astype(BF)
+
+        @pl.when(b != j)
         def _():
-            on(sy, dx).start()
-
-        waits.append(on(sx, dy))
-
-    zarr(ja)
-    xyarr(z)
-    zarr(jb)
-    xyarr(za)
-    zarr(jc)
-    xyarr(zb)
-    xyarr(zc)
-    b1 = 2 * (2 - g) + c
-    b2 = 2 * (3 * (1 - g)) + c
-    for k, block in ((3, b1), (5, b2)):
-        for part in range(CK):
-            xarrive(part, block)
-            copy = xcopy(k, part, block, d, pj)
-            copy.start()
-            xwaits.append(copy)
-
+            acopy(b).start()
+
+    def outer(i, _):
+        @pl.when(i == 4)
+        def _():
             @pl.when(near)
             def _():
-                xcopy(k + 1, part, block, d, ja).start()
-
-    for part in range(CK):
-        xarrive(part, ja)
-        copy = xcopy(7, part, ja, d, pj)
-        copy.start()
-        xwaits.append(copy)
-    for zz in (z, za, zb, zc):
-        slot = dxy * 8 + 2 * zz + c
-        warrive(slot)
-        wcopy(slot, d, pj)
-    for dp in (d, dx, dy, dxy):
-        for zz in (z, za, zb, zc):
-            warrive(dp * 8 + 2 * zz + 1 - c)
-    for block in (j, ja, b1, b2):
+                for part in range(CK):
+                    xcopy(0, part, b2, d, pj).wait_recv()
+                    xcopy(7, part, b2, d, ja).start()
+                    xcopy(5, part, b2, d, pj).start()
+
+            @pl.when(far)
+            def _():
+                for part in range(CK):
+                    xcopy(0, part, b1, d, pj).wait_recv()
+                    xcopy(4, part, b1, d, pj).start()
+
+            weights.along([sv] * 3)
+            weights.from_plane(0)
+            xarrive(b1 + 1 - 2 * c)
+
+        @pl.when(i == 6)
+        def _():
+            @pl.when(far)
+            def _():
+                for part in range(CK):
+                    xcopy(0, part, b2, d, pj).wait_recv()
+                    xcopy(5, part, b2, d, pj).start()
+
+            xarrive(b2 + 1 - 2 * c)
+
+        @pl.when(jnp.logical_or(i == 4, i == 6))
+        def _():
+            project_two(2 * (z1 + (z2 - z1) * ((i - 4) // 2)))
+
+        o = (1 - g) * i + g * (blocks - 1 - i)
+        first(o)
+        last = jnp.logical_and(g == 1, i == blocks - 1)
+        pl.when(last)(lambda: finish(o))
+
+        def inner(t, _):
+            q = (1 - g) * o + g * (o + 1 + t)
+            pair(q, (1 - g) * (o - 1 - t) + g * o)
+            pl.when(jnp.logical_or(last, jnp.logical_and(g == 0, t == i - 1)))(lambda: finish(q))
+
+            @pl.when(jnp.logical_and(i == blocks - 1, t == 3))
+            def _():
+                for k in range(1, 4):
+                    weights.from_line(k)
+
+            return 0
+
+        lax.fori_loop(0, i, inner, 0)
+        pl.when(jnp.logical_and(g == 0, i == 0))(lambda: finish(o))
+        return 0
+
+    lax.fori_loop(0, blocks, outer, 0)
+    att[j] = ov[j]
+    for k in range(1, 4):
+        weights.from_plane(k)
+    weights.from_corner()
+    weights.from_core()
+    for k in range(1, 8):
+        q = (j + k) % 8
+        remote(ov.at[q], att.at[q], ssend.at[q], srecv.at[q], d, q).wait_recv()
+    heads.wait_sent()
+    weights.wait_sent()
+    for k in range(6):
         for part in range(CK):
-            xarrive(part, block + 1 - 2 * c)
-    for copy in waits:
-        copy.wait_send()
-    for copy in xwaits:
-        copy.wait_send()
+            xcopy(k, part, j, d, pj).wait_send()
 
     @pl.when(near)
     def _():
-        for k, block in ((4, b1), (6, b2)):
+        for k in (6, 7):
             for part in range(CK):
-                xcopy(k, part, block, d, ja).wait_send()
-
-    ox.wait()
-    ow.wait()
-
-
-def gather(x, shard):
+                xcopy(k, part, j, d, pj).wait_send()
+
+    for k in range(1, 8):
+        acopy((j + k) % 8).wait_send()
+    keep.wait()
+
+
+def front(doc_len, doc_off, x, mats, small):
     _, rows, width = x.shape
+    per = mats[0].shape[0]
+    blocks = 8
+    tall = sum(m.shape[0] * (m.shape[1] // width) for m in mats[3:])
+    side = jax.ShapeDtypeStruct((2, blocks, rows, LANES), BF)
+    dma = pltpu.SemaphoreType.DMA
     return pl.pallas_call(
-        gather_kernel,
+        front_kernel,
         out_shape=(
-            jax.ShapeDtypeStruct((8, rows, width), BF),
-            jax.ShapeDtypeStruct((32,) + shard.shape, BF),
+            jax.ShapeDtypeStruct((blocks, rows, width), BF),
+            jax.ShapeDtypeStruct((32, tall, width), BF),
+            jax.ShapeDtypeStruct((width, 3 * LANES), BF),
+            jax.ShapeDtypeStruct((4, width), F32),
+            jax.ShapeDtypeStruct((blocks, rows, LANES), BF),
+            jax.ShapeDtypeStruct((blocks, rows, LANES), F32),
+            side, side, side,
         ),
-        in_specs=[ANY, ANY],
-        out_specs=(ANY, ANY),
+        in_specs=[INSM, INSM] + [ANY] * 9 + [INVM],
+        out_specs=(INVM, ANY) + (INVM,) * 7,
         scratch_shapes=[
-            pltpu.VMEM((rows, width), BF),
-            pltpu.VMEM(shard.shape, BF),
-            pltpu.SemaphoreType.DMA((2,)),
-            pltpu.SemaphoreType.DMA((32,)),
-            pltpu.SemaphoreType.DMA((32,)),
-            pltpu.SemaphoreType.DMA((8, CK)),
-            pltpu.SemaphoreType.DMA((8, CK)),
+            pltpu.VMEM((3 * per + 16, width), BF),
+            pltpu.VMEM((32, 3 * per + 16, width // 2), BF),
+            pltpu.VMEM((tall, width), BF),
+            pltpu.VMEM((2, blocks, SIDE + 16, rows), BF),
+            pltpu.VMEM((2, blocks, 1, rows), F32),
+            pltpu.VMEM((2, blocks, SIDE + 16, rows), F32),
+            pltpu.VMEM((blocks, rows, LANES), BF),
+            dma((12,)), dma, dma((32,)), dma((32,)), dma((32,)), dma((32,)),
+            dma((8, CK)), dma((8, CK)), dma((8,)), dma((8,)),
         ],
-        compiler_params=pltpu.CompilerParams(collective_id=0, has_side_effects=True),
-    )(x, shard)
+        compiler_params=pltpu.CompilerParams(
+            collective_id=0, has_side_effects=True, vmem_limit_bytes=VMEM_LIMIT
+        ),
+        name="front",
+    )(doc_len, doc_off, x, *mats, small)
 
 
 def swap_kernel(a_ref, b_ref, av, lsem, send, recv):
@@ -262,130 +528,6 @@
     )(a)
 
 
-LOG2E = 1.4426950408889634
-
-
-def lane_of(rows):
-    return lax.broadcasted_iota(jnp.int32, (rows, LANES), 1)
-
-
-def three(v):
-    a = v.astype(BF).astype(F32)
-    b = (v - a).astype(BF).astype(F32)
-    return a, b, v - a - b
-
-
-def beside(h, lane, values, parts):
-    first = SIDE * (1 - h)
-    own = (lane < SIDE) if h == 0 else (lane >= SIDE)
-    out = jnp.where(own, values, 0.0)
-    for k, part in enumerate(parts):
-        if part is not None:
-            out = jnp.where(lane == first + k, part, out)
-    return out.astype(BF)
-
-
-def upper(rows):
-    return lax.broadcasted_iota(jnp.int32, (rows, rows), 0) <= lax.broadcasted_iota(
-        jnp.int32, (rows, rows), 1
-    )
-
-
-def attend_kernel(doc, x_ref, w_ref, gain_ref, o_ref, o32_ref, qa, ka, va, vt):
-    blocks, rows, width = x_ref.shape
-    off = doc[0]
-    end = off + doc[1]
-    lane = lane_of(rows)
-    up = lax.broadcasted_iota(jnp.int32, (rows, 1), 0)
-    along = lax.broadcasted_iota(jnp.int32, (1, rows), 1)
-    gain = gain_ref[...].astype(F32)
-    tall = lax.broadcasted_iota(jnp.int32, (16, rows), 0)
-    ones = jnp.where(tall == 0, 1.0, 0.0).astype(BF)
-
-    def project(b, _):
-        x = x_ref[b].astype(F32)
-        n = (x * lax.rsqrt(jnp.mean(x * x, -1, keepdims=True) + EPS) * gain).astype(BF)
-        p = nn(n, w_ref[...])
-        pos = b * rows + up
-        bad = jnp.where(jnp.logical_and(pos >= off, pos < end), 0.0, NEG)
-        q = p[:, :LANES] * (HEAD_DIM ** (-0.5) * LOG2E)
-        k = p[:, LANES : 2 * LANES]
-        v = p[:, 2 * LANES :]
-        for h in range(2):
-            qa[h, b] = beside(h, lane, q, (1.0,))
-            ka[h, b] = beside(h, lane, k, (bad, 1.0, 1.0, 1.0))
-            va[h, b] = beside(h, lane, v, (None, 1.0, 1.0, 1.0))
-        turned = v.astype(BF).T
-        for h in range(2):
-            vt[h, b, :SIDE] = turned[h * SIDE : (h + 1) * SIDE]
-            vt[h, b, SIDE:] = ones
-        return 0
-
-    lax.fori_loop(0, blocks, project, 0)
-    keep = upper(rows)
-    sub = lax.broadcasted_iota(jnp.int32, (LANES, rows), 0)
-
-    def one(b, _):
-        pos = b * rows + along
-        live = jnp.logical_and(pos >= off, pos < end)
-
-        def score(h, kb, masked):
-            s = nt(ka[h, kb], qa[h, b])
-            return jnp.where(keep, s, NEG) if masked else s
-
-        def step(kb, carry, masked=False):
-            ss = [score(h, kb, masked) for h in range(2)]
-            new = [jnp.maximum(carry[h][0], jnp.max(ss[h], 0, keepdims=True)) for h in range(2)]
-            ps = [jnp.exp2(ss[h] - new[h]).astype(BF) for h in range(2)]
-            return tuple(
-                (new[h], carry[h][1] * jnp.exp2(carry[h][0] - new[h]) + nn(vt[h, kb], ps[h])) for h in range(2)
-            )
-
-        start = ((jnp.full((1, rows), NEG, F32), jnp.zeros((SIDE + 16, rows), F32)),) * 2
-        done = step(b, lax.fori_loop(0, b, step, start), True)
-        m = [v[0] for v in done]
-        acc = [v[1] for v in done]
-        outs = []
-        for h in range(2):
-            total = acc[h][SIDE : SIDE + 1]
-            lse = jnp.where(live, m[h] + jnp.log2(total), -NEG)
-            own = jnp.where(live, acc[h][:SIDE] / total, 0.0)
-            parts = three(lse)
-            side = jnp.zeros((SIDE, rows), F32)
-            for k in range(3):
-                side = jnp.where(sub[:SIDE] == k + 1, -parts[k], side)
-            both = (own, side) if h == 0 else (side, own)
-            out = jnp.concatenate(both, axis=0).T
-            first = SIDE * (1 - h)
-            aug = jnp.logical_and(lane > first, lane < first + 4)
-            qa[h, b] = jnp.where(aug, out, qa[h, b].astype(F32)).astype(BF)
-            outs.append(out)
-        out = jnp.where(lane < SIDE, outs[0], outs[1])
-        o32_ref[b] = out
-        o_ref[b] = out.astype(BF)
-        return 0
-
-    lax.fori_loop(0, blocks, one, 0)
-
-
-def attend(doc, xg, w, gain):
-    blocks, rows, width = xg.shape
-    side = jax.ShapeDtypeStruct((2, blocks, rows, LANES), BF)
-    return pl.pallas_call(
-        attend_kernel,
-        out_shape=(
-            jax.ShapeDtypeStruct((blocks, rows, LANES), BF),
-            jax.ShapeDtypeStruct((blocks, rows, LANES), F32),
-            side, side, side,
-        ),
-        in_specs=[INSM, INVM, INVM, INVM],
-        out_specs=(INVM,) * 5,
-        scratch_shapes=[pltpu.VMEM((2, blocks, SIDE + 16, rows), BF)],
-        compiler_params=pltpu.CompilerParams(vmem_limit_bytes=VMEM_LIMIT),
-        name="attend",
-    )(doc, xg, w, gain)
-
-
 def token_kernel(
     x_ref, c_ref, a_ref, wg, vec, out_ref, da_ref, dh_ref, dn_ref, g_ref, v_ref,
     gp, act, g_out, g_ga, g_gf, g_in, g_back,
@@ -400,7 +542,7 @@
 
     def back(k):
         n = wg.shape[0] // ff
-        return wg[k * n : (k + 1) * n, 10 * per : 10 * per + ff * per, :].reshape(width, width)
+        return wg[k * n : (k + 1) * n, 7 * per : 7 * per + ff * per, :].reshape(width, width)
 
     @pl.when(step == 0)
     def _():
@@ -412,44 +554,44 @@
     shift_a, shift_f = vec[2:3].astype(F32), vec[3:4].astype(F32)
     n1 = x * lax.rsqrt(jnp.mean(x * x, -1, keepdims=True) + EPS)
     na = (n1 * gain_a).astype(BF)
-    ga = jax.nn.sigmoid(nn(na, weight(4 * per)) + shift_a)
+    ga = jax.nn.sigmoid(nn(na, weight(per)) + shift_a)
     att = jnp.concatenate([a_ref[i] for i in range(4)], axis=1)
-    br = nn(att, weight(3 * per))
+    br = nn(att, weight(0))
     hid = ga * br + (1.0 - ga) * x
     r2 = lax.rsqrt(jnp.mean(hid * hid, -1, keepdims=True) + EPS)
     n2 = hid * r2
     nf = (n2 * gain_f).astype(BF)
     bf = jnp.zeros((rows, width), F32)
     for k in range(ff):
-        pre = nn(nf, weight((6 + k) * per))
+        pre = nn(nf, weight((3 + k) * per))
         sq = pre * pre
         t = jnp.tanh(GELU_C * pre * (1.0 + GELU_A * sq))
         half = 0.5 * (1.0 + t)
         act[k] = (pre * half).astype(BF)
         gp[k] = half + 0.5 * pre * (1.0 - t * t) * (GELU_C * (1.0 + 3.0 * GELU_A * sq))
         bf += nn(act[k], back(k))
-    gf = jax.nn.sigmoid(nn(nf, weight(5 * per)) + shift_f)
+    gf = jax.nn.sigmoid(nn(nf, weight(2 * per)) + shift_f)
     out_ref[0] = (gf * bf + (1.0 - gf) * hid).astype(BF)
     c = c_ref[0].astype(F32)
     dlf = (c * (bf - hid) * gf * (1.0 - gf)).astype(BF)
     dbf = (c * gf).astype(BF)
-    dnf = nt(dlf, weight(5 * per))
+    dnf = nt(dlf, weight(2 * per))
     g_gf[...] += tn(nf, dlf)
     for k in range(ff):
         dpre = (nt(dbf, back(k)) * gp[k]).astype(BF)
         g_back[k] += tn(act[k], dbf)
         g_in[k] += tn(nf, dpre)
-        dnf += nt(dpre, weight((6 + k) * per))
+        dnf += nt(dpre, weight((3 + k) * per))
     g2 = dnf * gain_f
     dh = c * (1.0 - gf) + r2 * (g2 - n2 * jnp.mean(g2 * n2, -1, keepdims=True))
     dba = (dh * ga).astype(BF)
     dla = (dh * (br - x) * ga * (1.0 - ga)).astype(BF)
     g_out[...] += tn(att, dba)
     g_ga[...] += tn(na, dla)
-    datt = nt(dba, weight(3 * per)).astype(BF)
+    datt = nt(dba, weight(0)).astype(BF)
     for i in range(4):
         da_ref[i] = datt[:, i * LANES : (i + 1) * LANES]
-    dna = nt(dla, weight(4 * per))
+    dna = nt(dla, weight(per))
     dh_ref[0] = dh * (1.0 - ga)
     dn_ref[0] = dna
     v_ref[0:1] += jnp.sum(dna * n1, 0, keepdims=True)
@@ -863,24 +1005,14 @@
     per = w_query.shape[0]
     ff = w_in.shape[1] // width
     j = lax.axis_index("seq")
-    g = j // 4
-    hi = j % 4
     x = layer_input[:, 0]
     cot = cotangent[:, 0]
-    vec = jnp.stack([norm_attn, norm_ffn, bias_attn, bias_ffn])
-    shard = jnp.concatenate(
-        [w_query, w_key, w_value, w_out, w_gate_attn, w_gate_ffn]
-        + [w_in[:, k * width : (k + 1) * width] for k in range(ff)]
-        + [w_back, jnp.pad(vec, ((0, 12), (0, width - per)))]
-    )
-    xg, wg = gather(x, shard)
-    vecs = wg[:, -16:-12, :per].transpose(1, 0, 2).reshape(4, width)
-    w = lax.dynamic_slice(wg, (0, 0, hi * LANES), (32, 3 * per, LANES))
-    w = w.reshape(32, 3, per, LANES).transpose(0, 2, 1, 3).reshape(width, 3 * LANES)
-    doc = jnp.stack([doc_offset[g, 0, 0], doc_len[g, 0, 0]])
+    small = jnp.pad(
+        jnp.stack([norm_attn, norm_ffn, bias_attn, bias_ffn] * 2), ((0, 8), (0, LANES - per))
+    )
+    mats = (w_query, w_key, w_value, w_out, w_gate_attn, w_gate_ffn, w_in, w_back)
+    xg, wg, w, vecs, att, o32, qa, ka, va = front(doc_len, doc_offset, x, mats, small)
     gain = vecs[0:1]
-    o, o32, qa, ka, va = attend(doc, xg, w, gain)
-    att = swap(o, 1)
     out, datt, dh, dna, grads, sums = tokens(x, cot, att, wg, vecs)
     do = swap(datt, 2)
     dn, gf, gq, gv = attend_back(xg, w, gain, o32, do, qa, ka, va, sums, grads)

time: 346 us -> 308 us (0.89)
  Pallas kernels: 314 us -> 290 us
  local copies, waits for them, and re-layouts: 19.5 us -> 9.55 us
    pallas_call x2 -> x1, Pallas kernels: 46.6 us -> 19.1 us  [swap(): pl.pallas_call(swap_kernel, out_shape=jax.ShapeDtypeStruct(a.shape, a.dty...]
    unnamed x22 -> x14, local copies, waits for them, and re-layouts: 9.93 us -> 2.98 us
    pallas_call x2 -> x1, Pallas kernels: 114 us -> 116 us  [front(): pl.pallas_call(front_kernel, out_shape=(jax.ShapeDtypeStruct((blocks, row...]
where the time goes in v3:
time: 308 us
  Pallas kernels  290 us (94%)
  local copies, waits for them, and re-layouts  9.55 us (3%)
  other arithmetic  8.14 us (3%)
    pallas_call x1, Pallas kernels, attend_back(): pl.pallas_call(attend_back_kernel, out_shape=(jax.ShapeDtypeStruct((2, ro...  123 us
    pallas_call x1, Pallas kernels, front(): pl.pallas_call(front_kernel, out_shape=(jax.ShapeDtypeStruct((blocks, row...  116 us
    pallas_call x1, Pallas kernels, tokens(): pl.pallas_call(token_kernel, grid=(micro,), out_shape=(jax.ShapeDtypeStru...  31.5 us
    pallas_call x1, Pallas kernels, swap(): pl.pallas_call(swap_kernel, out_shape=jax.ShapeDtypeStruct(a.shape, a.dty...  19.1 us

profile of v3, /device:TPU:0, one launch (start us, length us, event | category | flops | bytes accessed | tf_op | source)
XLA Modules:
  0.0 308.1 jit_solution(9826439231865103917)
XLA Ops:
  0.6 0.8 stack.23
  1.4 0.6 pad.4.small_ref
  2.0 1.3 copy.30.doc_len
  3.3 1.3 copy.31.doc_off
  4.6 116.5 %front.1 = (bf16[8,512,512]{2,1,0:T(8,128)(2,1)}, bf16[32,176,512]{2,1,0:T(8,128)(2,1)}, bf16[512,384]{1,0:T(8,128)(2,1)}, f32[4,512]{1,0:T(4,128)}, bf16[8,512,...) custom-call(s32[2,1,1]{2,1,0:T(1,128)} %copy.30.doc_len, ...), custom_call_target="tpu_custom_call" | custom-call | tf_op jit(solution)/shard_map/front/pallas_call | solution.py:464
  121.1 31.5 %shard_map.263 = (bf16[2,512,512]{2,1,0:T(8,128)(2,1)}, bf16[8,512,128]{2,1,0:T(8,128)(2,1)}, f32[2,512,512]{2,1,0:T(8,128)}, f32[2,512,512]{2,1,0:T(8,128)}, bf...) custom-call(bf16[2,512,512]{2,1,0:T(8,128)(2,1)} %bitcast.37, bf16[2,512,512]{2,1,0:T(8,128)(2,1)} %bitcast.38, ...), custom_call_target="tpu_custom_call" | custom-call | tf_op jit(solution)/shard_map/pallas_call | solution.py:629
  152.6 19.1 %shard_map.264.do_ref = bf16[8,512,128]{2,1,0:T(8,128)(2,1)} custom-call(bf16[8,512,128]{2,1,0:T(8,128)(2,1)} %get-tuple-element.42.a_ref), custom_call_target="tpu_custom_call" | custom-call | tf_op jit(solution)/shard_map/pallas_call | solution.py:516
  171.7 1.3 slice.39.gain_ref
  173.0 0.0 copy-start.5
  173.0 122.6 %attend_back.1 = (bf16[2,512,512]{2,1,0:T(8,128)(2,1)}, f32[176,512]{1,0:T(8,128)}, f32[3,16,512]{2,1,0:T(8,128)}, f32[8,512]{1,0:T(8,128)}) custom-call(bf16[8,512,512]{2,1,0:T(8,128)(2,1)} %get-tuple-element.39.x_ref, bf16[512,384]{1,0:T(8,128)(2,1)} %get-tuple-element.40.w_ref, f32[1,512]{1,0:T(1,128)} %slice.39.gain_ref, ...), custom_call_target="tpu_custom_call" | custom-call | tf_op jit(solution)/shard_map/attend_back/pallas_call | solution.py:961
  295.6 1.5 fusion.7
  297.1 0.0 copy-done.5
  297.1 0.0 copy-start
  297.1 0.0 copy-start.1
  297.1 0.0 copy-start.2
  297.2 3.0 fusion.2
  300.2 0.0 copy-done
  300.2 0.1 copy-done.1
  300.3 0.3 copy-done.2
  300.6 0.0 copy-start.3
  300.6 0.0 copy-start.4
  300.6 3.6 %fusion.6 = f32[2,1,512,512]{3,2,1,0:T(8,128)} fusion(f32[2,512,512]{2,1,0:T(8,128)} %get-tuple-element.37, f32[2,512,512]{2,1,0:T(8,128)S(1)} %copy-done.1, bf16[2,512,512]{2,1,0:T(8,128)(2,1)S(1)} %copy-done.2, f32[2,512]{1,0:T(2,128)S(1)} %broadcast_multiply_fusion, f32[512]{0:T(512)S(1)} %bitcast.42, f32[2,512]{1,0:T(2,128)S(1)} %add_rsqrt_fusion, ...), kind=kLoop, calls=%fused_computation.8 | loop fusion | flops 4718592 | bytes 8398848
  304.2 0.0 copy-done.3
  304.2 0.7 fusion.8
  304.9 0.7 copy.35
  305.5 0.6 fusion.9
  306.2 0.0 copy-done.4
  306.2 0.6 slice_bitcast_fusion
  306.8 0.8 constant_dynamic-slice_fusion
  307.6 0.5 slice_bitcast_fusion.3
  (2 shorter events, 0.0 us)
Async XLA Ops:
  173.0 124.1 %copy-start.5 = (f32[1,512]{1,0:T(1,128)S(1)}, f32[1,512]{1,0:T(1,128)}, u32[]{:S(2)}) copy-start(f32[1,512]{1,0:T(1,128)} %slice.39.gain_ref) | copy-start | bytes 6148
  297.1 3.1 copy-start
  297.1 3.2 %copy-start.1 = (f32[2,512,512]{2,1,0:T(8,128)S(1)}, f32[2,512,512]{2,1,0:T(8,128)}, u32[]{:S(2)}) copy-start(f32[2,512,512]{2,1,0:T(8,128)} %get-tuple-element.38) | copy-start | bytes 6291460
  297.1 3.4 %copy-start.2 = (bf16[2,512,512]{2,1,0:T(8,128)(2,1)S(1)}, bf16[2,512,512]{2,1,0:T(8,128)(2,1)}, u32[]{:S(2)}) copy-start(bf16[2,512,512]{2,1,0:T(8,128)(2,1)} %get-tuple-element.48) | copy-start | bytes 3145732
  300.6 3.6 %copy-start.3 = (f32[176,512]{1,0:T(8,128)S(1)}, f32[176,512]{1,0:T(8,128)}, u32[]{:S(2)}) copy-start(f32[176,512]{1,0:T(8,128)} %get-tuple-element.50) | copy-start | bytes 1081348
  300.6 5.6 %copy-start.4 = (f32[3,16,512]{2,1,0:T(8,128)S(1)}, f32[3,16,512]{2,1,0:T(8,128)}, u32[]{:S(2)}) copy-start(f32[3,16,512]{2,1,0:T(8,128)} %get-tuple-element.49) | copy-start | bytes 294916

commit v4 on v3

--- a/solution.py
+++ b/solution.py
@@ -184,7 +184,6 @@
 ):
     blocks, rows, width = xg.shape
     per = wq.shape[0]
-    half = width // 2
     d, j, z, c, dx, dy, dxy = place()
     me = d * 8 + j
     g = z // 2
@@ -205,27 +204,34 @@
         loads[-1].start()
     own = pltpu.make_async_copy(x_ref.at[g], xg.at[j], xsem)
     own.start()
-    lanes = lax.broadcasted_iota(jnp.int32, (LANES, half), 1)
-    subs = lax.broadcasted_iota(jnp.int32, (LANES, half), 0)
-    spots = [
-        nn(small_ref[...], jnp.where(lanes + k * half == me * per + subs, 1.0, 0.0).astype(BF)) for k in range(2)
-    ]
-    row = lax.broadcasted_iota(jnp.int32, (16, half), 0)
-    tile = jnp.where(row < 4, spots[0], spots[1]).astype(BF)
-    hv[3 * per :, :half] = tile
-    hv[3 * per :, half:] = tile
+    lanes = lax.broadcasted_iota(jnp.int32, (LANES, LANES), 1)
+    subs = lax.broadcasted_iota(jnp.int32, (LANES, LANES), 0)
+    row = lax.broadcasted_iota(jnp.int32, (16, LANES), 0)
+    tile = jnp.zeros((16, LANES), F32)
+    for k in range(4):
+        spot = jnp.where(lanes + k * LANES == me * per + subs, 1.0, 0.0).astype(BF)
+        tile = jnp.where(row // 4 == k, nn(small_ref[...], spot), tile)
+    for k in range(4):
+        hv[3 * per :, k * LANES : (k + 1) * LANES] = tile.astype(BF)
     for k in range(3):
         loads[k].wait()
-    greet([(d, (j + k) % 8) for k in range(1, 8)] + [(dx, j), (dy, j)])
-
-    heads = Spread(hg, hsend, hrecv)
+    greet([(d, (j + k) % 8) for k in range(1, 8)] + [(dx, j), (dy, j), (dxy, j)])
+
     weights = Spread(wg, wsend, wrecv)
 
-    def side(zz):
-        return hv.at[:, pl.ds(pl.multiple_of(half * (zz % 2), half), half)]
-
-    heads.along([side(zz) for zz in (za, zb, zc)])
-    heads.in_plane(side(z))
+    def mine(seq):
+        return hv.at[:, pl.ds(pl.multiple_of(LANES * (seq % 4), LANES), LANES)]
+
+    def hcopy(k):
+        seq = (j + k) % 8
+        return remote(mine(seq), hg.at[me], hsend.at[k], hrecv.at[j], d, seq)
+
+    def lcopy(k, dp):
+        line = hg.at[pl.ds(d * 8, 8)]
+        return remote(line, line, hsend.at[8 + k], hrecv.at[8 + k], dp, j)
+
+    for k in range(1, 8):
+        hcopy(k).start()
 
     def xcopy(k, part, block, dp, seq, src=None):
         piece = pl.ds(part * (rows // CK), rows // CK)
@@ -242,32 +248,32 @@
         xcopy(1, part, j, d, pj, g).start()
     for part in range(CK):
         xcopy(2, part, j, d, jn, 1 - g).start()
-    hg[me] = jnp.where(z % 2 == 0, hv[:, :half], hv[:, half:])
+    keep_h = pltpu.make_async_copy(mine(j), hg.at[me], lsem.at[1])
+    keep_h.start()
     for copy in loads[3:]:
         copy.wait()
     keep = pltpu.make_async_copy(sv, wg.at[me], lsem.at[0])
     keep.start()
     weights.in_plane(sv)
 
-    heads.from_line(1)
-    heads.from_plane(0)
-    heads.from_line(2)
-    heads.from_plane(1)
-    heads.from_line(3)
-    heads.from_plane(2)
-    heads.from_plane(3)
-    heads.from_corner()
-    heads.from_core()
-
-    vecs = jnp.zeros((16, half), F32)
+    weights.along([sv] * 3)
+    keep_h.wait()
+    for k in range(1, 8):
+        seq = (j + k) % 8
+        remote(mine(seq), hg.at[d * 8 + seq], hsend.at[k], hrecv.at[seq], d, seq).wait_recv()
+    for k, dp in enumerate((dx, dy, dxy)):
+        lcopy(k, dp).start()
+    for k, dp in enumerate((dx, dy, dxy)):
+        line = hg.at[pl.ds(dp * 8, 8)]
+        remote(line, line, hsend.at[8 + k], hrecv.at[8 + k], dp, j).wait_recv()
+
+    vecs = jnp.zeros((16, LANES), F32)
     for k in range(32):
         vecs += hg[k, 3 * per :].astype(F32)
-    for k in range(2):
-        vec_ref[:, k * half : (k + 1) * half] = vecs[4 * k : 4 * k + 4]
+    for k in range(4):
+        vec_ref[:, k * LANES : (k + 1) * LANES] = vecs[4 * k : 4 * k + 4]
     for k in range(3):
-        both = hg[:, k * per : (k + 1) * per, :]
-        picked = jnp.where(c == 0, both[:, :, :LANES], both[:, :, LANES:])
-        w_ref[:, k * LANES : (k + 1) * LANES] = picked.reshape(width, LANES)
+        w_ref[:, k * LANES : (k + 1) * LANES] = hg[:, k * per : (k + 1) * per, :].reshape(width, LANES)
 
     off = doc_off[g, 0, 0]
     end = off + doc_len[g, 0, 0]
@@ -374,7 +380,11 @@
             acopy(b).start()
 
     def outer(i, _):
-        @pl.when(i == 4)
+        @pl.when(i == 1)
+        def _():
+            weights.from_plane(0)
+
+        @pl.when(i == 3)
         def _():
             @pl.when(near)
             def _():
@@ -383,18 +393,24 @@
                     xcopy(7, part, b2, d, ja).start()
                     xcopy(5, part, b2, d, pj).start()
 
+            weights.from_line(1)
+
+        @pl.when(i == 4)
+        def _():
             @pl.when(far)
             def _():
                 for part in range(CK):
                     xcopy(0, part, b1, d, pj).wait_recv()
                     xcopy(4, part, b1, d, pj).start()
 
-            weights.along([sv] * 3)
-            weights.from_plane(0)
             xarrive(b1 + 1 - 2 * c)
+
+        pl.when(i == 5)(partial(weights.from_plane, 1))
 
         @pl.when(i == 6)
         def _():
+            weights.from_line(2)
+
             @pl.when(far)
             def _():
                 for part in range(CK):
@@ -402,42 +418,48 @@
                     xcopy(5, part, b2, d, pj).start()
 
             xarrive(b2 + 1 - 2 * c)
+            weights.from_line(3)
 
         @pl.when(jnp.logical_or(i == 4, i == 6))
         def _():
             project_two(2 * (z1 + (z2 - z1) * ((i - 4) // 2)))
 
-        o = (1 - g) * i + g * (blocks - 1 - i)
-        first(o)
-        last = jnp.logical_and(g == 1, i == blocks - 1)
-        pl.when(last)(lambda: finish(o))
+        pl.when(i == 7)(partial(weights.from_plane, 2))
+        pl.when(i == 8)(partial(weights.from_plane, 3))
+        pl.when(i == 10)(weights.from_corner)
+        tail = i >= blocks
+        o = jnp.where(g == 0, i, jnp.where(tail, i - 4, blocks - 1 - i))
+        early = jnp.where(jnp.logical_or(g == 0, i < 4), i, i - 4)
+        count = jnp.where(tail, 4 * g, early)
+        out_now = jnp.logical_and(g == 1, i == blocks - 1)
+
+        @pl.when(jnp.logical_not(tail))
+        def _():
+            first(o)
+
+        pl.when(i == 7 * g)(lambda: finish(o))
 
         def inner(t, _):
-            q = (1 - g) * o + g * (o + 1 + t)
-            pair(q, (1 - g) * (o - 1 - t) + g * o)
-            pl.when(jnp.logical_or(last, jnp.logical_and(g == 0, t == i - 1)))(lambda: finish(q))
-
-            @pl.when(jnp.logical_and(i == blocks - 1, t == 3))
-            def _():
-                for k in range(1, 4):
-                    weights.from_line(k)
-
+            q = jnp.where(jnp.logical_or(g == 0, tail), o, o + 1 + t)
+            k = jnp.where(g == 0, o - 1 - t, jnp.where(tail, t, o))
+            pair(q, k)
+            ends = jnp.logical_and(jnp.logical_or(g == 0, tail), t == count - 1)
+            pl.when(jnp.logical_or(out_now, ends))(lambda: finish(q))
             return 0
 
-        lax.fori_loop(0, i, inner, 0)
-        pl.when(jnp.logical_and(g == 0, i == 0))(lambda: finish(o))
+        lax.fori_loop(0, count, inner, 0)
         return 0
 
-    lax.fori_loop(0, blocks, outer, 0)
+    lax.fori_loop(0, blocks + 4, outer, 0)
     att[j] = ov[j]
-    for k in range(1, 4):
-        weights.from_plane(k)
-    weights.from_corner()
     weights.from_core()
     for k in range(1, 8):
         q = (j + k) % 8
         remote(ov.at[q], att.at[q], ssend.at[q], srecv.at[q], d, q).wait_recv()
-    heads.wait_sent()
+    for k in range(1, 8):
+        hcopy(k).wait_send()
+    for k, dp in enumerate((dx, dy, dxy)):
+        lcopy(k, dp).wait_send()
     weights.wait_sent()
     for k in range(6):
         for part in range(CK):
@@ -476,13 +498,13 @@
         out_specs=(INVM, ANY) + (INVM,) * 7,
         scratch_shapes=[
             pltpu.VMEM((3 * per + 16, width), BF),
-            pltpu.VMEM((32, 3 * per + 16, width // 2), BF),
+            pltpu.VMEM((32, 3 * per + 16, LANES), BF),
             pltpu.VMEM((tall, width), BF),
             pltpu.VMEM((2, blocks, SIDE + 16, rows), BF),
             pltpu.VMEM((2, blocks, 1, rows), F32),
             pltpu.VMEM((2, blocks, SIDE + 16, rows), F32),
             pltpu.VMEM((blocks, rows, LANES), BF),
-            dma((12,)), dma, dma((32,)), dma((32,)), dma((32,)), dma((32,)),
+            dma((12,)), dma, dma((11,)), dma((11,)), dma((32,)), dma((32,)),
             dma((8, CK)), dma((8, CK)), dma((8,)), dma((8,)),
         ],
         compiler_params=pltpu.CompilerParams(
@@ -492,47 +514,12 @@
     )(doc_len, doc_off, x, *mats, small)
 
 
-def swap_kernel(a_ref, b_ref, av, lsem, send, recv):
-    d = lax.axis_index("dp")
-    j = lax.axis_index("seq")
-    load = pltpu.make_async_copy(a_ref.at[j], av, lsem)
-    load.start()
-    peers = [(d, (j + k) % 8) for k in range(1, 8)]
-    greet(peers)
-    copies = []
-    for k, (dp, seq) in enumerate(peers):
-        copy = remote(a_ref.at[seq], b_ref.at[j], send.at[k], recv.at[k], dp, seq)
-        copy.start()
-        copies.append(copy)
-    load.wait()
-    keep = pltpu.make_async_copy(av, b_ref.at[j], lsem)
-    keep.start()
-    for copy in copies:
-        copy.wait()
-    keep.wait()
-
-
-def swap(a, cid):
-    return pl.pallas_call(
-        swap_kernel,
-        out_shape=jax.ShapeDtypeStruct(a.shape, a.dtype),
-        in_specs=[ANY],
-        out_specs=ANY,
-        scratch_shapes=[
-            pltpu.VMEM(a.shape[1:], a.dtype),
-            pltpu.SemaphoreType.DMA,
-            pltpu.SemaphoreType.DMA((7,)),
-            pltpu.SemaphoreType.DMA((7,)),
-        ],
-        compiler_params=pltpu.CompilerParams(collective_id=cid, has_side_effects=True),
-    )(a)
-
-
 def token_kernel(
-    x_ref, c_ref, a_ref, wg, vec, out_ref, da_ref, dh_ref, dn_ref, g_ref, v_ref,
-    gp, act, g_out, g_ga, g_gf, g_in, g_back,
+    x_ref, c_ref, a_ref, wg, vec, out_ref, do_ref, dh_ref, dn_ref, g_ref, v_ref,
+    gp, act, da, dpres, g_out, g_ga, g_gf, g_in, g_back, send, recv,
 ):
-    step = pl.program_id(0)
+    d, j = lax.axis_index("dp"), lax.axis_index("seq")
+    g = j // 4
     rows, width = x_ref.shape[1:]
     ff = gp.shape[0]
     per = width // 32
@@ -544,91 +531,101 @@
         n = wg.shape[0] // ff
         return wg[k * n : (k + 1) * n, 7 * per : 7 * per + ff * per, :].reshape(width, width)
 
-    @pl.when(step == 0)
-    def _():
-        for ref in (g_out, g_ga, g_gf, g_in, g_back, v_ref):
-            ref[...] = jnp.zeros_like(ref)
-
-    x = x_ref[0].astype(F32)
-    gain_a, gain_f = vec[0:1].astype(F32), vec[1:2].astype(F32)
-    shift_a, shift_f = vec[2:3].astype(F32), vec[3:4].astype(F32)
-    n1 = x * lax.rsqrt(jnp.mean(x * x, -1, keepdims=True) + EPS)
-    na = (n1 * gain_a).astype(BF)
-    ga = jax.nn.sigmoid(nn(na, weight(per)) + shift_a)
-    att = jnp.concatenate([a_ref[i] for i in range(4)], axis=1)
-    br = nn(att, weight(0))
-    hid = ga * br + (1.0 - ga) * x
-    r2 = lax.rsqrt(jnp.mean(hid * hid, -1, keepdims=True) + EPS)
-    n2 = hid * r2
-    nf = (n2 * gain_f).astype(BF)
-    bf = jnp.zeros((rows, width), F32)
+    for ref in (g_out, g_ga, g_gf, g_in, g_back, v_ref):
+        ref[...] = jnp.zeros_like(ref)
+    greet([(d, (j + k) % 8) for k in range(1, 8)])
+
+    def dcopy(q):
+        return remote(da.at[q], do_ref.at[j], send.at[q], recv.at[j], d, q)
+
+    def one(t, _):
+        m = (1 - g) * (1 - t) + g * t
+        x = x_ref[m].astype(F32)
+        gain_a, gain_f = vec[0:1].astype(F32), vec[1:2].astype(F32)
+        shift_a, shift_f = vec[2:3].astype(F32), vec[3:4].astype(F32)
+        n1 = x * lax.rsqrt(jnp.mean(x * x, -1, keepdims=True) + EPS)
+        na = (n1 * gain_a).astype(BF)
+        ga = jax.nn.sigmoid(nn(na, weight(per)) + shift_a)
+        att = jnp.concatenate([a_ref[4 * m + i] for i in range(4)], axis=1)
+        br = nn(att, weight(0))
+        hid = ga * br + (1.0 - ga) * x
+        r2 = lax.rsqrt(jnp.mean(hid * hid, -1, keepdims=True) + EPS)
+        n2 = hid * r2
+        nf = (n2 * gain_f).astype(BF)
+        bf = jnp.zeros((rows, width), F32)
+        for k in range(ff):
+            pre = nn(nf, weight((3 + k) * per))
+            sq = pre * pre
+            t = jnp.tanh(GELU_C * pre * (1.0 + GELU_A * sq))
+            half = 0.5 * (1.0 + t)
+            act[k] = (pre * half).astype(BF)
+            gp[k] = half + 0.5 * pre * (1.0 - t * t) * (GELU_C * (1.0 + 3.0 * GELU_A * sq))
+            bf += nn(act[k], back(k))
+        gf = jax.nn.sigmoid(nn(nf, weight(2 * per)) + shift_f)
+        out_ref[m] = (gf * bf + (1.0 - gf) * hid).astype(BF)
+        c = c_ref[m].astype(F32)
+        dlf = (c * (bf - hid) * gf * (1.0 - gf)).astype(BF)
+        dbf = (c * gf).astype(BF)
+        dnf = nt(dlf, weight(2 * per))
+        for k in range(ff):
+            dpre = (nt(dbf, back(k)) * gp[k]).astype(BF)
+            dpres[k] = dpre
+            dnf += nt(dpre, weight((3 + k) * per))
+        g2 = dnf * gain_f
+        dh = c * (1.0 - gf) + r2 * (g2 - n2 * jnp.mean(g2 * n2, -1, keepdims=True))
+        dba = (dh * ga).astype(BF)
+        dla = (dh * (br - x) * ga * (1.0 - ga)).astype(BF)
+        datt = nt(dba, weight(0)).astype(BF)
+        for i in range(4):
+            da[4 * m + i] = datt[:, i * LANES : (i + 1) * LANES]
+
+            @pl.when(j != 4 * m + i)
+            def _():
+                dcopy(4 * m + i).start()
+
+        dna = nt(dla, weight(per))
+        g_out[...] += tn(att, dba)
+        g_ga[...] += tn(na, dla)
+        g_gf[...] += tn(nf, dlf)
+        for k in range(ff):
+            g_back[k] += tn(act[k], dbf)
+            g_in[k] += tn(nf, dpres[k])
+        dh_ref[m] = dh * (1.0 - ga)
+        dn_ref[m] = dna
+        v_ref[0:1] += jnp.sum(dna * n1, 0, keepdims=True)
+        v_ref[1:2] += jnp.sum(dnf * n2, 0, keepdims=True)
+        v_ref[2:3] += jnp.sum(dla.astype(F32), 0, keepdims=True)
+        v_ref[3:4] += jnp.sum(dlf.astype(F32), 0, keepdims=True)
+        return 0
+
+    lax.fori_loop(0, 2, one, 0)
+
+    def put(lo, value):
+        g_ref[:, lo : lo + per, :] = value.astype(BF).reshape(32, per, width)
+
+    put(0, g_out[...])
+    put(per, g_ga[...])
+    put(2 * per, g_gf[...])
     for k in range(ff):
-        pre = nn(nf, weight((3 + k) * per))
-        sq = pre * pre
-        t = jnp.tanh(GELU_C * pre * (1.0 + GELU_A * sq))
-        half = 0.5 * (1.0 + t)
-        act[k] = (pre * half).astype(BF)
-        gp[k] = half + 0.5 * pre * (1.0 - t * t) * (GELU_C * (1.0 + 3.0 * GELU_A * sq))
-        bf += nn(act[k], back(k))
-    gf = jax.nn.sigmoid(nn(nf, weight(2 * per)) + shift_f)
-    out_ref[0] = (gf * bf + (1.0 - gf) * hid).astype(BF)
-    c = c_ref[0].astype(F32)
-    dlf = (c * (bf - hid) * gf * (1.0 - gf)).astype(BF)
-    dbf = (c * gf).astype(BF)
-    dnf = nt(dlf, weight(2 * per))
-    g_gf[...] += tn(nf, dlf)
-    for k in range(ff):
-        dpre = (nt(dbf, back(k)) * gp[k]).astype(BF)
-        g_back[k] += tn(act[k], dbf)
-        g_in[k] += tn(nf, dpre)
-        dnf += nt(dpre, weight((3 + k) * per))
-    g2 = dnf * gain_f
-    dh = c * (1.0 - gf) + r2 * (g2 - n2 * jnp.mean(g2 * n2, -1, keepdims=True))
-    dba = (dh * ga).astype(BF)
-    dla = (dh * (br - x) * ga * (1.0 - ga)).astype(BF)
-    g_out[...] += tn(att, dba)
-    g_ga[...] += tn(na, dla)
-    datt = nt(dba, weight(0)).astype(BF)
-    for i in range(4):
-        da_ref[i] = datt[:, i * LANES : (i + 1) * LANES]
-    dna = nt(dla, weight(per))
-    dh_ref[0] = dh * (1.0 - ga)
-    dn_ref[0] = dna
-    v_ref[0:1] += jnp.sum(dna * n1, 0, keepdims=True)
-    v_ref[1:2] += jnp.sum(dnf * n2, 0, keepdims=True)
-    v_ref[2:3] += jnp.sum(dla.astype(F32), 0, keepdims=True)
-    v_ref[3:4] += jnp.sum(dlf.astype(F32), 0, keepdims=True)
-
-    @pl.when(step == pl.num_programs(0) - 1)
-    def _():
-        def put(lo, value):
-            g_ref[:, lo : lo + per, :] = value.astype(BF).reshape(32, per, width)
-
-        put(0, g_out[...])
-        put(per, g_ga[...])
-        put(2 * per, g_gf[...])
-        for k in range(ff):
-            put((3 + k) * per, g_in[k])
-            n = 32 // ff
-            g_ref[k * n : (k + 1) * n, (3 + ff) * per :, :] = (
-                g_back[k].astype(BF).reshape(n, ff * per, width)
-            )
+        put((3 + k) * per, g_in[k])
+        n = 32 // ff
+        g_ref[k * n : (k + 1) * n, (3 + ff) * per :, :] = (
+            g_back[k].astype(BF).reshape(n, ff * per, width)
+        )
+    do_ref[j] = da[j]
+    for k in range(1, 8):
+        q = (j + k) % 8
+        remote(da.at[q], do_ref.at[q], send.at[q], recv.at[q], d, q).wait_recv()
+        dcopy(q).wait_send()
 
 
 def tokens(x, cot, att, wg, vec):
     micro, rows, width = x.shape
     ff = 4
     per = width // 32
-    tok = pl.BlockSpec((1, rows, width), lambda i: (i, 0, 0))
-    head = pl.BlockSpec((4, rows, LANES), lambda i: (i, 0, 0))
-
-    def whole(shape):
-        return pl.BlockSpec(shape, lambda i: (0,) * len(shape), pipeline_mode=pl.Buffered(1))
-
     grads = (32, (3 + 2 * ff) * per, width)
     return pl.pallas_call(
         token_kernel,
-        grid=(micro,),
         out_shape=(
             jax.ShapeDtypeStruct((micro, rows, width), BF),
             jax.ShapeDtypeStruct((4 * micro, rows, LANES), BF),
@@ -637,18 +634,25 @@
             jax.ShapeDtypeStruct(grads, BF),
             jax.ShapeDtypeStruct((8, width), F32),
         ),
-        in_specs=[tok, tok, head, whole(wg.shape), whole(vec.shape)],
-        out_specs=(tok, head, tok, tok, whole(grads), whole((8, width))),
+        in_specs=[INVM] * 5,
+        out_specs=(INVM,) * 6,
         scratch_shapes=[
             pltpu.VMEM((ff, rows, width), F32),
+            pltpu.VMEM((ff, rows, width), BF),
+            pltpu.VMEM((4 * micro, rows, LANES), BF),
             pltpu.VMEM((ff, rows, width), BF),
             pltpu.VMEM((width, width), F32),
             pltpu.VMEM((width, width), F32),
             pltpu.VMEM((width, width), F32),
             pltpu.VMEM((ff, width, width), F32),
             pltpu.VMEM((ff, width, width), F32),
+            pltpu.SemaphoreType.DMA((8,)),
+            pltpu.SemaphoreType.DMA((8,)),
         ],
-        compiler_params=pltpu.CompilerParams(vmem_limit_bytes=VMEM_LIMIT),
+        compiler_params=pltpu.CompilerParams(
+            collective_id=1, has_side_effects=True, vmem_limit_bytes=VMEM_LIMIT
+        ),
+        name="tokens",
     )(x, cot, att, wg, vec)
 
 
@@ -1008,13 +1012,12 @@
     x = layer_input[:, 0]
     cot = cotangent[:, 0]
     small = jnp.pad(
-        jnp.stack([norm_attn, norm_ffn, bias_attn, bias_ffn] * 2), ((0, 8), (0, LANES - per))
+        jnp.stack([norm_attn, norm_ffn, bias_attn, bias_ffn] * 4), ((0, 0), (0, LANES - per))
     )
     mats = (w_query, w_key, w_value, w_out, w_gate_attn, w_gate_ffn, w_in, w_back)
     xg, wg, w, vecs, att, o32, qa, ka, va = front(doc_len, doc_offset, x, mats, small)
     gain = vecs[0:1]
-    out, datt, dh, dna, grads, sums = tokens(x, cot, att, wg, vecs)
-    do = swap(datt, 2)
+    out, do, dh, dna, grads, sums = tokens(x, cot, att, wg, vecs)
     dn, gf, gq, gv = attend_back(xg, w, gain, o32, do, qa, ka, va, sums, grads)
     x32 = x.astype(F32)
     r1 = lax.rsqrt(jnp.mean(x32 * x32, -1, keepdims=True) + EPS)

time: 308 us -> 281 us (0.912)
  Pallas kernels: 290 us -> 261 us
    pallas_call x1, Pallas kernels: 116 us -> 103 us  [front(): pl.pallas_call(front_kernel, out_shape=(jax.ShapeDtypeStruct((blocks, row...]
    pallas_call x2 -> x1, Pallas kernels: 50.6 us -> 38.9 us  [tokens(): pl.pallas_call(token_kernel, out_shape=(jax.ShapeDtypeStruct((micro, rows...]
    pallas_call x1, Pallas kernels: 123 us -> 118 us  [attend_back(): pl.pallas_call(attend_back_kernel, out_shape=(jax.ShapeDtypeStruct((2, ro...]
where the time goes in v4:
time: 281 us
  Pallas kernels  261 us (93%)
  local copies, waits for them, and re-layouts  11.3 us (4%)
  other arithmetic  8.2 us (3%)
    pallas_call x1, Pallas kernels, attend_back(): pl.pallas_call(attend_back_kernel, out_shape=(jax.ShapeDtypeStruct((2, ro...  118 us
    pallas_call x1, Pallas kernels, front(): pl.pallas_call(front_kernel, out_shape=(jax.ShapeDtypeStruct((blocks, row...  103 us
    pallas_call x1, Pallas kernels, tokens(): pl.pallas_call(token_kernel, out_shape=(jax.ShapeDtypeStruct((micro, rows...  38.9 us

profile of v4, /device:TPU:0, one launch (start us, length us, event | category | flops | bytes accessed | tf_op | source)
XLA Modules:
  0.0 280.9 jit_solution(7647994484234741426)
XLA Ops:
  0.6 1.6 stack.14
  2.2 0.6 pad.4.small_ref
  2.8 1.3 copy.30.doc_len
  4.1 1.3 copy.31.doc_off
  5.4 103.3 %front.1 = (bf16[8,512,512]{2,1,0:T(8,128)(2,1)}, bf16[32,176,512]{2,1,0:T(8,128)(2,1)}, bf16[512,384]{1,0:T(8,128)(2,1)}, f32[4,512]{1,0:T(4,128)}, bf16[8,512,...) custom-call(s32[2,1,1]{2,1,0:T(1,128)} %copy.30.doc_len, ...), custom_call_target="tpu_custom_call" | custom-call | tf_op jit(solution)/shard_map/front/pallas_call | solution.py:486
  108.8 38.9 %tokens.1 = (bf16[2,512,512]{2,1,0:T(8,128)(2,1)}, bf16[8,512,128]{2,1,0:T(8,128)(2,1)}, f32[2,512,512]{2,1,0:T(8,128)}, f32[2,512,512]{2,1,0:T(8,128)}, bf16[32...) custom-call(bf16[2,512,512]{2,1,0:T(8,128)(2,1)} %bitcast.37, bf16[2,512,512]{2,1,0:T(8,128)(2,1)} %bitcast.38, ...), custom_call_target="tpu_custom_call" | custom-call | tf_op jit(solution)/shard_map/tokens/pallas_call | solution.py:627
  147.7 1.3 slice.39.gain_ref
  148.9 0.0 copy-start.6
  148.9 118.4 %attend_back.1 = (bf16[2,512,512]{2,1,0:T(8,128)(2,1)}, f32[176,512]{1,0:T(8,128)}, f32[3,16,512]{2,1,0:T(8,128)}, f32[8,512]{1,0:T(8,128)}) custom-call(bf16[8,512,512]{2,1,0:T(8,128)(2,1)} %get-tuple-element.39.x_ref, bf16[512,384]{1,0:T(8,128)(2,1)} %get-tuple-element.40.w_ref, f32[1,512]{1,0:T(1,128)} %slice.39.gain_ref, ...), custom_call_target="tpu_custom_call" | custom-call | tf_op jit(solution)/shard_map/attend_back/pallas_call | solution.py:965
  267.4 1.5 fusion.7
  268.9 0.0 copy-done.6
  268.9 0.0 copy-start
  268.9 0.0 copy-start.1
  268.9 0.0 copy-start.2
  269.0 3.0 %fusion.2 = f32[2,512]{1,0:T(2,128)S(1)} fusion(f32[2,512,512]{2,1,0:T(8,128)} %get-tuple-element.38, bf16[2,512,512]{2,1,0:T(8,128)(2,1)} %get-tuple-element.48, f32[512]{0:T(512)S(1)} %bitcast.42, f32[2,512]{1,0:T(2,128)S(1)} %add_rsqrt_fusion, bf16[2,1,512,512]{3,2,1,0:T(8,128)(2,1)} %param.16), kind=kLoop, calls=%fused_computation.4 | loop fusion | flops 3668992 | bytes 4204544 | tf_op jit(solution)/shard_map/reduce_sum | solution.py:1026
  272.0 0.0 copy-done
  272.0 0.1 copy-done.1
  272.1 0.3 copy-done.2
  272.4 0.0 copy-start.4
  272.4 0.0 copy-start.5
  272.4 0.0 copy-start.3
  272.4 3.7 %fusion.6 = f32[2,1,512,512]{3,2,1,0:T(8,128)} fusion(f32[2,512,512]{2,1,0:T(8,128)} %get-tuple-element.37, f32[2,512,512]{2,1,0:T(8,128)S(1)} %copy-done.1, bf16[2,512,512]{2,1,0:T(8,128)(2,1)S(1)} %copy-done.2, f32[2,512]{1,0:T(2,128)S(1)} %broadcast_multiply_fusion, f32[512]{0:T(512)S(1)} %bitcast.43, f32[2,512]{1,0:T(2,128)S(1)} %add_rsqrt_fusion, ...), kind=kLoop, calls=%fused_computation.8 | loop fusion | flops 4718592 | bytes 8398848
  276.0 0.0 copy-done.4
  276.0 0.7 fusion.8
  276.7 0.7 copy.35
  277.4 0.0 copy-done.5
  277.4 0.6 slice_bitcast_fusion
  278.0 0.6 fusion.9
  278.7 0.8 constant_dynamic-slice_fusion
  279.4 0.5 slice_bitcast_fusion.3
  279.9 0.0 copy-done.3
  279.9 1.0 copy.37
  (2 shorter events, 0.0 us)
Async XLA Ops:
  148.9 120.0 %copy-start.6 = (f32[1,512]{1,0:T(1,128)S(1)}, f32[1,512]{1,0:T(1,128)}, u32[]{:S(2)}) copy-start(f32[1,512]{1,0:T(1,128)} %slice.39.gain_ref) | copy-start | bytes 6148
  268.9 3.1 %copy-start = (bf16[2,1,512,512]{3,2,1,0:T(8,128)(2,1)S(1)}, bf16[2,1,512,512]{3,2,1,0:T(8,128)(2,1)}, u32[]{:S(2)}) copy-start(bf16[2,1,512,512]{3,2,1,0:T(8,128)(2,1)} %param.16) | copy-start | bytes 3145732
  268.9 3.2 %copy-start.1 = (f32[2,512,512]{2,1,0:T(8,128)S(1)}, f32[2,512,512]{2,1,0:T(8,128)}, u32[]{:S(2)}) copy-start(f32[2,512,512]{2,1,0:T(8,128)} %get-tuple-element.38) | copy-start | bytes 6291460
  268.9 3.4 %copy-start.2 = (bf16[2,512,512]{2,1,0:T(8,128)(2,1)S(1)}, bf16[2,512,512]{2,1,0:T(8,128)(2,1)}, u32[]{:S(2)}) copy-start(bf16[2,512,512]{2,1,0:T(8,128)(2,1)} %get-tuple-element.48) | copy-start | bytes 3145732
  272.4 3.7 %copy-start.4 = (f32[176,512]{1,0:T(8,128)S(1)}, f32[176,512]{1,0:T(8,128)}, u32[]{:S(2)}) copy-start(f32[176,512]{1,0:T(8,128)} %get-tuple-element.50) | copy-start | bytes 1081348
  272.4 5.0 %copy-start.5 = (f32[3,16,512]{2,1,0:T(8,128)S(1)}, f32[3,16,512]{2,1,0:T(8,128)}, u32[]{:S(2)}) copy-start(f32[3,16,512]{2,1,0:T(8,128)} %get-tuple-element.49) | copy-start | bytes 294916
  272.4 7.6 %copy-start.3 = (bf16[2,512,512]{2,1,0:T(8,128)(2,1)S(1)}, bf16[2,512,512]{2,1,0:T(8,128)(2,1)}, u32[]{:S(2)}) copy-start(bf16[2,512,512]{2,1,0:T(8,128)(2,1)} %get-tuple-element.36) | copy-start | bytes 3145732

commit v5 on v4

--- a/solution.py
+++ b/solution.py
@@ -409,7 +409,7 @@
 
         @pl.when(i == 6)
         def _():
-            weights.from_line(2)
+            weights.from_line(3)
 
             @pl.when(far)
             def _():
@@ -418,15 +418,15 @@
                     xcopy(5, part, b2, d, pj).start()
 
             xarrive(b2 + 1 - 2 * c)
-            weights.from_line(3)
+            weights.from_plane(2)
 
         @pl.when(jnp.logical_or(i == 4, i == 6))
         def _():
             project_two(2 * (z1 + (z2 - z1) * ((i - 4) // 2)))
 
-        pl.when(i == 7)(partial(weights.from_plane, 2))
-        pl.when(i == 8)(partial(weights.from_plane, 3))
-        pl.when(i == 10)(weights.from_corner)
+        pl.when(i == 5)(partial(weights.from_line, 2))
+        pl.when(i == 7)(partial(weights.from_plane, 3))
+        pl.when(i == 8)(weights.from_corner)
         tail = i >= blocks
         o = jnp.where(g == 0, i, jnp.where(tail, i - 4, blocks - 1 - i))
         early = jnp.where(jnp.logical_or(g == 0, i < 4), i, i - 4)
@@ -663,7 +663,7 @@
 
     def body(i, _):
         piece = pl.ds(i * per, per)
-        dst[piece, :] = (dst[piece, :].astype(F32) + src[piece, :].astype(F32)).astype(BF)
+        dst[piece, :] += src[piece, :]
         return 0
 
     lax.fori_loop(0, rows // per, body, 0)
@@ -737,9 +737,12 @@
         slot = (me + k) % 32
         return remote(hs_buf.at[slot], hb.at[me], hs.at[k], hr.at[me], slot // 8, slot % 8)
 
+    def part_of(dp):
+        return vs_buf.at[:, pl.ds(pl.multiple_of(dp * LANES, LANES), LANES)]
+
     def vcopy(k):
         slot = (me + k) % 32
-        return remote(vs_buf, vb.at[me], vs.at[k], vr.at[me], slot // 8, slot % 8)
+        return remote(part_of(slot // 8), vb.at[me], vs.at[k], vr.at[me], slot // 8, slot % 8)
 
     for zz, dp in first + rest:
         gcopy(zz, dp).start()
@@ -871,7 +874,7 @@
     wide = dw[...].T.astype(BF)
     hs_buf[...] = wide.reshape(32, per, 3 * LANES)
     keep_h = pltpu.make_async_copy(hs_buf.at[me], hb.at[me], lo.at[0])
-    keep_v = pltpu.make_async_copy(vs_buf, vb.at[me], lo.at[1])
+    keep_v = pltpu.make_async_copy(part_of(d), vb.at[me], lo.at[1])
     keep_h.start()
     keep_v.start()
 
@@ -880,13 +883,13 @@
         vcopy(k).start()
         return 0
 
+    lax.fori_loop(1, 32, hstart, 0)
     both_cores(wf)
 
     @pl.when(near)
     def _():
         tcopy(wf).start()
 
-    lax.fori_loop(1, 32, hstart, 0)
     for zz in (za, zb, zc):
         remote(acc.at[0], b4.at[zz], s4.at[0], r4.at[zz], d, ja).wait_recv()
     gf_ref[...] = (
@@ -899,7 +902,7 @@
     def harrive(k, _):
         slot = (me + k) % 32
         remote(hs_buf.at[0], hb.at[slot], hs.at[0], hr.at[slot], d, pj).wait_recv()
-        remote(vs_buf, vb.at[slot], vs.at[0], vr.at[slot], d, pj).wait_recv()
+        remote(part_of(d), vb.at[slot], vs.at[0], vr.at[slot], d, pj).wait_recv()
         return 0
 
     lax.fori_loop(1, 32, harrive, 0)
@@ -917,7 +920,7 @@
 
     def mine(i, _):
         piece = pl.ds(i * 128, 128)
-        own[piece, :] = (pb[j, piece, :].astype(F32) + q2[z, piece, :].astype(F32)).astype(BF)
+        own[piece, :] = pb[j, piece, :] + q2[z, piece, :]
         return 0
 
     lax.fori_loop(0, rows // 128, mine, 0)
@@ -968,7 +971,7 @@
             jax.ShapeDtypeStruct((2, rows, width), BF),
             jax.ShapeDtypeStruct(g, F32),
             jax.ShapeDtypeStruct((3, per, width), F32),
-            jax.ShapeDtypeStruct(sums.shape, F32),
+            jax.ShapeDtypeStruct((sums.shape[0], LANES), F32),
         ),
         in_specs=[INVM] * 9 + [ANY],
         out_specs=(ANY, INVM, INVM, INVM),
@@ -986,7 +989,7 @@
             pltpu.VMEM((4, rows, width), BF),
             pltpu.VMEM((4, rows, width), BF),
             pltpu.VMEM((32, per, 3 * LANES), BF),
-            pltpu.VMEM((32,) + sums.shape, F32),
+            pltpu.VMEM((32, sums.shape[0], LANES), F32),
             pltpu.VMEM((rows, width), BF),
             dma((16,)), dma((3,)),
             dma((16,)), dma((16,)), dma((16,)), dma((16,)), dma((4,)), dma((4,)), dma((4,)), dma((4,)),
@@ -1024,7 +1027,7 @@
     n1 = x32 * r1
     g1 = (dna + dn.astype(F32)) * gain.astype(F32)
     grad = dh + r1 * (g1 - n1 * jnp.mean(g1 * n1, -1, keepdims=True))
-    gv = lax.dynamic_slice(gv, (0, (lax.axis_index("dp") * 8 + j) * per), (4, per))
+    gv = lax.dynamic_slice(gv, (0, lax.axis_index("seq") * per), (4, per))
     return (
         out[:, None],
         grad[:, None],

time: 281 us -> 265 us (0.943)
  Pallas kernels: 261 us -> 245 us
    pallas_call x1, Pallas kernels: 103 us -> 90.4 us  [front(): pl.pallas_call(front_kernel, out_shape=(jax.ShapeDtypeStruct((blocks, row...]
    pallas_call x1, Pallas kernels: 118 us -> 112 us  [attend_back(): pl.pallas_call(attend_back_kernel, out_shape=(jax.ShapeDtypeStruct((2, ro...]
    pallas_call x1, Pallas kernels: 38.9 us -> 43 us  [tokens(): pl.pallas_call(token_kernel, out_shape=(jax.ShapeDtypeStruct((micro, rows...]
where the time goes in v5:
time: 265 us
  Pallas kernels  245 us (92%)
  local copies, waits for them, and re-layouts  10.6 us (4%)
  other arithmetic  8.2 us (3%)
    pallas_call x1, Pallas kernels, attend_back(): pl.pallas_call(attend_back_kernel, out_shape=(jax.ShapeDtypeStruct((2, ro...  112 us
    pallas_call x1, Pallas kernels, front(): pl.pallas_call(front_kernel, out_shape=(jax.ShapeDtypeStruct((blocks, row...  90.4 us
    pallas_call x1, Pallas kernels, tokens(): pl.pallas_call(token_kernel, out_shape=(jax.ShapeDtypeStruct((micro, rows...  43 us

profile of v5, /device:TPU:0, one launch (start us, length us, event | category | flops | bytes accessed | tf_op | source)
XLA Modules:
  0.0 264.6 jit_solution(8382231087971555749)
XLA Ops:
  0.6 1.6 stack.14
  2.2 0.6 pad.4.small_ref
  2.8 1.3 copy.30.doc_len
  4.1 1.3 copy.31.doc_off
  5.4 90.4 %front.1 = (bf16[8,512,512]{2,1,0:T(8,128)(2,1)}, bf16[32,176,512]{2,1,0:T(8,128)(2,1)}, bf16[512,384]{1,0:T(8,128)(2,1)}, f32[4,512]{1,0:T(4,128)}, bf16[8,512,...) custom-call(s32[2,1,1]{2,1,0:T(1,128)} %copy.30.doc_len, ...), custom_call_target="tpu_custom_call" | custom-call | tf_op jit(solution)/shard_map/front/pallas_call | solution.py:486
  95.8 43.0 %tokens.1 = (bf16[2,512,512]{2,1,0:T(8,128)(2,1)}, bf16[8,512,128]{2,1,0:T(8,128)(2,1)}, f32[2,512,512]{2,1,0:T(8,128)}, f32[2,512,512]{2,1,0:T(8,128)}, bf16[32...) custom-call(bf16[2,512,512]{2,1,0:T(8,128)(2,1)} %bitcast.37, bf16[2,512,512]{2,1,0:T(8,128)(2,1)} %bitcast.38, ...), custom_call_target="tpu_custom_call" | custom-call | tf_op jit(solution)/shard_map/tokens/pallas_call | solution.py:627
  138.8 1.3 slice.39.gain_ref
  140.1 0.0 copy-start.6
  140.1 111.7 %attend_back.1 = (bf16[2,512,512]{2,1,0:T(8,128)(2,1)}, f32[176,512]{1,0:T(8,128)}, f32[3,16,512]{2,1,0:T(8,128)}, f32[8,128]{1,0:T(8,128)}) custom-call(bf16[8,512,512]{2,1,0:T(8,128)(2,1)} %get-tuple-element.39.x_ref, bf16[512,384]{1,0:T(8,128)(2,1)} %get-tuple-element.40.w_ref, f32[1,512]{1,0:T(1,128)} %slice.39.gain_ref, ...), custom_call_target="tpu_custom_call" | custom-call | tf_op jit(solution)/shard_map/attend_back/pallas_call | solution.py:968
  251.8 1.5 fusion.7
  253.3 0.0 copy-done.6
  253.3 0.0 copy-start
  253.3 0.0 copy-start.1
  253.3 0.0 copy-start.2
  253.3 3.0 %fusion.2 = f32[2,512]{1,0:T(2,128)S(1)} fusion(f32[2,512,512]{2,1,0:T(8,128)} %get-tuple-element.38, bf16[2,512,512]{2,1,0:T(8,128)(2,1)} %get-tuple-element.48, f32[512]{0:T(512)S(1)} %bitcast.42, f32[2,512]{1,0:T(2,128)S(1)} %add_rsqrt_fusion, bf16[2,1,512,512]{3,2,1,0:T(8,128)(2,1)} %param.16), kind=kLoop, calls=%fused_computation.4 | loop fusion | flops 3668992 | bytes 4204544 | tf_op jit(solution)/shard_map/reduce_sum | solution.py:1029
  256.4 0.0 copy-done
  256.4 0.1 copy-done.1
  256.5 0.3 copy-done.2
  256.7 0.0 copy-start.4
  256.7 0.0 copy-start.5
  256.7 0.0 copy-start.7
  256.8 0.0 copy-start.3
  256.8 3.7 %fusion.6 = f32[2,1,512,512]{3,2,1,0:T(8,128)} fusion(f32[2,512,512]{2,1,0:T(8,128)} %get-tuple-element.37, f32[2,512,512]{2,1,0:T(8,128)S(1)} %copy-done.1, bf16[2,512,512]{2,1,0:T(8,128)(2,1)S(1)} %copy-done.2, f32[2,512]{1,0:T(2,128)S(1)} %broadcast_multiply_fusion, f32[512]{0:T(512)S(1)} %bitcast.43, f32[2,512]{1,0:T(2,128)S(1)} %add_rsqrt_fusion, ...), kind=kLoop, calls=%fused_computation.8 | loop fusion | flops 4718592 | bytes 8398848
  260.4 0.0 copy-done.4
  260.4 0.7 fusion.8
  261.1 0.7 copy.35
  261.8 0.0 copy-done.5
  261.8 0.6 slice_bitcast_fusion
  262.4 0.6 fusion.9
  263.0 0.0 copy-done.7
  263.0 0.1 constant_dynamic-slice_fusion
  263.1 0.5 slice_bitcast_fusion.3
  263.7 0.0 copy-done.3
  263.7 1.0 copy.37
  (2 shorter events, 0.0 us)
Async XLA Ops:
  140.1 113.2 %copy-start.6 = (f32[1,512]{1,0:T(1,128)S(1)}, f32[1,512]{1,0:T(1,128)}, u32[]{:S(2)}) copy-start(f32[1,512]{1,0:T(1,128)} %slice.39.gain_ref) | copy-start | bytes 6148
  253.3 3.1 %copy-start = (bf16[2,1,512,512]{3,2,1,0:T(8,128)(2,1)S(1)}, bf16[2,1,512,512]{3,2,1,0:T(8,128)(2,1)}, u32[]{:S(2)}) copy-start(bf16[2,1,512,512]{3,2,1,0:T(8,128)(2,1)} %param.16) | copy-start | bytes 3145732
  253.3 3.2 %copy-start.1 = (f32[2,512,512]{2,1,0:T(8,128)S(1)}, f32[2,512,512]{2,1,0:T(8,128)}, u32[]{:S(2)}) copy-start(f32[2,512,512]{2,1,0:T(8,128)} %get-tuple-element.38) | copy-start | bytes 6291460
  253.3 3.4 %copy-start.2 = (bf16[2,512,512]{2,1,0:T(8,128)(2,1)S(1)}, bf16[2,512,512]{2,1,0:T(8,128)(2,1)}, u32[]{:S(2)}) copy-start(bf16[2,512,512]{2,1,0:T(8,128)(2,1)} %get-tuple-element.48) | copy-start | bytes 3145732
  256.7 3.7 %copy-start.4 = (f32[176,512]{1,0:T(8,128)S(1)}, f32[176,512]{1,0:T(8,128)}, u32[]{:S(2)}) copy-start(f32[176,512]{1,0:T(8,128)} %get-tuple-element.50) | copy-start | bytes 1081348
  256.7 5.0 %copy-start.5 = (f32[3,16,512]{2,1,0:T(8,128)S(1)}, f32[3,16,512]{2,1,0:T(8,128)}, u32[]{:S(2)}) copy-start(f32[3,16,512]{2,1,0:T(8,128)} %get-tuple-element.49) | copy-start | bytes 294916
  256.7 6.3 %copy-start.7 = (f32[8,128]{1,0:T(8,128)S(1)}, f32[8,128]{1,0:T(8,128)}, u32[]{:S(2)}) copy-start(f32[8,128]{1,0:T(8,128)} %get-tuple-element.51) | copy-start | bytes 12292
  256.8 6.9 %copy-start.3 = (bf16[2,512,512]{2,1,0:T(8,128)(2,1)S(1)}, bf16[2,512,512]{2,1,0:T(8,128)(2,1)}, u32[]{:S(2)}) copy-start(bf16[2,512,512]{2,1,0:T(8,128)(2,1)} %get-tuple-element.36) | copy-start | bytes 3145732
